TPU v7x, 512 devices: a whole 4x4x16 slice. The times are simulated.
512 devices in a mesh: plane: 16 (over x, z_hi), tile: 32 (over z_lo, y, core).
Axes of the slice: x: 4, y: 4, z: 16 (z_hi: 4, z_lo: 4; z = z_hi * 4 + z_lo), core: 2. Of those that a mesh axis runs over, the one named last changes fastest.
Arguments:
- density: float32 [48, 256, 2048], P('plane', 'tile'), may hold values from -6 to 6
- plane_slot: int32 [48], replicated, may hold values from 0 to 95, as said below
- paint_weight: float32 [32, 9], replicated, may hold values from -2 to 2
- paint_bias: float32 [32], replicated, may hold values from -0.5 to 0.5
- mix_weight: float32 [32], replicated, may hold values from -1 to 1
- short_kernel: float32 [5, 5], replicated, may hold values from -1 to 1
Outputs:
- distortion: float32 [4, 48, 256, 2048], P(None, 'plane', 'tile')
Inputs may be any that keep to these rules, and one draw needn't show every extreme that they name: `plane_slot`: strictly increasing along the planes; the first is 0 and the last is 95.
All inputs are finite; a program needn't handle non-finite values.
Results may differ from a plain program's by a relative error of at most 0.00026.
Values sent between devices are 32-bit elements; how exact they have to be, the bound alone decides.
No kernel may reach another device: no remote copies, remote signals or barrier semaphores. Data moves between devices by JAX's collectives and lax.ppermute only.
A program may use at most 64 MiB of HBM per device.

v0:
```python
import math

import jax
import jax.numpy as jnp
from jax import lax
from jax.sharding import PartitionSpec as P

highest = lax.Precision.HIGHEST
lens_gain = 0.25


def extended_2(block, sides, width):
    for axis, dim in sides:
        count = lax.axis_size(axis)
        forward = [(i, i + 1) for i in range(count - 1)]
        backward = [(target, source) for source, target in forward]
        low = lax.ppermute(
            lax.slice_in_dim(block, block.shape[dim] - width, None, axis=dim), axis, forward
        )
        high = lax.ppermute(lax.slice_in_dim(block, 0, width, axis=dim), axis, backward)
        block = jnp.concatenate([low, block, high], axis=dim)
    return block


def from_behind(value, axis, by):
    devices = lax.axis_size(axis)
    pairs = [(i, i + by) for i in range(devices) if 0 <= i + by < devices]
    return lax.ppermute(value, axis, pairs)


def paint_rows(extended, paint_weight, paint_bias, mix_weight):
    row_count = extended.shape[-2] - 4
    col_count = extended.shape[-1]
    padded = jnp.pad(extended, [(0, 0)] * (extended.ndim - 1) + [(2, 2)])
    stacked = jnp.stack(
        [
            padded[
                ...,
                2 + 2 * row_step : 2 + 2 * row_step + row_count,
                2 + 2 * col_step : 2 + 2 * col_step + col_count,
            ]
            for row_step in (-1, 0, 1)
            for col_step in (-1, 0, 1)
        ],
        axis=0,
    )
    before = jnp.einsum("ct,t...->c...", paint_weight, stacked, precision=highest)
    hidden = jnp.tanh(before + paint_bias.reshape((-1,) + (1,) * (before.ndim - 1)))
    return jnp.einsum("c,c...->...", mix_weight, hidden, precision=highest)


def short_rows(extended, short_kernel):
    row_count = extended.shape[-2] - 4
    col_count = extended.shape[-1]
    padded = jnp.pad(extended, [(0, 0)] * (extended.ndim - 1) + [(2, 2)])
    running = jnp.zeros(extended.shape[:-2] + (row_count, col_count), jnp.float32)
    for row_tap in range(5):
        for col_tap in range(5):
            running = (
                running
                + short_kernel[row_tap, col_tap]
                * padded[..., row_tap : row_tap + row_count, col_tap : col_tap + col_count]
            )
    return running


def hessian_rows(extended):
    padded = jnp.pad(extended, [(0, 0)] * (extended.ndim - 1) + [(1, 1)])
    center = padded[..., 1:-1, 1:-1]
    second_rows = padded[..., 2:, 1:-1] - 2.0 * center + padded[..., :-2, 1:-1]
    second_cols = padded[..., 1:-1, 2:] - 2.0 * center + padded[..., 1:-1, :-2]
    mixed_part = (
        padded[..., 2:, 2:] - padded[..., 2:, :-2] - padded[..., :-2, 2:] + padded[..., :-2, :-2]
    ) * 0.25
    return jnp.stack([second_rows, second_cols, mixed_part], axis=0)


def lens_step(lens_state, shear_field, mixing, bending):
    previous = lens_state[0:2]
    current = lens_state[2:4]
    bent_first = shear_field[0] * current[0] + shear_field[2] * current[1]
    bent_second = shear_field[2] * current[0] + shear_field[1] * current[1]
    bent_rows = jnp.stack([bent_first, bent_second], axis=0)
    advanced = (1.0 - mixing) * previous + mixing * current - bending * bent_rows
    return jnp.concatenate([current, advanced], axis=0)


def distances(plane_slot, slot_total):
    distance = (plane_slot.astype(jnp.float32) + 1.0) / slot_total
    before = jnp.concatenate([jnp.zeros((1,), jnp.float32), distance[:-1]])
    after = jnp.concatenate(
        [distance[1:], jnp.full((1,), (slot_total + 1.0) / slot_total, jnp.float32)]
    )
    mixing = before * (after - distance) / (distance * (after - before))
    bending = lens_gain * (after - distance) / after
    return (mixing, bending)


def coarse_kernel(row_global, col_global, scale):
    gap = row_global.astype(jnp.float32)[:, None] - col_global.astype(jnp.float32)[None, :]
    return jnp.exp(-jnp.abs(gap) / scale)


def start_for(row_count, col_count):
    pattern = jnp.array([[1.0, 0.0], [0.0, 1.0], [1.0, 0.0], [0.0, 1.0]], jnp.float32)
    return jnp.broadcast_to(pattern[:, :, None, None], (4, 2, row_count, col_count))


def body(density, plane_slot, paint_weight, paint_bias, mix_weight, short_kernel):
    plane_count, row_count, col_count = density.shape
    tile_count = lax.axis_size("tile")
    tile_index = lax.axis_index("tile")
    plane_index = lax.axis_index("plane")
    total_rows = row_count * tile_count
    coarse_here = row_count // 4
    coarse_cols = col_count // 4
    row_scale = total_rows / 16.0
    col_scale = col_count / 16.0
    long_gain = 1.0 / math.sqrt(row_scale * col_scale)
    col_kernel = coarse_kernel(
        jnp.arange(coarse_cols, dtype=jnp.int32),
        jnp.arange(coarse_cols, dtype=jnp.int32),
        col_scale,
    )
    mixing_all, bending_all = distances(plane_slot, 2 * plane_slot.shape[0])
    mixing_here = lax.dynamic_slice_in_dim(mixing_all, plane_index * plane_count, plane_count)
    bending_here = lax.dynamic_slice_in_dim(bending_all, plane_index * plane_count, plane_count)
    extended = extended_2(density, (("tile", 1),), 2)
    convergence = paint_rows(extended, paint_weight, paint_bias, mix_weight)
    convergence_wide = extended_2(convergence, (("tile", 1),), 2)
    short_part = short_rows(convergence_wide, short_kernel)
    row_global = tile_index * coarse_here + 0 + jnp.arange(coarse_here, dtype=jnp.int32)
    coarse = convergence.reshape(plane_count, coarse_here, 4, coarse_cols, 4).mean(axis=(2, 4))
    received = lax.all_gather(coarse, "tile", axis=1, tiled=True)
    span_cols = received.shape[1]
    kernel_block = coarse_kernel(row_global, jnp.arange(span_cols, dtype=jnp.int32), row_scale)
    summed = jnp.einsum("ik,pkx->pix", kernel_block, received, precision=highest)
    potential = short_part + jnp.repeat(
        jnp.repeat(
            long_gain * jnp.einsum("pix,xy->piy", summed, col_kernel, precision=highest), 4, axis=1
        ),
        4,
        axis=2,
    )
    potential_wide = extended_2(potential, (("tile", 1),), 1)
    shear_field = hessian_rows(potential_wide)

    def run_planes(lens_state):
        results = []
        for plane_pos in range(plane_count):
            lens_state = lens_step(
                lens_state,
                shear_field[:, plane_pos],
                mixing_here[plane_pos],
                bending_here[plane_pos],
            )
            results.append(lens_state[2:4].reshape(4, row_count, col_count))
        return (lens_state, jnp.stack(results, axis=1))

    start_state = start_for(row_count, col_count)

    def relay_turn(iteration, state_in):
        state_out, unused_results = run_planes(state_in)
        incoming = from_behind(state_out, "plane", 1)
        return jnp.where(plane_index == 0, start_state, incoming)

    state_in = lax.fori_loop(0, lax.axis_size("plane") - 1, relay_turn, start_state)
    unused_state, results = run_planes(state_in)
    return results


def solution(mesh):
    placed = (P("plane", "tile", None), P(), P(), P(), P(), P())
    return jax.shard_map(
        body, mesh=mesh, in_specs=placed, out_specs=P(None, "plane", "tile", None), check_vma=False
    )
```

profile of v0, /device:TPU:108, one launch (start us, length us, event | category | flops | bytes accessed | tf_op | source)
XLA Modules:
  0.0 1031.1 jit_solution(7631755121506922006)
XLA Ops:
  3.0 3.6 collective-permute-start.2
  24.1 6.6 stack.90
  30.8 7.6 fusion.61
  38.4 3.8 fusion.3
  43.0 7.9 reshape.65
  52.8 3.6 collective-permute-start.4
  56.4 3.3 reduce_sum.9
  59.8 36.7 %all_gather.3 = f32[3,64,512]{2,0,1:T(4,128)S(1)} all-gather(f32[3,2,512]{2,0,1:T(4,128)S(1)} %copy.220), channel_id=1, replica_groups=mesh['plane'=16,'tile'=32] {'tile'}, dimensions={1}, use_global_device_ids=true | all-gather | bytes 405504 | tf_op jit(solution)/shard_map/all_gather | solution.py:134
  102.8 17.4 %fusion.33 = f32[3,8,2048]{2,1,0:T(8,128)S(1)} fusion(f32[3,8,2048]{2,1,0:T(8,128)S(1)} %copy.225, f32[3,8,2048]{2,1,0:T(8,128)S(1)} %bitcast.137, f32[3,2,2048]{2,1,0:T(2,128)} %collective-permute-done.4, f32[3,2,2048]{2,1,0:T(2,128)} %collective-permute-done.3, f32[3,12,2052]{2,1,0:T(8,128)S(1)} %select_maximum_fusion.2, f32[]{:T(128)} %bitcast.37, ...), kind=kLoop, calls=%fused_computation.74 | loop fusion | flops 2654208 | bytes 4620388 | tf_op jit(solution)/shard_map/add | solution.py:138
  128.2 895.2 %while.13 = (s32[]{:T(128)}, f32[4,2,8,2048]{3,2,1,0:T(8,128)S(1)}, pred[]{:T(512)}, f32[]{:T(128)}, f32[3]{0:T(128)S(1)}, /*index=5*/f32[]{:T(128)}, f32[3]{0:T...) while((s32[]{:T(128)}, f32[4,2,8,2048]{3,2,1,0:T(8,128)S(1)}, ...), condition=%wide.region_2.3_spmd.clone, body=%wide.region_1.2_spmd.sunk.clone.sunk | while | flops 2818050 | bytes 11469090 | solution.py:167
  130.3 2.6 fusion.93
  132.9 2.7 fusion.94
  135.6 9.1 collective-permute-start
  144.7 35.9 %collective-permute-done = f32[4,2,8,2048]{3,2,1,0:T(8,128)S(1)} collective-permute-done((f32[4,2,8,2048]{3,2,1,0:T(8,128)S(1)}, f32[4,2,8,2048]{3,2,1,0:T(8,128)S(1)}, u32[]{:S(2)}, u32[]{:S(2)}) %collective-permute-start) | collective-permute-done | bytes 524320 | tf_op jit(solution)/shard_map/while/body/eval_jaxpr/ppermute | solution.py:28
  182.8 2.6 fusion.93
  185.4 2.7 fusion.94
  188.2 6.8 collective-permute-start
  195.0 27.6 %collective-permute-done = f32[4,2,8,2048]{3,2,1,0:T(8,128)S(1)} collective-permute-done((f32[4,2,8,2048]{3,2,1,0:T(8,128)S(1)}, f32[4,2,8,2048]{3,2,1,0:T(8,128)S(1)}, u32[]{:S(2)}, u32[]{:S(2)}) %collective-permute-start) | collective-permute-done | bytes 524320 | tf_op jit(solution)/shard_map/while/body/eval_jaxpr/ppermute | solution.py:28
  224.8 2.6 fusion.93
  227.4 2.7 fusion.94
  232.1 90.6 %collective-permute-done = f32[4,2,8,2048]{3,2,1,0:T(8,128)S(1)} collective-permute-done((f32[4,2,8,2048]{3,2,1,0:T(8,128)S(1)}, f32[4,2,8,2048]{3,2,1,0:T(8,128)S(1)}, u32[]{:S(2)}, u32[]{:S(2)}) %collective-permute-start) | collective-permute-done | bytes 524320 | tf_op jit(solution)/shard_map/while/body/eval_jaxpr/ppermute | solution.py:28
  324.9 2.6 fusion.93
  327.5 2.7 fusion.94
  330.2 8.4 collective-permute-start
  338.6 54.5 %collective-permute-done = f32[4,2,8,2048]{3,2,1,0:T(8,128)S(1)} collective-permute-done((f32[4,2,8,2048]{3,2,1,0:T(8,128)S(1)}, f32[4,2,8,2048]{3,2,1,0:T(8,128)S(1)}, u32[]{:S(2)}, u32[]{:S(2)}) %collective-permute-start) | collective-permute-done | bytes 524320 | tf_op jit(solution)/shard_map/while/body/eval_jaxpr/ppermute | solution.py:28
  395.3 2.6 fusion.93
  397.9 2.7 fusion.94
  402.6 14.2 %collective-permute-done = f32[4,2,8,2048]{3,2,1,0:T(8,128)S(1)} collective-permute-done((f32[4,2,8,2048]{3,2,1,0:T(8,128)S(1)}, f32[4,2,8,2048]{3,2,1,0:T(8,128)S(1)}, u32[]{:S(2)}, u32[]{:S(2)}) %collective-permute-start) | collective-permute-done | bytes 524320 | tf_op jit(solution)/shard_map/while/body/eval_jaxpr/ppermute | solution.py:28
  419.0 2.6 fusion.93
  421.6 2.7 fusion.94
  424.4 78.4 %collective-permute-start = (f32[4,2,8,2048]{3,2,1,0:T(8,128)S(1)}, f32[4,2,8,2048]{3,2,1,0:T(8,128)S(1)}, u32[]{:S(2)}, u32[]{:S(2)}) collective-permute-start(f32[4,2,8,2048]{3,2,1,0:T(8,128)S(1)} %pad_maximum_fusion.12), channel_id=1, source_target_pairs={{0,32},{32,64},{64,96},{96,128},{128,160},{160,192},{192,224},{224... | collective-permute-start | bytes 1572872 | tf_op jit(solution)/shard_map/while/body/eval_jaxpr/ppermute | solution.py:28
  502.8 10.5 %collective-permute-done = f32[4,2,8,2048]{3,2,1,0:T(8,128)S(1)} collective-permute-done((f32[4,2,8,2048]{3,2,1,0:T(8,128)S(1)}, f32[4,2,8,2048]{3,2,1,0:T(8,128)S(1)}, u32[]{:S(2)}, u32[]{:S(2)}) %collective-permute-start) | collective-permute-done | bytes 524320 | tf_op jit(solution)/shard_map/while/body/eval_jaxpr/ppermute | solution.py:28
  515.6 2.6 fusion.93
  518.2 2.7 fusion.94
  520.9 38.9 %collective-permute-start = (f32[4,2,8,2048]{3,2,1,0:T(8,128)S(1)}, f32[4,2,8,2048]{3,2,1,0:T(8,128)S(1)}, u32[]{:S(2)}, u32[]{:S(2)}) collective-permute-start(f32[4,2,8,2048]{3,2,1,0:T(8,128)S(1)} %pad_maximum_fusion.12), channel_id=1, source_target_pairs={{0,32},{32,64},{64,96},{96,128},{128,160},{160,192},{192,224},{224... | collective-permute-start | bytes 1572872 | tf_op jit(solution)/shard_map/while/body/eval_jaxpr/ppermute | solution.py:28
  559.8 9.2 collective-permute-done
  571.3 2.6 fusion.93
  573.9 2.7 fusion.94
  576.6 86.0 %collective-permute-start = (f32[4,2,8,2048]{3,2,1,0:T(8,128)S(1)}, f32[4,2,8,2048]{3,2,1,0:T(8,128)S(1)}, u32[]{:S(2)}, u32[]{:S(2)}) collective-permute-start(f32[4,2,8,2048]{3,2,1,0:T(8,128)S(1)} %pad_maximum_fusion.12), channel_id=1, source_target_pairs={{0,32},{32,64},{64,96},{96,128},{128,160},{160,192},{192,224},{224... | collective-permute-start | bytes 1572872 | tf_op jit(solution)/shard_map/while/body/eval_jaxpr/ppermute | solution.py:28
  662.6 70.1 %collective-permute-done = f32[4,2,8,2048]{3,2,1,0:T(8,128)S(1)} collective-permute-done((f32[4,2,8,2048]{3,2,1,0:T(8,128)S(1)}, f32[4,2,8,2048]{3,2,1,0:T(8,128)S(1)}, u32[]{:S(2)}, u32[]{:S(2)}) %collective-permute-start) | collective-permute-done | bytes 524320 | tf_op jit(solution)/shard_map/while/body/eval_jaxpr/ppermute | solution.py:28
  735.0 2.6 fusion.93
  737.6 2.7 fusion.94
  740.3 38.8 %collective-permute-start = (f32[4,2,8,2048]{3,2,1,0:T(8,128)S(1)}, f32[4,2,8,2048]{3,2,1,0:T(8,128)S(1)}, u32[]{:S(2)}, u32[]{:S(2)}) collective-permute-start(f32[4,2,8,2048]{3,2,1,0:T(8,128)S(1)} %pad_maximum_fusion.12), channel_id=1, source_target_pairs={{0,32},{32,64},{64,96},{96,128},{128,160},{160,192},{192,224},{224... | collective-permute-start | bytes 1572872 | tf_op jit(solution)/shard_map/while/body/eval_jaxpr/ppermute | solution.py:28
  779.2 52.8 %collective-permute-done = f32[4,2,8,2048]{3,2,1,0:T(8,128)S(1)} collective-permute-done((f32[4,2,8,2048]{3,2,1,0:T(8,128)S(1)}, f32[4,2,8,2048]{3,2,1,0:T(8,128)S(1)}, u32[]{:S(2)}, u32[]{:S(2)}) %collective-permute-start) | collective-permute-done | bytes 524320 | tf_op jit(solution)/shard_map/while/body/eval_jaxpr/ppermute | solution.py:28
  836.8 2.7 fusion.94
  839.5 8.3 collective-permute-start
  847.8 27.7 %collective-permute-done = f32[4,2,8,2048]{3,2,1,0:T(8,128)S(1)} collective-permute-done((f32[4,2,8,2048]{3,2,1,0:T(8,128)S(1)}, f32[4,2,8,2048]{3,2,1,0:T(8,128)S(1)}, u32[]{:S(2)}, u32[]{:S(2)}) %collective-permute-start) | collective-permute-done | bytes 524320 | tf_op jit(solution)/shard_map/while/body/eval_jaxpr/ppermute | solution.py:28
  877.8 2.6 fusion.93
  880.4 2.7 fusion.94
  883.2 8.3 collective-permute-start
  891.5 7.7 collective-permute-done
  901.4 2.6 fusion.93
  904.0 2.7 fusion.94
  906.8 12.1 %collective-permute-start = (f32[4,2,8,2048]{3,2,1,0:T(8,128)S(1)}, f32[4,2,8,2048]{3,2,1,0:T(8,128)S(1)}, u32[]{:S(2)}, u32[]{:S(2)}) collective-permute-start(f32[4,2,8,2048]{3,2,1,0:T(8,128)S(1)} %pad_maximum_fusion.12), channel_id=1, source_target_pairs={{0,32},{32,64},{64,96},{96,128},{128,160},{160,192},{192,224},{224... | collective-permute-start | bytes 1572872 | tf_op jit(solution)/shard_map/while/body/eval_jaxpr/ppermute | solution.py:28
  918.9 12.8 %collective-permute-done = f32[4,2,8,2048]{3,2,1,0:T(8,128)S(1)} collective-permute-done((f32[4,2,8,2048]{3,2,1,0:T(8,128)S(1)}, f32[4,2,8,2048]{3,2,1,0:T(8,128)S(1)}, u32[]{:S(2)}, u32[]{:S(2)}) %collective-permute-start) | collective-permute-done | bytes 524320 | tf_op jit(solution)/shard_map/while/body/eval_jaxpr/ppermute | solution.py:28
  936.5 2.7 fusion.94
  939.2 8.3 collective-permute-start
  947.5 20.1 %collective-permute-done = f32[4,2,8,2048]{3,2,1,0:T(8,128)S(1)} collective-permute-done((f32[4,2,8,2048]{3,2,1,0:T(8,128)S(1)}, f32[4,2,8,2048]{3,2,1,0:T(8,128)S(1)}, u32[]{:S(2)}, u32[]{:S(2)}) %collective-permute-start) | collective-permute-done | bytes 524320 | tf_op jit(solution)/shard_map/while/body/eval_jaxpr/ppermute | solution.py:28
  972.5 2.7 fusion.94
  975.2 3.0 collective-permute-start
  978.2 21.6 %collective-permute-done = f32[4,2,8,2048]{3,2,1,0:T(8,128)S(1)} collective-permute-done((f32[4,2,8,2048]{3,2,1,0:T(8,128)S(1)}, f32[4,2,8,2048]{3,2,1,0:T(8,128)S(1)}, u32[]{:S(2)}, u32[]{:S(2)}) %collective-permute-start) | collective-permute-done | bytes 524320 | tf_op jit(solution)/shard_map/while/body/eval_jaxpr/ppermute | solution.py:28
  1004.7 2.7 fusion.94
  1009.3 14.0 %collective-permute-done = f32[4,2,8,2048]{3,2,1,0:T(8,128)S(1)} collective-permute-done((f32[4,2,8,2048]{3,2,1,0:T(8,128)S(1)}, f32[4,2,8,2048]{3,2,1,0:T(8,128)S(1)}, u32[]{:S(2)}, u32[]{:S(2)}) %collective-permute-start) | collective-permute-done | bytes 524320 | tf_op jit(solution)/shard_map/while/body/eval_jaxpr/ppermute | solution.py:28
  1027.4 2.7 fusion.22
  (202 shorter events, 90.5 us)
Async XLA Ops:
  0.0 30.7 %copy-start = (f32[32,9]{0,1:T(8,128)S(1)}, f32[32,9]{0,1:T(8,128)}, u32[]{:S(2)}) copy-start(f32[32,9]{0,1:T(8,128)} %param.11) | copy-start | bytes 3460
  1.1 14.3 %collective-permute-start.1 = (f32[3,2,2048]{2,1,0:T(2,128)S(1)}, f32[3,2,2048]{2,1,0:T(2,128)S(1)}, u32[]{:S(2)}, u32[]{:S(2)}) collective-permute-start(f32[3,2,2048]{2,1,0:T(2,128)S(1)} %get-tuple-element.225), channel_id=1, source_target_pairs={{0,1},{1,2},{2,3},{3,4},{4,5},{5,6},{6,7},{7,8},{8,9},{9,10},{10,1... | collective-permute-start | bytes 147464 | tf_op jit(solution)/shard_map/ppermute | solution.py:17
  3.0 12.4 %collective-permute-start.2 = (f32[3,2,2048]{2,1,0:T(2,128)S(1)}, f32[3,2,2048]{2,1,0:T(2,128)S(1)}, u32[]{:S(2)}, u32[]{:S(2)}) collective-permute-start(f32[3,2,2048]{2,1,0:T(2,128)S(1)} %get-tuple-element.226), channel_id=1, source_target_pairs={{1,0},{2,1},{3,2},{4,3},{5,4},{6,5},{7,6},{8,7},{9,8},{10,9},{11,1... | collective-permute-start | bytes 147464 | tf_op jit(solution)/shard_map/ppermute | solution.py:20
  30.7 7.6 copy-start.5
  30.8 7.6 copy-start.6
  43.0 53.4 %copy-start.3 = (f32[64]{0:T(128)S(1)}, f32[64]{0:T(128)}, u32[]{:S(2)}) copy-start(f32[64]{0:T(128)} %iota_convert_fusion.1) | copy-start | bytes 772
  43.0 53.4 %copy-start.4 = (f32[2]{0:T(128)S(1)}, f32[2]{0:T(128)}, u32[]{:S(2)}) copy-start(f32[2]{0:T(128)} %add_convert_fusion) | copy-start | bytes 28
  43.0 53.9 %copy-start.2 = (f32[512]{0:T(512)S(1)}, f32[512]{0:T(512)}, u32[]{:S(2)}) copy-start(f32[512]{0:T(512)} %iota_convert_fusion) | copy-start | bytes 6148
  50.9 50.8 %collective-permute-start.3 = (f32[3,2,2048]{2,1,0:T(2,128)}, f32[3,2,2048]{2,1,0:T(2,128)}, u32[]{:S(2)}, u32[]{:S(2)}) collective-permute-start(f32[3,2,2048]{2,1,0:T(2,128)} %get-tuple-element.221), channel_id=1, source_target_pairs={{0,1},{1,2},{2,3},{3,4},{4,5},{5,6},{6,7},{7,8},{8,9},{9,10},{10,1... | collective-permute-start | bytes 147464 | tf_op jit(solution)/shard_map/ppermute | solution.py:17
  52.8 48.9 %collective-permute-start.4 = (f32[3,2,2048]{2,1,0:T(2,128)}, f32[3,2,2048]{2,1,0:T(2,128)}, u32[]{:S(2)}, u32[]{:S(2)}) collective-permute-start(f32[3,2,2048]{2,1,0:T(2,128)} %get-tuple-element.222), channel_id=1, source_target_pairs={{1,0},{2,1},{3,2},{4,3},{5,4},{6,5},{7,6},{8,7},{9,8},{10,9},{11,1... | collective-permute-start | bytes 147464 | tf_op jit(solution)/shard_map/ppermute | solution.py:20
  101.7 26.3 %copy-start.1 = (f32[4,2]{1,0:T(4,128)S(1)}, f32[4,2]{1,0:T(4,128)}, u32[]{:S(2)}) copy-start(f32[4,2]{1,0:T(4,128)} %constant.62.clone) | copy-start | bytes 100
  120.3 6.8 collective-permute-start.5
  122.2 5.1 collective-permute-start.6
  135.6 45.0 %collective-permute-start = (f32[4,2,8,2048]{3,2,1,0:T(8,128)S(1)}, f32[4,2,8,2048]{3,2,1,0:T(8,128)S(1)}, u32[]{:S(2)}, u32[]{:S(2)}) collective-permute-start(f32[4,2,8,2048]{3,2,1,0:T(8,128)S(1)} %pad_maximum_fusion.12), channel_id=1, source_target_pairs={{0,32},{32,64},{64,96},{96,128},{128,160},{160,192},{192,224},{224... | collective-permute-start | bytes 1572872 | tf_op jit(solution)/shard_map/while/body/eval_jaxpr/ppermute | solution.py:28
  188.2 34.4 %collective-permute-start = (f32[4,2,8,2048]{3,2,1,0:T(8,128)S(1)}, f32[4,2,8,2048]{3,2,1,0:T(8,128)S(1)}, u32[]{:S(2)}, u32[]{:S(2)}) collective-permute-start(f32[4,2,8,2048]{3,2,1,0:T(8,128)S(1)} %pad_maximum_fusion.12), channel_id=1, source_target_pairs={{0,32},{32,64},{64,96},{96,128},{128,160},{160,192},{192,224},{224... | collective-permute-start | bytes 1572872 | tf_op jit(solution)/shard_map/while/body/eval_jaxpr/ppermute | solution.py:28
  230.1 92.5 %collective-permute-start = (f32[4,2,8,2048]{3,2,1,0:T(8,128)S(1)}, f32[4,2,8,2048]{3,2,1,0:T(8,128)S(1)}, u32[]{:S(2)}, u32[]{:S(2)}) collective-permute-start(f32[4,2,8,2048]{3,2,1,0:T(8,128)S(1)} %pad_maximum_fusion.12), channel_id=1, source_target_pairs={{0,32},{32,64},{64,96},{96,128},{128,160},{160,192},{192,224},{224... | collective-permute-start | bytes 1572872 | tf_op jit(solution)/shard_map/while/body/eval_jaxpr/ppermute | solution.py:28
  330.2 62.8 %collective-permute-start = (f32[4,2,8,2048]{3,2,1,0:T(8,128)S(1)}, f32[4,2,8,2048]{3,2,1,0:T(8,128)S(1)}, u32[]{:S(2)}, u32[]{:S(2)}) collective-permute-start(f32[4,2,8,2048]{3,2,1,0:T(8,128)S(1)} %pad_maximum_fusion.12), channel_id=1, source_target_pairs={{0,32},{32,64},{64,96},{96,128},{128,160},{160,192},{192,224},{224... | collective-permute-start | bytes 1572872 | tf_op jit(solution)/shard_map/while/body/eval_jaxpr/ppermute | solution.py:28
  400.6 16.1 %collective-permute-start = (f32[4,2,8,2048]{3,2,1,0:T(8,128)S(1)}, f32[4,2,8,2048]{3,2,1,0:T(8,128)S(1)}, u32[]{:S(2)}, u32[]{:S(2)}) collective-permute-start(f32[4,2,8,2048]{3,2,1,0:T(8,128)S(1)} %pad_maximum_fusion.12), channel_id=1, source_target_pairs={{0,32},{32,64},{64,96},{96,128},{128,160},{160,192},{192,224},{224... | collective-permute-start | bytes 1572872 | tf_op jit(solution)/shard_map/while/body/eval_jaxpr/ppermute | solution.py:28
  424.4 89.0 %collective-permute-start = (f32[4,2,8,2048]{3,2,1,0:T(8,128)S(1)}, f32[4,2,8,2048]{3,2,1,0:T(8,128)S(1)}, u32[]{:S(2)}, u32[]{:S(2)}) collective-permute-start(f32[4,2,8,2048]{3,2,1,0:T(8,128)S(1)} %pad_maximum_fusion.12), channel_id=1, source_target_pairs={{0,32},{32,64},{64,96},{96,128},{128,160},{160,192},{192,224},{224... | collective-permute-start | bytes 1572872 | tf_op jit(solution)/shard_map/while/body/eval_jaxpr/ppermute | solution.py:28
  520.9 48.1 %collective-permute-start = (f32[4,2,8,2048]{3,2,1,0:T(8,128)S(1)}, f32[4,2,8,2048]{3,2,1,0:T(8,128)S(1)}, u32[]{:S(2)}, u32[]{:S(2)}) collective-permute-start(f32[4,2,8,2048]{3,2,1,0:T(8,128)S(1)} %pad_maximum_fusion.12), channel_id=1, source_target_pairs={{0,32},{32,64},{64,96},{96,128},{128,160},{160,192},{192,224},{224... | collective-permute-start | bytes 1572872 | tf_op jit(solution)/shard_map/while/body/eval_jaxpr/ppermute | solution.py:28
  576.6 156.1 %collective-permute-start = (f32[4,2,8,2048]{3,2,1,0:T(8,128)S(1)}, f32[4,2,8,2048]{3,2,1,0:T(8,128)S(1)}, u32[]{:S(2)}, u32[]{:S(2)}) collective-permute-start(f32[4,2,8,2048]{3,2,1,0:T(8,128)S(1)} %pad_maximum_fusion.12), channel_id=1, source_target_pairs={{0,32},{32,64},{64,96},{96,128},{128,160},{160,192},{192,224},{224... | collective-permute-start | bytes 1572872 | tf_op jit(solution)/shard_map/while/body/eval_jaxpr/ppermute | solution.py:28
  740.3 91.6 %collective-permute-start = (f32[4,2,8,2048]{3,2,1,0:T(8,128)S(1)}, f32[4,2,8,2048]{3,2,1,0:T(8,128)S(1)}, u32[]{:S(2)}, u32[]{:S(2)}) collective-permute-start(f32[4,2,8,2048]{3,2,1,0:T(8,128)S(1)} %pad_maximum_fusion.12), channel_id=1, source_target_pairs={{0,32},{32,64},{64,96},{96,128},{128,160},{160,192},{192,224},{224... | collective-permute-start | bytes 1572872 | tf_op jit(solution)/shard_map/while/body/eval_jaxpr/ppermute | solution.py:28
  839.5 36.1 %collective-permute-start = (f32[4,2,8,2048]{3,2,1,0:T(8,128)S(1)}, f32[4,2,8,2048]{3,2,1,0:T(8,128)S(1)}, u32[]{:S(2)}, u32[]{:S(2)}) collective-permute-start(f32[4,2,8,2048]{3,2,1,0:T(8,128)S(1)} %pad_maximum_fusion.12), channel_id=1, source_target_pairs={{0,32},{32,64},{64,96},{96,128},{128,160},{160,192},{192,224},{224... | collective-permute-start | bytes 1572872 | tf_op jit(solution)/shard_map/while/body/eval_jaxpr/ppermute | solution.py:28
  883.2 16.0 %collective-permute-start = (f32[4,2,8,2048]{3,2,1,0:T(8,128)S(1)}, f32[4,2,8,2048]{3,2,1,0:T(8,128)S(1)}, u32[]{:S(2)}, u32[]{:S(2)}) collective-permute-start(f32[4,2,8,2048]{3,2,1,0:T(8,128)S(1)} %pad_maximum_fusion.12), channel_id=1, source_target_pairs={{0,32},{32,64},{64,96},{96,128},{128,160},{160,192},{192,224},{224... | collective-permute-start | bytes 1572872 | tf_op jit(solution)/shard_map/while/body/eval_jaxpr/ppermute | solution.py:28
  906.8 24.9 %collective-permute-start = (f32[4,2,8,2048]{3,2,1,0:T(8,128)S(1)}, f32[4,2,8,2048]{3,2,1,0:T(8,128)S(1)}, u32[]{:S(2)}, u32[]{:S(2)}) collective-permute-start(f32[4,2,8,2048]{3,2,1,0:T(8,128)S(1)} %pad_maximum_fusion.12), channel_id=1, source_target_pairs={{0,32},{32,64},{64,96},{96,128},{128,160},{160,192},{192,224},{224... | collective-permute-start | bytes 1572872 | tf_op jit(solution)/shard_map/while/body/eval_jaxpr/ppermute | solution.py:28
  939.2 28.4 %collective-permute-start = (f32[4,2,8,2048]{3,2,1,0:T(8,128)S(1)}, f32[4,2,8,2048]{3,2,1,0:T(8,128)S(1)}, u32[]{:S(2)}, u32[]{:S(2)}) collective-permute-start(f32[4,2,8,2048]{3,2,1,0:T(8,128)S(1)} %pad_maximum_fusion.12), channel_id=1, source_target_pairs={{0,32},{32,64},{64,96},{96,128},{128,160},{160,192},{192,224},{224... | collective-permute-start | bytes 1572872 | tf_op jit(solution)/shard_map/while/body/eval_jaxpr/ppermute | solution.py:28
  975.2 24.6 %collective-permute-start = (f32[4,2,8,2048]{3,2,1,0:T(8,128)S(1)}, f32[4,2,8,2048]{3,2,1,0:T(8,128)S(1)}, u32[]{:S(2)}, u32[]{:S(2)}) collective-permute-start(f32[4,2,8,2048]{3,2,1,0:T(8,128)S(1)} %pad_maximum_fusion.12), channel_id=1, source_target_pairs={{0,32},{32,64},{64,96},{96,128},{128,160},{160,192},{192,224},{224... | collective-permute-start | bytes 1572872 | tf_op jit(solution)/shard_map/while/body/eval_jaxpr/ppermute | solution.py:28
  1007.4 15.9 %collective-permute-start = (f32[4,2,8,2048]{3,2,1,0:T(8,128)S(1)}, f32[4,2,8,2048]{3,2,1,0:T(8,128)S(1)}, u32[]{:S(2)}, u32[]{:S(2)}) collective-permute-start(f32[4,2,8,2048]{3,2,1,0:T(8,128)S(1)} %pad_maximum_fusion.12), channel_id=1, source_target_pairs={{0,32},{32,64},{64,96},{96,128},{128,160},{160,192},{192,224},{224... | collective-permute-start | bytes 1572872 | tf_op jit(solution)/shard_map/while/body/eval_jaxpr/ppermute | solution.py:28
where the time goes:
time: 1030 us
  waiting for transfers between devices  469 us (46%)
  starting transfers between devices  328 us (32%)
  other arithmetic  138 us (13%)
  local copies, waits for them, and re-layouts  43.6 us (4%)
  blocking collectives  36.7 us (4%)
  matrix products  12.7 us (1%)
    ppermute x15, waiting for transfers between devices, from_behind(): return lax.ppermute(value, axis, pairs)  469 us
    ppermute x15, starting transfers between devices, from_behind(): return lax.ppermute(value, axis, pairs)  312 us
    sub x48, other arithmetic, lens_step(): (1.0 - mixing) * previous + mixing * current - bending * bent_rows  105 us
    all_gather x1, blocking collectives, body(): received = lax.all_gather(coarse, 'tile', axis=1, tiled=True)  36.7 us
  transfers between devices with their start and end apart: 21, of which 16 were waited for; matrix products, arithmetic and copies ran while one was open for 2% of the time, Pallas kernels for 0%

commit v1 on v0

v1 whole, which is shorter than its diff:
```python
import functools
import math

import jax
import jax.numpy as jnp
from jax import lax
from jax.experimental import pallas as pl
from jax.experimental.pallas import tpu as pltpu
from jax.sharding import PartitionSpec as P

f32 = jnp.float32
bf16 = jnp.bfloat16
lens_gain = 0.25
channels = 32
highest = lax.Precision.HIGHEST


def distances(plane_slot, slot_total):
    distance = (plane_slot.astype(f32) + 1.0) / slot_total
    before = jnp.concatenate([jnp.zeros((1,), f32), distance[:-1]])
    after = jnp.concatenate([distance[1:], jnp.full((1,), (slot_total + 1.0) / slot_total, f32)])
    mixing = before * (after - distance) / (distance * (after - before))
    bending = lens_gain * (after - distance) / after
    return (mixing, bending)


def shifted(value, by):
    width = value.shape[-1]
    rolled = pltpu.roll(value, (-by) % width, value.ndim - 1)
    lane = lax.broadcasted_iota(jnp.int32, value.shape, value.ndim - 1)
    keep = lane < width - by if by > 0 else lane >= -by
    return jnp.where(keep, rolled, 0.0)


def paint_matrix(paint_weight, paint_bias):
    high = lax.reduce_precision(paint_weight, 8, 7)
    low = lax.reduce_precision(paint_weight - high, 8, 7)
    bias_0 = lax.reduce_precision(paint_bias, 8, 7)
    bias_1 = lax.reduce_precision(paint_bias - bias_0, 8, 7)
    bias_2 = paint_bias - bias_0 - bias_1
    spread = lambda value: jnp.repeat(value, 8, axis=0)
    high, low = spread(high), spread(low)
    shape = (channels * 8, 160)
    row = lax.broadcasted_iota(jnp.int32, shape, 0) % 8
    col = lax.broadcasted_iota(jnp.int32, shape, 1)
    part, in_row = col // 16, col % 16
    total = jnp.zeros(shape, f32)
    for i in range(3):
        for j in range(3):
            here = (in_row == row + 2 * i) & (part % 3 == j) & (part < 9)
            tap = 3 * i + j
            value = jnp.where(part < 6, high[:, tap : tap + 1], low[:, tap : tap + 1])
            total = jnp.where(here, value, total)
    for k, value in enumerate((bias_0, bias_1, bias_2)):
        total = jnp.where(col == 144 + k, spread(value[:, None]), total)
    return total.astype(bf16)


def paint_kernel(edge_ref, mix_ref, x_ref, low_ref, high_ref, w_ref, pool_ref, c_ref, coarse_ref, wide, stack, sums):
    cols = x_ref.shape[-1]
    wide[...] = jnp.zeros_like(wide)
    sums[...] = jnp.zeros_like(sums)
    stack[144:160, :] = jnp.ones((16, cols), bf16)
    first = edge_ref[0] == 0
    last = edge_ref[1] == 0
    row = lax.broadcasted_iota(jnp.int32, (8, 256), 0)
    for p in range(3):
        wide[0, 0:5, :] = low_ref[p]
        wide[0, 5:13, :] = x_ref[p]
        wide[1, 0:7, :] = x_ref[p, 1:8, :]
        wide[1, 7:12, :] = high_ref[p]
        for window in range(2):
            value = wide[window]
            for j in range(3):
                moved = value if j == 1 else shifted(value, 2 * (j - 1))
                upper = moved.astype(bf16)
                lower = (moved - upper.astype(f32)).astype(bf16)
                stack[16 * j : 16 * j + 16, :] = upper
                stack[48 + 16 * j : 64 + 16 * j, :] = lower
                stack[96 + 16 * j : 112 + 16 * j, :] = upper

            def one_chunk(chunk, carry):
                at = pl.ds(pl.multiple_of(chunk * 256, 256), 256)
                before = jnp.dot(w_ref[...], stack[:, at], preferred_element_type=f32)
                total = jnp.zeros((8, 256), f32)
                for c in range(channels):
                    total = total + mix_ref[c] * jnp.tanh(before[8 * c : 8 * c + 8, :])
                if window == 0:
                    total = jnp.where(first & (row < 3), 0.0, total)
                    c_ref[p, 0:8, at] = total
                else:
                    total = jnp.where(last & (row >= 5), 0.0, total)
                    c_ref[p, 8:14, at] = total[2:8]
                return carry

            lax.fori_loop(0, cols // 256, one_chunk, 0)
        value = c_ref[p, 3:11, :]
        sums[p : p + 1, :] = jnp.sum(value[0:4], axis=0, keepdims=True)
        sums[3 + p : 4 + p, :] = jnp.sum(value[4:8], axis=0, keepdims=True)
    c_ref[:, 14:16, :] = jnp.zeros((3, 2, cols), f32)
    quarter = cols // 4
    stacked = jnp.concatenate([sums[:, quarter * v : quarter * (v + 1)] for v in range(4)], axis=0)
    pooled = jnp.dot(stacked, pool_ref[...], precision=highest, preferred_element_type=f32)
    for v in range(4):
        coarse_ref[:, 128 * v : 128 * v + 128] = pooled[8 * v : 8 * v + 8]


def short_kernel_body(k_ref, c_ref, s_ref, held):
    cols = c_ref.shape[-1]
    for p in range(3):
        held[0:16, :] = c_ref[p]
        held[16:24, :] = jnp.zeros((8, cols), f32)
        for window in range(2):
            total = jnp.zeros((8, cols), f32)
            for b in range(5):
                part = jnp.zeros((8, cols), f32)
                for a in range(5):
                    start = 8 * window + a
                    part = part + k_ref[5 * a + b] * held[start : start + 8, :]
                total = total + (part if b == 2 else shifted(part, b - 2))
            s_ref[p, 8 * window : 8 * window + 8, :] = total


def bend_kernel(decay, gain, edge_ref, s_ref, coarse_ref, acc_ref, ec_ref, grow_ref, u_ref, rows, pot):
    cols = s_ref.shape[-1]
    e = decay
    c0, c1 = coarse_ref[0:3, :], coarse_ref[3:6, :]
    up, down = acc_ref[0:3, :], acc_ref[3:6, :]
    rows[12:16, :] = jnp.zeros((4, rows.shape[-1]), f32)
    rows[0:3, :] = e * c0 + e * e * c1 + e * e * down + up * (1.0 / e)
    rows[3:6, :] = c0 + e * c1 + up + e * down
    rows[6:9, :] = c1 + e * c0 + e * up + down
    rows[9:12, :] = e * e * c0 + e * c1 + e * e * up + down * (1.0 / e)
    smooth = gain * jnp.dot(rows[...], ec_ref[...], precision=highest, preferred_element_type=f32)
    stacked = jnp.concatenate([smooth[:, 128 * v : 128 * v + 128] for v in range(4)], axis=0)
    grown = jnp.dot(stacked, grow_ref[...], precision=highest, preferred_element_type=f32)
    long = jnp.concatenate([grown[16 * v : 16 * v + 16] for v in range(4)], axis=1)
    row = lax.broadcasted_iota(jnp.int32, (8, cols), 0)
    top = edge_ref[0] != 0
    bottom = edge_ref[1] != 0
    for p in range(3):
        part = s_ref[p]
        wide = jnp.where(
            row < 4,
            jnp.broadcast_to(long[3 + p : 4 + p], (8, cols)),
            jnp.broadcast_to(long[6 + p : 7 + p], (8, cols)),
        )
        here = part[1:9] + wide
        pot[7:8, :] = jnp.where(top, part[0:1] + long[p : p + 1], 0.0)
        pot[8:16, :] = here
        pot[16:17, :] = jnp.where(bottom, part[9:10] + long[9 + p : 10 + p], 0.0)
        above, below = pot[7:15, :], pot[9:17, :]
        u11 = below - 2.0 * here + above
        u22 = shifted(here, 1) - 2.0 * here + shifted(here, -1)
        step = below - above
        u12 = (shifted(step, 1) - shifted(step, -1)) * 0.25
        for d in range(cols // 128):
            at = slice(128 * d, 128 * d + 128)
            u_ref[9 * d + 3 * p] = u11[:, at]
            u_ref[9 * d + 3 * p + 1] = u12[:, at]
            u_ref[9 * d + 3 * p + 2] = u22[:, at]


def advance(previous, current, u11, u12, u22, mixing, bending):
    kept = 1.0 - mixing
    bent = (
        u11 * current[0] + u12 * current[2],
        u11 * current[1] + u12 * current[3],
        u12 * current[0] + u22 * current[2],
        u12 * current[1] + u22 * current[3],
    )
    return tuple(kept * previous[i] + mixing * current[i] - bending * bent[i] for i in range(4))


def scan_kernel(mixing_ref, bending_ref, u_ref, state_ref):
    one = jnp.ones((8, 128), f32)
    zero = jnp.zeros((8, 128), f32)
    groups = u_ref.shape[0] // 9

    def one_group(g, carry):
        previous, current = carry
        for i in range(4):
            state_ref[8 * g + i] = previous[i]
            state_ref[8 * g + 4 + i] = current[i]
        for p in range(3):
            at = 9 * g + 3 * p
            k = 3 * g + p
            later = advance(previous, current, u_ref[at], u_ref[at + 1], u_ref[at + 2], mixing_ref[k], bending_ref[k])
            previous, current = current, later
        return (previous, current)

    start = (one, zero, zero, one)
    lax.fori_loop(0, groups, one_group, (start, start))


def final_kernel(mixing_ref, bending_ref, u_ref, state_ref, out_ref):
    blocks = u_ref.shape[0] // 9

    def one_block(d, carry):
        at = pl.ds(pl.multiple_of(d * 128, 128), 128)
        previous = tuple(state_ref[8 * d + i] for i in range(4))
        current = tuple(state_ref[8 * d + 4 + i] for i in range(4))
        for p in range(3):
            k = 9 * d + 3 * p
            later = advance(
                previous, current, u_ref[k], u_ref[k + 1], u_ref[k + 2], mixing_ref[p], bending_ref[p]
            )
            for i in range(4):
                out_ref[i, p, :, at] = later[i]
            previous, current = current, later
        return carry

    lax.fori_loop(0, blocks, one_block, 0)


vmem = pl.BlockSpec(memory_space=pltpu.VMEM)
smem = pl.BlockSpec(memory_space=pltpu.SMEM)


def sds(*shape):
    return jax.ShapeDtypeStruct(shape, f32)


def call(kernel, name, n_smem, n_vmem, out_shape, scratch=(), cost=(0, 0, 0)):
    outs = jax.tree.map(lambda _: vmem, out_shape)
    return pl.pallas_call(
        kernel,
        name=name,
        out_shape=out_shape,
        in_specs=[smem] * n_smem + [vmem] * n_vmem,
        out_specs=outs,
        scratch_shapes=list(scratch),
        cost_estimate=pl.CostEstimate(flops=cost[0], bytes_accessed=cost[1], transcendentals=cost[2]),
        compiler_params=pltpu.CompilerParams(vmem_limit_bytes=24 << 20),
    )


def row_scan(message, tile_index, tile_count):
    row = lax.broadcasted_iota(jnp.int32, (8, 1), 0)
    forward = row < 3
    block = message
    total = jnp.zeros_like(message)
    size = 1
    while size < tile_count:
        received = lax.ppermute(block, "tile", [(i, i ^ size) for i in range(tile_count)])
        from_lower = (tile_index & size) != 0
        place = (tile_index % size).astype(f32)
        weight = jnp.where(forward, jnp.exp(-place / 8.0), jnp.exp(-(size - 1 - place) / 8.0))
        used = forward == from_lower
        total = total + jnp.where(used, weight, 0.0) * received
        far = math.exp(-size / 8.0)
        block = jnp.where(used, block + far * received, far * block + received)
        size *= 2
    return total


def body(density, plane_slot, paint_weight, paint_bias, mix_weight, short_kernel):
    plane_count, row_count, col_count = density.shape
    tile_count = lax.axis_size("tile")
    group_count = lax.axis_size("plane")
    tile_index = lax.axis_index("tile")
    plane_index = lax.axis_index("plane")
    coarse_cols = col_count // 4
    row_scale = row_count * tile_count / 16.0
    col_scale = col_count / 16.0
    long_gain = 1.0 / math.sqrt(row_scale * col_scale)
    decay = math.exp(-1.0 / row_scale)

    up = [(i, i + 1) for i in range(tile_count - 1)]
    low = lax.ppermute(density[:, 3:8, :], "tile", up)
    high = lax.ppermute(density[:, 0:5, :], "tile", [(b, a) for a, b in up])

    edge = jnp.stack([tile_index, tile_count - 1 - tile_index]).astype(jnp.int32)
    mixing, bending = distances(plane_slot, 2 * plane_slot.shape[0])
    mixing_here = lax.dynamic_slice_in_dim(mixing, plane_index * plane_count, plane_count)
    bending_here = lax.dynamic_slice_in_dim(bending, plane_index * plane_count, plane_count)
    weights = paint_matrix(paint_weight, paint_bias)
    gap = lax.broadcasted_iota(jnp.int32, (coarse_cols, coarse_cols), 0) - lax.broadcasted_iota(
        jnp.int32, (coarse_cols, coarse_cols), 1
    )
    col_kernel = jnp.exp(-jnp.abs(gap.astype(f32)) / col_scale)
    pool = jnp.where(
        lax.broadcasted_iota(jnp.int32, (512, 128), 0) // 4 == lax.broadcasted_iota(jnp.int32, (512, 128), 1),
        1.0 / 16.0,
        0.0,
    ).astype(f32)
    grow = jnp.where(
        lax.broadcasted_iota(jnp.int32, (128, 512), 1) // 4 == lax.broadcasted_iota(jnp.int32, (128, 512), 0), 1.0, 0.0
    ).astype(f32)

    convergence, coarse = call(
        paint_kernel,
        "paint",
        2,
        5,
        (sds(3, 16, col_count), sds(8, coarse_cols)),
        [pltpu.VMEM((2, 16, col_count), f32), pltpu.VMEM((160, col_count), bf16), pltpu.VMEM((8, col_count), f32)],
        (8 * 10**9, 2 * 10**6, 10**6),
    )(edge, mix_weight, density, low, high, weights, pool)

    e = decay
    c0, c1 = coarse[0:3], coarse[3:6]
    message = jnp.concatenate([e * e * c0 + e * c1, e * c0 + e * e * c1, jnp.zeros_like(coarse[0:2])], axis=0)
    received = row_scan(message, tile_index, tile_count)

    short_part = call(
        short_kernel_body,
        "short",
        1,
        1,
        sds(3, 16, col_count),
        [pltpu.VMEM((24, col_count), f32)],
        (10**7, 10**6, 0),
    )(short_kernel.reshape(25), convergence)

    shear = call(
        functools.partial(bend_kernel, decay, long_gain),
        "bend",
        1,
        5,
        sds(group_count * 9, 8, 128),
        [pltpu.VMEM((16, coarse_cols), f32), pltpu.VMEM((24, col_count), f32)],
        (10**8, 2 * 10**6, 0),
    )(edge, short_part, coarse, received, col_kernel, grow)

    gathered = lax.all_to_all(shear, "plane", 0, 0, tiled=True)
    states = call(scan_kernel, "scan", 2, 1, sds(group_count * 8, 8, 128), (), (10**7, 10**6, 0))(
        mixing, bending, gathered
    )
    mine = lax.all_to_all(states, "plane", 0, 0, tiled=True)
    return call(final_kernel, "final", 2, 2, sds(4, plane_count, row_count, col_count), (), (10**7, 10**6, 0))(
        mixing_here, bending_here, shear, mine
    )


def solution(mesh):
    placed = (P("plane", "tile", None), P(), P(), P(), P(), P())
    return jax.shard_map(
        body, mesh=mesh, in_specs=placed, out_specs=P(None, "plane", "tile", None), check_vma=False
    )
```

time: 1030 us -> 148 us (0.14)
  the two profiles are of different devices: /device:TPU:108 before, /device:TPU:64 now
where the time goes in v1:
time: 148 us; the launch traced here: 147 us
  waiting for transfers between devices  77.9 us (53%)
  starting transfers between devices  41.4 us (28%)
  Pallas kernels  20.5 us (14%)
  local copies, waits for them, and re-layouts  4.12 us (3%)
  other arithmetic  2.35 us (2%)
    all_to_all x1, waiting for transfers between devices, body(): mine = lax.all_to_all(states, 'plane', 0, 0, tiled=True)  33.5 us
    all_to_all x1, waiting for transfers between devices, body(): gathered = lax.all_to_all(shear, 'plane', 0, 0, tiled=True)  33.2 us
    all_to_all x1, starting transfers between devices, body(): gathered = lax.all_to_all(shear, 'plane', 0, 0, tiled=True)  16 us
    ppermute x5, starting transfers between devices, row_scan(): lax.ppermute(block, 'tile', [(i, i ^ size) for i in range(tile_count)])  14.2 us
    pallas_call x1, Pallas kernels, body(): call(paint_kernel, 'paint', 2, 5, (sds(3, 16, col_count), sds(8, coarse_c...  11.7 us
    ppermute x5, waiting for transfers between devices, row_scan(): lax.ppermute(block, 'tile', [(i, i ^ size) for i in range(tile_count)])  11.3 us
    ppermute x1, starting transfers between devices, body(): high = lax.ppermute(density[:, 0:5, :], 'tile', [(b, a) for a, b in up])  5.75 us
    all_to_all x1, starting transfers between devices, body(): mine = lax.all_to_all(states, 'plane', 0, 0, tiled=True)  3.57 us
  transfers between devices with their start and end apart: 9, of which 7 were waited for; matrix products, arithmetic and copies ran while one was open for 2% of the time, Pallas kernels for 2%

profile of v1, /device:TPU:64, one launch (start us, length us, event | category | flops | bytes accessed | tf_op | source)
XLA Modules:
  0.0 147.1 jit_solution(17391408939625795234)
XLA Ops:
  0.0 1.0 fusion.47
  1.1 1.9 %collective-permute-start = (f32[3,5,2048]{2,1,0:T(8,128)S(1)}, f32[3,5,2048]{2,1,0:T(8,128)S(1)}, u32[]{:S(2)}, u32[]{:S(2)}) collective-permute-start(f32[3,5,2048]{2,1,0:T(8,128)S(1)} %get-tuple-element.10), channel_id=1, source_target_pairs={{0,1},{1,2},{2,3},{3,4},{4,5},{5,6},{6,7},{7,8},{8,9},{9,10},{10,1... | collective-permute-start | bytes 368648 | tf_op jit(solution)/shard_map/ppermute | solution.py:270
  3.0 5.8 %collective-permute-start.1 = (f32[3,5,2048]{2,1,0:T(8,128)S(1)}, f32[3,5,2048]{2,1,0:T(8,128)S(1)}, u32[]{:S(2)}, u32[]{:S(2)}) collective-permute-start(f32[3,5,2048]{2,1,0:T(8,128)S(1)} %get-tuple-element.9), channel_id=1, source_target_pairs={{1,0},{2,1},{3,2},{4,3},{5,4},{6,5},{7,6},{8,7},{9,8},{10,9},{11,1... | collective-permute-start | bytes 368648 | tf_op jit(solution)/shard_map/ppermute | solution.py:271
  8.9 0.3 fusion.39.pool_ref
  9.2 0.0 copy-start.2
  9.2 0.2 multiply_exponential_fusion.ec_ref
  9.4 0.5 copy-done.2
  9.9 0.1 broadcast_in_dim.266
  10.0 0.1 reshape.65
  10.1 0.1 broadcast_in_dim.269
  10.2 0.1 reshape.66
  10.4 0.0 copy-start.5
  10.4 0.6 copy-done.5
  11.0 0.1 broadcast_in_dim.257
  11.1 0.1 broadcast_in_dim.258
  11.2 0.1 broadcast_in_dim.260
  11.3 0.1 broadcast_in_dim.261
  11.4 0.1 broadcast_in_dim.263
  11.5 0.0 copy-start
  11.5 0.1 broadcast_in_dim.264
  11.8 1.1 fusion.26.w_ref
  12.9 0.1 pad_add_fusion.edge_ref
  13.1 0.1 pad.2.clone
  13.2 0.0 copy-start.1
  13.2 0.0 collective-permute-done.low_ref
  13.2 0.0 collective-permute-done.1.high_ref
  13.2 0.0 copy-done
  13.3 0.6 copy-done.1
  13.9 11.7 %paint.1 = (f32[3,16,2048]{2,1,0:T(8,128)S(1)}, f32[8,512]{1,0:T(8,128)S(1)}) custom-call(s32[2]{0:T(128)S(1)} %pad_add_fusion.edge_ref, f32[32]{0:T(128)S(1)} %copy-done.1, f32[3,8,2048]{2,1,0:T(8,128)S(1)} %copy-done, f32[3,5,2048]{2,1,0:T(8,128)S(1)} %collective-permute-done.low_ref, f32[3,5,2048]{2,1,0:T(8,128)S(1)} %collective-permute-done.1.high_ref, ...), custom_call_target="tpu_custom_call" | custom-call | flops 8000000000 | bytes 2000000 | tf_op jit(solution)/shard_map/paint/pallas_call | solution.py:291
  25.6 0.1 maximum_maximum_fusion
  25.7 1.9 %collective-permute-start.2 = (f32[8,512]{1,0:T(8,128)S(1)}, f32[8,512]{1,0:T(8,128)S(1)}, u32[]{:S(2)}, u32[]{:S(2)}) collective-permute-start(f32[8,512]{1,0:T(8,128)S(1)} %maximum_maximum_fusion), channel_id=1, source_target_pairs={{0,1},{1,0},{2,3},{3,2},{4,5},{5,4},{6,7},{7,6},{8,9},{9,8},{10,11... | collective-permute-start | bytes 49160 | tf_op jit(solution)/shard_map/ppermute | solution.py:245
  27.6 1.1 collective-permute-done.2
  28.8 0.1 add_select_fusion.3
  28.8 1.9 %collective-permute-start.3 = (f32[8,512]{1,0:T(8,128)S(1)}, f32[8,512]{1,0:T(8,128)S(1)}, u32[]{:S(2)}, u32[]{:S(2)}) collective-permute-start(f32[8,512]{1,0:T(8,128)S(1)} %add_select_fusion.3), channel_id=1, source_target_pairs={{0,2},{1,3},{2,0},{3,1},{4,6},{5,7},{6,4},{7,5},{8,10},{9,11},{10,... | collective-permute-start | bytes 49160 | tf_op jit(solution)/shard_map/ppermute | solution.py:245
  30.8 3.7 %collective-permute-done.3 = f32[8,512]{1,0:T(8,128)S(1)} collective-permute-done((f32[8,512]{1,0:T(8,128)S(1)}, f32[8,512]{1,0:T(8,128)S(1)}, u32[]{:S(2)}, u32[]{:S(2)}) %collective-permute-start.3) | collective-permute-done | bytes 16416 | tf_op jit(solution)/shard_map/ppermute | solution.py:245
  34.5 0.1 add_select_fusion.2
  34.5 3.9 %collective-permute-start.4 = (f32[8,512]{1,0:T(8,128)S(1)}, f32[8,512]{1,0:T(8,128)S(1)}, u32[]{:S(2)}, u32[]{:S(2)}) collective-permute-start(f32[8,512]{1,0:T(8,128)S(1)} %add_select_fusion.2), channel_id=1, source_target_pairs={{0,4},{1,5},{2,6},{3,7},{4,0},{5,1},{6,2},{7,3},{8,12},{9,13},{10,... | collective-permute-start | bytes 49160 | tf_op jit(solution)/shard_map/ppermute | solution.py:245
  38.5 3.2 %collective-permute-done.4 = f32[8,512]{1,0:T(8,128)S(1)} collective-permute-done((f32[8,512]{1,0:T(8,128)S(1)}, f32[8,512]{1,0:T(8,128)S(1)}, u32[]{:S(2)}, u32[]{:S(2)}) %collective-permute-start.4) | collective-permute-done | bytes 16416 | tf_op jit(solution)/shard_map/ppermute | solution.py:245
  41.7 0.1 add_select_fusion.1
  41.7 3.8 %collective-permute-start.5 = (f32[8,512]{1,0:T(8,128)S(1)}, f32[8,512]{1,0:T(8,128)S(1)}, u32[]{:S(2)}, u32[]{:S(2)}) collective-permute-start(f32[8,512]{1,0:T(8,128)S(1)} %add_select_fusion.1), channel_id=1, source_target_pairs={{0,8},{1,9},{2,10},{3,11},{4,12},{5,13},{6,14},{7,15},{8,0},{9,1},... | collective-permute-start | bytes 49160 | tf_op jit(solution)/shard_map/ppermute | solution.py:245
  45.6 1.8 %collective-permute-done.5 = f32[8,512]{1,0:T(8,128)S(1)} collective-permute-done((f32[8,512]{1,0:T(8,128)S(1)}, f32[8,512]{1,0:T(8,128)S(1)}, u32[]{:S(2)}, u32[]{:S(2)}) %collective-permute-start.5) | collective-permute-done | bytes 16416 | tf_op jit(solution)/shard_map/ppermute | solution.py:245
  47.3 0.0 copy-start.3
  47.4 0.1 add_select_fusion
  47.4 2.6 %collective-permute-start.6 = (f32[8,512]{1,0:T(8,128)S(1)}, f32[8,512]{1,0:T(8,128)S(1)}, u32[]{:S(2)}, u32[]{:S(2)}) collective-permute-start(f32[8,512]{1,0:T(8,128)S(1)} %add_select_fusion), channel_id=1, source_target_pairs={{0,16},{1,17},{2,18},{3,19},{4,20},{5,21},{6,22},{7,23},{8,24},{9,... | collective-permute-start | bytes 49160 | tf_op jit(solution)/shard_map/ppermute | solution.py:245
  50.1 0.0 copy-done.3
  50.1 0.1 reshape.64.k_ref
  50.2 2.3 %short.1.s_ref = f32[3,16,2048]{2,1,0:T(8,128)S(1)} custom-call(f32[25]{0:T(128)S(1)} %reshape.64.k_ref, f32[3,16,2048]{2,1,0:T(8,128)S(1)} %get-tuple-element.7.c_ref), custom_call_target="tpu_custom_call" | custom-call | flops 10000000 | bytes 1000000 | tf_op jit(solution)/shard_map/short/pallas_call | solution.py:306
  52.4 1.5 %collective-permute-done.6 = f32[8,512]{1,0:T(8,128)S(1)} collective-permute-done((f32[8,512]{1,0:T(8,128)S(1)}, f32[8,512]{1,0:T(8,128)S(1)}, u32[]{:S(2)}, u32[]{:S(2)}) %collective-permute-start.6) | collective-permute-done | bytes 16416 | tf_op jit(solution)/shard_map/ppermute | solution.py:245
  53.9 0.1 multiply_add_fusion.acc_ref
  54.0 2.6 %bend.1.u_ref = f32[144,8,128]{2,1,0:T(8,128)} custom-call(s32[2]{0:T(128)S(1)} %pad_add_fusion.edge_ref, f32[3,16,2048]{2,1,0:T(8,128)S(1)} %short.1.s_ref, f32[8,512]{1,0:T(8,128)S(1)} %get-tuple-element.8.coarse_ref, f32[8,512]{1,0:T(8,128)S(1)} %multiply_add_fusion.acc_ref, f32[512,512]{1,0:T(8,128)S(1)} %multiply_exponential_fusion.ec_ref, ...), custom_call_target="tpu_custom_call" | custom-call | flops 100000000 | bytes 2000000 | tf_op jit(solution)/shard_map/bend/pallas_call | solution.py:316
  56.6 0.0 copy-start.4
  56.6 16.0 %all-to-all-start = ((f32[144,8,128]{2,1,0:T(8,128)}), f32[144,8,128]{2,1,0:T(8,128)S(1)}, u32[]{:S(2)}, u32[]{:S(2)}) async-start(f32[144,8,128]{2,1,0:T(8,128)} %bend.1.u_ref), calls=%async_computation | async-start | bytes 1179648 | tf_op jit(solution)/shard_map/all_to_all | solution.py:326
  72.6 0.0 copy-done.4
  72.7 0.1 fusion.51
  72.7 0.1 multiply_divide_fusion
  72.8 33.2 %all-to-all-done.u_ref = f32[144,8,128]{2,1,0:T(8,128)S(1)} async-done(((f32[144,8,128]{2,1,0:T(8,128)}), f32[144,8,128]{2,1,0:T(8,128)S(1)}, u32[]{:S(2)}, u32[]{:S(2)}) %all-to-all-start) | async-done | bytes 589856 | tf_op jit(solution)/shard_map/all_to_all | solution.py:326
  106.0 1.6 %scan.1 = f32[128,8,128]{2,1,0:T(8,128)} custom-call(f32[48]{0:T(128)S(1)} %get-tuple-element.34.mixing_ref, f32[48]{0:T(128)S(1)} %get-tuple-element.33.bending_ref, f32[144,8,128]{2,1,0:T(8,128)S(1)} %all-to-all-done.u_ref), custom_call_target="tpu_custom_call" | custom-call | flops 10000000 | bytes 1000000 | tf_op jit(solution)/shard_map/scan/pallas_call | solution.py:327
  107.6 3.6 %all-to-all-start.1 = ((f32[128,8,128]{2,1,0:T(8,128)}), f32[128,8,128]{2,1,0:T(8,128)S(1)}, u32[]{:S(2)}, u32[]{:S(2)}) async-start(f32[128,8,128]{2,1,0:T(8,128)} %scan.1), calls=%async_computation.1 | async-start | bytes 1048576 | tf_op jit(solution)/shard_map/all_to_all | solution.py:330
  111.2 0.1 dynamic_slice.7.bending_ref
  111.3 0.1 dynamic_slice.6.mixing_ref
  111.3 33.5 %all-to-all-done.1.state_ref = f32[128,8,128]{2,1,0:T(8,128)S(1)} async-done(((f32[128,8,128]{2,1,0:T(8,128)}), f32[128,8,128]{2,1,0:T(8,128)S(1)}, u32[]{:S(2)}, u32[]{:S(2)}) %all-to-all-start.1) | async-done | bytes 524320 | tf_op jit(solution)/shard_map/all_to_all | solution.py:330
  144.8 2.3 %final.1 = f32[4,3,8,2048]{3,2,1,0:T(8,128)} custom-call(f32[3]{0:T(128)S(1)} %dynamic_slice.6.mixing_ref, f32[3]{0:T(128)S(1)} %dynamic_slice.7.bending_ref, f32[144,8,128]{2,1,0:T(8,128)} %bend.1.u_ref, f32[128,8,128]{2,1,0:T(8,128)S(1)} %all-to-all-done.1.state_ref), custom_call_target="tpu_custom_call" | custom-call | flops 10000000 | bytes 1000000 | tf_op jit(solution)/shard_map/final/pallas_call | solution.py:331
  (24 shorter events, 0.2 us)
Async XLA Ops:
  1.1 12.2 %collective-permute-start = (f32[3,5,2048]{2,1,0:T(8,128)S(1)}, f32[3,5,2048]{2,1,0:T(8,128)S(1)}, u32[]{:S(2)}, u32[]{:S(2)}) collective-permute-start(f32[3,5,2048]{2,1,0:T(8,128)S(1)} %get-tuple-element.10), channel_id=1, source_target_pairs={{0,1},{1,2},{2,3},{3,4},{4,5},{5,6},{6,7},{7,8},{8,9},{9,10},{10,1... | collective-permute-start | bytes 368648 | tf_op jit(solution)/shard_map/ppermute | solution.py:270
  3.0 10.3 %collective-permute-start.1 = (f32[3,5,2048]{2,1,0:T(8,128)S(1)}, f32[3,5,2048]{2,1,0:T(8,128)S(1)}, u32[]{:S(2)}, u32[]{:S(2)}) collective-permute-start(f32[3,5,2048]{2,1,0:T(8,128)S(1)} %get-tuple-element.9), channel_id=1, source_target_pairs={{1,0},{2,1},{3,2},{4,3},{5,4},{6,5},{7,6},{8,7},{9,8},{10,9},{11,1... | collective-permute-start | bytes 368648 | tf_op jit(solution)/shard_map/ppermute | solution.py:271
  9.2 0.7 copy-start.2
  10.4 0.7 copy-start.5
  11.5 1.8 %copy-start = (f32[3,8,2048]{2,1,0:T(8,128)S(1)}, f32[3,8,2048]{2,1,0:T(8,128)}, u32[]{:S(2)}) copy-start(f32[3,8,2048]{2,1,0:T(8,128)} %x_ref.1) | copy-start | bytes 589828
  13.2 0.7 copy-start.1
  25.7 3.1 %collective-permute-start.2 = (f32[8,512]{1,0:T(8,128)S(1)}, f32[8,512]{1,0:T(8,128)S(1)}, u32[]{:S(2)}, u32[]{:S(2)}) collective-permute-start(f32[8,512]{1,0:T(8,128)S(1)} %maximum_maximum_fusion), channel_id=1, source_target_pairs={{0,1},{1,0},{2,3},{3,2},{4,5},{5,4},{6,7},{7,6},{8,9},{9,8},{10,11... | collective-permute-start | bytes 49160 | tf_op jit(solution)/shard_map/ppermute | solution.py:245
  28.8 5.6 %collective-permute-start.3 = (f32[8,512]{1,0:T(8,128)S(1)}, f32[8,512]{1,0:T(8,128)S(1)}, u32[]{:S(2)}, u32[]{:S(2)}) collective-permute-start(f32[8,512]{1,0:T(8,128)S(1)} %add_select_fusion.3), channel_id=1, source_target_pairs={{0,2},{1,3},{2,0},{3,1},{4,6},{5,7},{6,4},{7,5},{8,10},{9,11},{10,... | collective-permute-start | bytes 49160 | tf_op jit(solution)/shard_map/ppermute | solution.py:245
  34.5 7.1 %collective-permute-start.4 = (f32[8,512]{1,0:T(8,128)S(1)}, f32[8,512]{1,0:T(8,128)S(1)}, u32[]{:S(2)}, u32[]{:S(2)}) collective-permute-start(f32[8,512]{1,0:T(8,128)S(1)} %add_select_fusion.2), channel_id=1, source_target_pairs={{0,4},{1,5},{2,6},{3,7},{4,0},{5,1},{6,2},{7,3},{8,12},{9,13},{10,... | collective-permute-start | bytes 49160 | tf_op jit(solution)/shard_map/ppermute | solution.py:245
  41.7 5.6 %collective-permute-start.5 = (f32[8,512]{1,0:T(8,128)S(1)}, f32[8,512]{1,0:T(8,128)S(1)}, u32[]{:S(2)}, u32[]{:S(2)}) collective-permute-start(f32[8,512]{1,0:T(8,128)S(1)} %add_select_fusion.1), channel_id=1, source_target_pairs={{0,8},{1,9},{2,10},{3,11},{4,12},{5,13},{6,14},{7,15},{8,0},{9,1},... | collective-permute-start | bytes 49160 | tf_op jit(solution)/shard_map/ppermute | solution.py:245
  47.3 2.7 %copy-start.3 = (f32[5,5]{1,0:T(8,128)S(1)}, f32[5,5]{1,0:T(8,128)}, u32[]{:S(2)}) copy-start(f32[5,5]{1,0:T(8,128)} %param.11) | copy-start | bytes 304
  47.4 6.5 %collective-permute-start.6 = (f32[8,512]{1,0:T(8,128)S(1)}, f32[8,512]{1,0:T(8,128)S(1)}, u32[]{:S(2)}, u32[]{:S(2)}) collective-permute-start(f32[8,512]{1,0:T(8,128)S(1)} %add_select_fusion), channel_id=1, source_target_pairs={{0,16},{1,17},{2,18},{3,19},{4,20},{5,21},{6,22},{7,23},{8,24},{9,... | collective-permute-start | bytes 49160 | tf_op jit(solution)/shard_map/ppermute | solution.py:245
  56.6 16.0 %copy-start.4 = (s32[48]{0:T(128)S(1)}, s32[48]{0:T(128)}, u32[]{:S(2)}) copy-start(s32[48]{0:T(128)} %param.7) | copy-start | bytes 580
  56.6 49.3 %all-to-all-start = ((f32[144,8,128]{2,1,0:T(8,128)}), f32[144,8,128]{2,1,0:T(8,128)S(1)}, u32[]{:S(2)}, u32[]{:S(2)}) async-start(f32[144,8,128]{2,1,0:T(8,128)} %bend.1.u_ref), calls=%async_computation | async-start | bytes 1179648 | tf_op jit(solution)/shard_map/all_to_all | solution.py:326
  107.6 37.2 %all-to-all-start.1 = ((f32[128,8,128]{2,1,0:T(8,128)}), f32[128,8,128]{2,1,0:T(8,128)S(1)}, u32[]{:S(2)}, u32[]{:S(2)}) async-start(f32[128,8,128]{2,1,0:T(8,128)} %scan.1), calls=%async_computation.1 | async-start | bytes 1048576 | tf_op jit(solution)/shard_map/all_to_all | solution.py:330

commit v2 on v1

--- a/solution.py
+++ b/solution.py
@@ -297,6 +297,9 @@
         [pltpu.VMEM((2, 16, col_count), f32), pltpu.VMEM((160, col_count), bf16), pltpu.VMEM((8, col_count), f32)],
         (8 * 10**9, 2 * 10**6, 10**6),
     )(edge, mix_weight, density, low, high, weights, pool)
+    coarse, convergence, mixing, bending, mixing_here, bending_here = lax.optimization_barrier(
+        (coarse, convergence, mixing, bending, mixing_here, bending_here)
+    )
 
     e = decay
     c0, c1 = coarse[0:3], coarse[3:6]

time: 148 us -> 147 us (level)
  the two profiles are of different devices: /device:TPU:64 before, /device:TPU:57 now
where the time goes in v2:
time: 147 us; the launch traced here: 146 us
  blocking collectives  91.2 us (62%)
  starting transfers between devices  18.6 us (13%)
  Pallas kernels  18.4 us (13%)
  waiting for transfers between devices  10.3 us (7%)
  local copies, waits for them, and re-layouts  4.78 us (3%)
  other arithmetic  2.35 us (2%)
    all_to_all x1, blocking collectives, body(): gathered = lax.all_to_all(shear, 'plane', 0, 0, tiled=True)  51.5 us
    all_to_all x1, blocking collectives, body(): mine = lax.all_to_all(states, 'plane', 0, 0, tiled=True)  39.7 us
    pallas_call x1, Pallas kernels, body(): call(paint_kernel, 'paint', 2, 5, (sds(3, 16, col_count), sds(8, coarse_c...  11.7 us
    ppermute x5, starting transfers between devices, row_scan(): lax.ppermute(block, 'tile', [(i, i ^ size) for i in range(tile_count)])  10.9 us
    ppermute x5, waiting for transfers between devices, row_scan(): lax.ppermute(block, 'tile', [(i, i ^ size) for i in range(tile_count)])  10.3 us
    ppermute x1, starting transfers between devices, body(): low = lax.ppermute(density[:, 3:8, :], 'tile', up)  5.09 us
  transfers between devices with their start and end apart: 7, of which 4 were waited for; matrix products, arithmetic and copies ran while one was open for 2% of the time, Pallas kernels for 2%

profile of v2, /device:TPU:57, one launch (start us, length us, event | category | flops | bytes accessed | tf_op | source)
XLA Modules:
  0.0 146.3 jit_solution(16439161331498046863)
XLA Ops:
  0.0 1.0 fusion.47
  1.1 2.6 %collective-permute-start.1 = (f32[3,5,2048]{2,1,0:T(8,128)S(1)}, f32[3,5,2048]{2,1,0:T(8,128)S(1)}, u32[]{:S(2)}, u32[]{:S(2)}) collective-permute-start(f32[3,5,2048]{2,1,0:T(8,128)S(1)} %get-tuple-element.21), channel_id=1, source_target_pairs={{1,0},{2,1},{3,2},{4,3},{5,4},{6,5},{7,6},{8,7},{9,8},{10,9},{11,1... | collective-permute-start | bytes 368648 | tf_op jit(solution)/shard_map/ppermute | solution.py:271
  3.6 5.1 %collective-permute-start = (f32[3,5,2048]{2,1,0:T(8,128)S(1)}, f32[3,5,2048]{2,1,0:T(8,128)S(1)}, u32[]{:S(2)}, u32[]{:S(2)}) collective-permute-start(f32[3,5,2048]{2,1,0:T(8,128)S(1)} %get-tuple-element.22), channel_id=1, source_target_pairs={{0,1},{1,2},{2,3},{3,4},{4,5},{5,6},{6,7},{7,8},{8,9},{9,10},{10,1... | collective-permute-start | bytes 368648 | tf_op jit(solution)/shard_map/ppermute | solution.py:270
  8.9 0.3 fusion.39.pool_ref
  9.2 0.2 multiply_exponential_fusion.ec_ref
  9.6 0.0 copy-start.4
  9.6 0.6 copy-done.4
  10.3 0.0 copy-start.5
  10.3 0.1 fusion.51
  10.3 0.6 copy-done.5
  10.9 0.1 broadcast_in_dim.257
  11.0 0.1 broadcast_in_dim.258
  11.1 0.1 broadcast_in_dim.260
  11.2 0.1 broadcast_in_dim.261
  11.3 0.0 copy-start.2
  11.3 0.1 broadcast_in_dim.263
  11.4 0.1 broadcast_in_dim.264
  11.5 0.5 copy-done.2
  12.0 0.1 broadcast_in_dim.266
  12.1 0.1 reshape.64
  12.2 0.1 broadcast_in_dim.269
  12.3 0.1 reshape.65
  12.5 0.0 copy-start
  12.5 0.1 multiply_divide_fusion
  12.6 1.1 fusion.26.w_ref
  13.7 0.1 pad_add_fusion.edge_ref
  14.0 0.1 dynamic_slice.7.bending_ref
  14.0 0.1 dynamic_slice.6.mixing_ref
  14.1 0.1 pad.2.clone
  14.2 0.0 copy-start.1
  14.2 0.0 collective-permute-done.1.high_ref
  14.2 0.0 collective-permute-done.low_ref
  14.2 0.0 copy-done
  14.2 0.6 copy-done.1
  14.9 11.7 %paint.1 = (f32[3,16,2048]{2,1,0:T(8,128)S(1)}, f32[8,512]{1,0:T(8,128)S(1)}) custom-call(s32[2]{0:T(128)S(1)} %pad_add_fusion.edge_ref, f32[32]{0:T(128)S(1)} %copy-done.1, f32[3,8,2048]{2,1,0:T(8,128)S(1)} %copy-done, f32[3,5,2048]{2,1,0:T(8,128)S(1)} %collective-permute-done.low_ref, f32[3,5,2048]{2,1,0:T(8,128)S(1)} %collective-permute-done.1.high_ref, ...), custom_call_target="tpu_custom_call" | custom-call | flops 8000000000 | bytes 2000000 | tf_op jit(solution)/shard_map/paint/pallas_call | solution.py:291
  26.6 0.1 maximum_maximum_fusion
  26.7 1.9 %collective-permute-start.2 = (f32[8,512]{1,0:T(8,128)S(1)}, f32[8,512]{1,0:T(8,128)S(1)}, u32[]{:S(2)}, u32[]{:S(2)}) collective-permute-start(f32[8,512]{1,0:T(8,128)S(1)} %maximum_maximum_fusion), channel_id=1, source_target_pairs={{0,1},{1,0},{2,3},{3,2},{4,5},{5,4},{6,7},{7,6},{8,9},{9,8},{10,11... | collective-permute-start | bytes 49160 | tf_op jit(solution)/shard_map/ppermute | solution.py:245
  28.6 1.1 collective-permute-done.2
  29.7 0.1 add_select_fusion.3
  29.8 1.9 %collective-permute-start.3 = (f32[8,512]{1,0:T(8,128)S(1)}, f32[8,512]{1,0:T(8,128)S(1)}, u32[]{:S(2)}, u32[]{:S(2)}) collective-permute-start(f32[8,512]{1,0:T(8,128)S(1)} %add_select_fusion.3), channel_id=1, source_target_pairs={{0,2},{1,3},{2,0},{3,1},{4,6},{5,7},{6,4},{7,5},{8,10},{9,11},{10,... | collective-permute-start | bytes 49160 | tf_op jit(solution)/shard_map/ppermute | solution.py:245
  31.7 2.5 %collective-permute-done.3 = f32[8,512]{1,0:T(8,128)S(1)} collective-permute-done((f32[8,512]{1,0:T(8,128)S(1)}, f32[8,512]{1,0:T(8,128)S(1)}, u32[]{:S(2)}, u32[]{:S(2)}) %collective-permute-start.3) | collective-permute-done | bytes 16416 | tf_op jit(solution)/shard_map/ppermute | solution.py:245
  34.3 0.1 add_select_fusion.2
  34.4 1.9 %collective-permute-start.4 = (f32[8,512]{1,0:T(8,128)S(1)}, f32[8,512]{1,0:T(8,128)S(1)}, u32[]{:S(2)}, u32[]{:S(2)}) collective-permute-start(f32[8,512]{1,0:T(8,128)S(1)} %add_select_fusion.2), channel_id=1, source_target_pairs={{0,4},{1,5},{2,6},{3,7},{4,0},{5,1},{6,2},{7,3},{8,12},{9,13},{10,... | collective-permute-start | bytes 49160 | tf_op jit(solution)/shard_map/ppermute | solution.py:245
  36.3 4.0 %collective-permute-done.4 = f32[8,512]{1,0:T(8,128)S(1)} collective-permute-done((f32[8,512]{1,0:T(8,128)S(1)}, f32[8,512]{1,0:T(8,128)S(1)}, u32[]{:S(2)}, u32[]{:S(2)}) %collective-permute-start.4) | collective-permute-done | bytes 16416 | tf_op jit(solution)/shard_map/ppermute | solution.py:245
  40.3 0.1 add_select_fusion.1
  40.4 1.9 %collective-permute-start.5 = (f32[8,512]{1,0:T(8,128)S(1)}, f32[8,512]{1,0:T(8,128)S(1)}, u32[]{:S(2)}, u32[]{:S(2)}) collective-permute-start(f32[8,512]{1,0:T(8,128)S(1)} %add_select_fusion.1), channel_id=1, source_target_pairs={{0,8},{1,9},{2,10},{3,11},{4,12},{5,13},{6,14},{7,15},{8,0},{9,1},... | collective-permute-start | bytes 49160 | tf_op jit(solution)/shard_map/ppermute | solution.py:245
  42.3 2.5 %collective-permute-done.5 = f32[8,512]{1,0:T(8,128)S(1)} collective-permute-done((f32[8,512]{1,0:T(8,128)S(1)}, f32[8,512]{1,0:T(8,128)S(1)}, u32[]{:S(2)}, u32[]{:S(2)}) %collective-permute-start.5) | collective-permute-done | bytes 16416 | tf_op jit(solution)/shard_map/ppermute | solution.py:245
  44.9 0.0 copy-start.3
  44.9 0.1 add_select_fusion
  45.0 3.3 %collective-permute-start.6 = (f32[8,512]{1,0:T(8,128)S(1)}, f32[8,512]{1,0:T(8,128)S(1)}, u32[]{:S(2)}, u32[]{:S(2)}) collective-permute-start(f32[8,512]{1,0:T(8,128)S(1)} %add_select_fusion), channel_id=1, source_target_pairs={{0,16},{1,17},{2,18},{3,19},{4,20},{5,21},{6,22},{7,23},{8,24},{9,... | collective-permute-start | bytes 49160 | tf_op jit(solution)/shard_map/ppermute | solution.py:245
  48.2 0.0 copy-done.3
  48.3 0.1 reshape.66.k_ref
  48.3 2.3 %short.1.s_ref = f32[3,16,2048]{2,1,0:T(8,128)S(1)} custom-call(f32[25]{0:T(128)S(1)} %reshape.66.k_ref, f32[3,16,2048]{2,1,0:T(8,128)S(1)} %get-tuple-element.17.c_ref), custom_call_target="tpu_custom_call" | custom-call | flops 10000000 | bytes 1000000 | tf_op jit(solution)/shard_map/short/pallas_call | solution.py:309
  50.6 0.0 collective-permute-done.6
  50.6 0.1 multiply_add_fusion.acc_ref
  50.7 1.8 %bend.1.u_ref = f32[144,8,128]{2,1,0:T(8,128)S(1)} custom-call(s32[2]{0:T(128)S(1)} %pad_add_fusion.edge_ref, f32[3,16,2048]{2,1,0:T(8,128)S(1)} %short.1.s_ref, f32[8,512]{1,0:T(8,128)S(1)} %get-tuple-element.18.coarse_ref, f32[8,512]{1,0:T(8,128)S(1)} %multiply_add_fusion.acc_ref, f32[512,512]{1,0:T(8,128)S(1)} %multiply_exponential_fusion.ec_ref, ...), custom_call_target="tpu_custom_call" | custom-call | flops 100000000 | bytes 2000000 | tf_op jit(solution)/shard_map/bend/pallas_call | solution.py:319
  52.5 51.5 %all_to_all.10.u_ref = f32[144,8,128]{2,1,0:T(8,128)S(1)} all-to-all(f32[144,8,128]{2,1,0:T(8,128)S(1)} %bend.1.u_ref), channel_id=1, replica_groups=mesh['plane'=16,'tile'=32] {'plane'}, dimensions={0} | all-to-all | bytes 1179648 | tf_op jit(solution)/shard_map/all_to_all | solution.py:329
  104.0 0.8 scan.1
  104.9 39.7 %all_to_all.11.state_ref = f32[128,8,128]{2,1,0:T(8,128)S(1)} all-to-all(f32[128,8,128]{2,1,0:T(8,128)S(1)} %scan.1), channel_id=1, replica_groups=mesh['plane'=16,'tile'=32] {'plane'}, dimensions={0} | all-to-all | bytes 1048576 | tf_op jit(solution)/shard_map/all_to_all | solution.py:333
  144.5 1.8 %final.1 = f32[4,3,8,2048]{3,2,1,0:T(8,128)} custom-call(f32[3]{0:T(128)S(1)} %dynamic_slice.6.mixing_ref, f32[3]{0:T(128)S(1)} %dynamic_slice.7.bending_ref, f32[144,8,128]{2,1,0:T(8,128)S(1)} %bend.1.u_ref, f32[128,8,128]{2,1,0:T(8,128)S(1)} %all_to_all.11.state_ref), custom_call_target="tpu_custom_call" | custom-call | flops 10000000 | bytes 1000000 | tf_op jit(solution)/shard_map/final/pallas_call | solution.py:334
  (24 shorter events, 0.2 us)
Async XLA Ops:
  1.1 13.2 %collective-permute-start.1 = (f32[3,5,2048]{2,1,0:T(8,128)S(1)}, f32[3,5,2048]{2,1,0:T(8,128)S(1)}, u32[]{:S(2)}, u32[]{:S(2)}) collective-permute-start(f32[3,5,2048]{2,1,0:T(8,128)S(1)} %get-tuple-element.21), channel_id=1, source_target_pairs={{1,0},{2,1},{3,2},{4,3},{5,4},{6,5},{7,6},{8,7},{9,8},{10,9},{11,1... | collective-permute-start | bytes 368648 | tf_op jit(solution)/shard_map/ppermute | solution.py:271
  3.6 10.6 %collective-permute-start = (f32[3,5,2048]{2,1,0:T(8,128)S(1)}, f32[3,5,2048]{2,1,0:T(8,128)S(1)}, u32[]{:S(2)}, u32[]{:S(2)}) collective-permute-start(f32[3,5,2048]{2,1,0:T(8,128)S(1)} %get-tuple-element.22), channel_id=1, source_target_pairs={{0,1},{1,2},{2,3},{3,4},{4,5},{5,6},{6,7},{7,8},{8,9},{9,10},{10,1... | collective-permute-start | bytes 368648 | tf_op jit(solution)/shard_map/ppermute | solution.py:270
  9.6 0.7 copy-start.4
  10.3 0.7 copy-start.5
  11.3 0.7 copy-start.2
  12.5 1.7 %copy-start = (f32[3,8,2048]{2,1,0:T(8,128)S(1)}, f32[3,8,2048]{2,1,0:T(8,128)}, u32[]{:S(2)}) copy-start(f32[3,8,2048]{2,1,0:T(8,128)} %x_ref.1) | copy-start | bytes 589828
  14.2 0.7 copy-start.1
  26.7 3.1 %collective-permute-start.2 = (f32[8,512]{1,0:T(8,128)S(1)}, f32[8,512]{1,0:T(8,128)S(1)}, u32[]{:S(2)}, u32[]{:S(2)}) collective-permute-start(f32[8,512]{1,0:T(8,128)S(1)} %maximum_maximum_fusion), channel_id=1, source_target_pairs={{0,1},{1,0},{2,3},{3,2},{4,5},{5,4},{6,7},{7,6},{8,9},{9,8},{10,11... | collective-permute-start | bytes 49160 | tf_op jit(solution)/shard_map/ppermute | solution.py:245
  29.8 4.5 %collective-permute-start.3 = (f32[8,512]{1,0:T(8,128)S(1)}, f32[8,512]{1,0:T(8,128)S(1)}, u32[]{:S(2)}, u32[]{:S(2)}) collective-permute-start(f32[8,512]{1,0:T(8,128)S(1)} %add_select_fusion.3), channel_id=1, source_target_pairs={{0,2},{1,3},{2,0},{3,1},{4,6},{5,7},{6,4},{7,5},{8,10},{9,11},{10,... | collective-permute-start | bytes 49160 | tf_op jit(solution)/shard_map/ppermute | solution.py:245
  34.4 6.0 %collective-permute-start.4 = (f32[8,512]{1,0:T(8,128)S(1)}, f32[8,512]{1,0:T(8,128)S(1)}, u32[]{:S(2)}, u32[]{:S(2)}) collective-permute-start(f32[8,512]{1,0:T(8,128)S(1)} %add_select_fusion.2), channel_id=1, source_target_pairs={{0,4},{1,5},{2,6},{3,7},{4,0},{5,1},{6,2},{7,3},{8,12},{9,13},{10,... | collective-permute-start | bytes 49160 | tf_op jit(solution)/shard_map/ppermute | solution.py:245
  40.4 4.5 %collective-permute-start.5 = (f32[8,512]{1,0:T(8,128)S(1)}, f32[8,512]{1,0:T(8,128)S(1)}, u32[]{:S(2)}, u32[]{:S(2)}) collective-permute-start(f32[8,512]{1,0:T(8,128)S(1)} %add_select_fusion.1), channel_id=1, source_target_pairs={{0,8},{1,9},{2,10},{3,11},{4,12},{5,13},{6,14},{7,15},{8,0},{9,1},... | collective-permute-start | bytes 49160 | tf_op jit(solution)/shard_map/ppermute | solution.py:245
  44.9 3.4 %copy-start.3 = (f32[5,5]{1,0:T(8,128)S(1)}, f32[5,5]{1,0:T(8,128)}, u32[]{:S(2)}) copy-start(f32[5,5]{1,0:T(8,128)} %param.11) | copy-start | bytes 304
  45.0 5.7 %collective-permute-start.6 = (f32[8,512]{1,0:T(8,128)S(1)}, f32[8,512]{1,0:T(8,128)S(1)}, u32[]{:S(2)}, u32[]{:S(2)}) collective-permute-start(f32[8,512]{1,0:T(8,128)S(1)} %add_select_fusion), channel_id=1, source_target_pairs={{0,16},{1,17},{2,18},{3,19},{4,20},{5,21},{6,22},{7,23},{8,24},{9,... | collective-permute-start | bytes 49160 | tf_op jit(solution)/shard_map/ppermute | solution.py:245

commit v3 on v2

--- a/solution.py
+++ b/solution.py
@@ -6,6 +6,7 @@
 from jax import lax
 from jax.experimental import pallas as pl
 from jax.experimental.pallas import tpu as pltpu
+from jax.sharding import Mesh
 from jax.sharding import PartitionSpec as P
 
 f32 = jnp.float32
@@ -93,7 +94,7 @@
                     c_ref[p, 8:14, at] = total[2:8]
                 return carry
 
-            lax.fori_loop(0, cols // 256, one_chunk, 0)
+            lax.fori_loop(0, cols // 256, one_chunk, 0, unroll=True)
         value = c_ref[p, 3:11, :]
         sums[p : p + 1, :] = jnp.sum(value[0:4], axis=0, keepdims=True)
         sums[3 + p : 4 + p, :] = jnp.sum(value[4:8], axis=0, keepdims=True)
@@ -121,7 +122,7 @@
             s_ref[p, 8 * window : 8 * window + 8, :] = total
 
 
-def bend_kernel(decay, gain, edge_ref, s_ref, coarse_ref, acc_ref, ec_ref, grow_ref, u_ref, rows, pot):
+def bend_kernel(decay, gain, edge_ref, s_ref, coarse_ref, acc_ref, ec_ref, grow_ref, sent_ref, u_ref, rows, pot, rim):
     cols = s_ref.shape[-1]
     e = decay
     c0, c1 = coarse_ref[0:3, :], coarse_ref[3:6, :]
@@ -136,8 +137,11 @@
     grown = jnp.dot(stacked, grow_ref[...], precision=highest, preferred_element_type=f32)
     long = jnp.concatenate([grown[16 * v : 16 * v + 16] for v in range(4)], axis=1)
     row = lax.broadcasted_iota(jnp.int32, (8, cols), 0)
+    lane = lax.broadcasted_iota(jnp.int32, (8, cols), 1) % 128
     top = edge_ref[0] != 0
     bottom = edge_ref[1] != 0
+    rim[...] = jnp.zeros_like(rim)
+    side = jnp.zeros((8, cols), f32)
     for p in range(3):
         part = s_ref[p]
         wide = jnp.where(
@@ -146,19 +150,33 @@
             jnp.broadcast_to(long[6 + p : 7 + p], (8, cols)),
         )
         here = part[1:9] + wide
-        pot[7:8, :] = jnp.where(top, part[0:1] + long[p : p + 1], 0.0)
+        above_row = jnp.where(top, part[0:1] + long[p : p + 1], 0.0)
+        below_row = jnp.where(bottom, part[9:10] + long[9 + p : 10 + p], 0.0)
+        pot[7:8, :] = above_row
         pot[8:16, :] = here
-        pot[16:17, :] = jnp.where(bottom, part[9:10] + long[9 + p : 10 + p], 0.0)
+        pot[16:17, :] = below_row
+        rim[p : p + 1, :] = above_row
+        rim[3 + p : 4 + p, :] = below_row
         above, below = pot[7:15, :], pot[9:17, :]
         u11 = below - 2.0 * here + above
         u22 = shifted(here, 1) - 2.0 * here + shifted(here, -1)
         step = below - above
         u12 = (shifted(step, 1) - shifted(step, -1)) * 0.25
+        side = jnp.where(lane == 2 * p, shifted(here, -1 - 2 * p), side)
+        side = jnp.where(lane == 2 * p + 1, shifted(here, 127 - 2 * p), side)
         for d in range(cols // 128):
             at = slice(128 * d, 128 * d + 128)
+            sent_ref[5 * d + p] = here[:, at]
             u_ref[9 * d + 3 * p] = u11[:, at]
             u_ref[9 * d + 3 * p + 1] = u12[:, at]
             u_ref[9 * d + 3 * p + 2] = u22[:, at]
+    rim_rows = rim[...]
+    side = jnp.where(lane == 6, shifted(rim_rows, -7), side)
+    side = jnp.where(lane == 7, shifted(rim_rows, 121), side)
+    for d in range(cols // 128):
+        at = slice(128 * d, 128 * d + 128)
+        sent_ref[5 * d + 3] = rim_rows[:, at]
+        sent_ref[5 * d + 4] = side[:, at]
 
 
 def advance(previous, current, u11, u12, u22, mixing, bending):
@@ -172,25 +190,49 @@
     return tuple(kept * previous[i] + mixing * current[i] - bending * bent[i] for i in range(4))
 
 
-def scan_kernel(mixing_ref, bending_ref, u_ref, state_ref):
+def beside(value, left, right):
+    lane = lax.broadcasted_iota(jnp.int32, value.shape, 1)
+    before = jnp.where(lane == 0, jnp.broadcast_to(left, value.shape), pltpu.roll(value, 1, 1))
+    after = jnp.where(lane == 127, jnp.broadcast_to(right, value.shape), pltpu.roll(value, 127, 1))
+    return before, after
+
+
+def over_rows(value, above, below):
+    row = lax.broadcasted_iota(jnp.int32, value.shape, 0)
+    before = jnp.where(row == 0, jnp.broadcast_to(above, value.shape), pltpu.roll(value, 1, 0))
+    after = jnp.where(row == 7, jnp.broadcast_to(below, value.shape), pltpu.roll(value, 7, 0))
+    return before, after
+
+
+def scan_kernel(mixing_ref, bending_ref, sent_ref, state_ref):
     one = jnp.ones((8, 128), f32)
     zero = jnp.zeros((8, 128), f32)
-    groups = u_ref.shape[0] // 9
+    groups = sent_ref.shape[0] // 5
 
     def one_group(g, carry):
         previous, current = carry
         for i in range(4):
             state_ref[8 * g + i] = previous[i]
             state_ref[8 * g + 4 + i] = current[i]
+        rim = sent_ref[5 * g + 3]
+        side = sent_ref[5 * g + 4]
+        rim_left, rim_right = beside(rim, side[:, 6:7], side[:, 7:8])
+        rim_step = rim_right - rim_left
         for p in range(3):
-            at = 9 * g + 3 * p
             k = 3 * g + p
-            later = advance(previous, current, u_ref[at], u_ref[at + 1], u_ref[at + 2], mixing_ref[k], bending_ref[k])
+            here = sent_ref[5 * g + p]
+            above, below = over_rows(here, rim[p : p + 1], rim[3 + p : 4 + p])
+            left, right = beside(here, side[:, 2 * p : 2 * p + 1], side[:, 2 * p + 1 : 2 * p + 2])
+            u11 = below - 2.0 * here + above
+            u22 = right - 2.0 * here + left
+            step_above, step_below = over_rows(right - left, rim_step[p : p + 1], rim_step[3 + p : 4 + p])
+            u12 = (step_below - step_above) * 0.25
+            later = advance(previous, current, u11, u12, u22, mixing_ref[k], bending_ref[k])
             previous, current = current, later
         return (previous, current)
 
     start = (one, zero, zero, one)
-    lax.fori_loop(0, groups, one_group, (start, start))
+    lax.fori_loop(0, groups, one_group, (start, start), unroll=True)
 
 
 def final_kernel(mixing_ref, bending_ref, u_ref, state_ref, out_ref):
@@ -235,30 +277,37 @@
     )
 
 
-def row_scan(message, tile_index, tile_count):
-    row = lax.broadcasted_iota(jnp.int32, (8, 1), 0)
-    forward = row < 3
-    block = message
-    total = jnp.zeros_like(message)
-    size = 1
-    while size < tile_count:
-        received = lax.ppermute(block, "tile", [(i, i ^ size) for i in range(tile_count)])
-        from_lower = (tile_index & size) != 0
-        place = (tile_index % size).astype(f32)
-        weight = jnp.where(forward, jnp.exp(-place / 8.0), jnp.exp(-(size - 1 - place) / 8.0))
-        used = forward == from_lower
-        total = total + jnp.where(used, weight, 0.0) * received
-        far = math.exp(-size / 8.0)
-        block = jnp.where(used, block + far * received, far * block + received)
-        size *= 2
-    return total
+def row_scan(message, near_index, far_index):
+    rows, cols = message.shape
+    near, far = lax.axis_size("near"), lax.axis_size("far")
+    forward = lax.broadcasted_iota(jnp.int32, (1, rows, 1), 1) < 3
+    decayed = lambda tiles: jnp.exp(tiles.astype(f32) / -8.0)
+
+    def everyone(value, axis, count):
+        copies = jnp.broadcast_to(value[None], (count, rows, cols))
+        return lax.all_to_all(copies, axis, 0, 0, tiled=True)
+
+    q = lax.broadcasted_iota(jnp.int32, (near, 1, 1), 0)
+    gap = jnp.where(forward, near_index - q, q - near_index) - 1
+    to_edge = jnp.where(forward, near - 1 - q, q)
+    received = everyone(message, "near", near)
+    total = jnp.sum(jnp.where(gap >= 0, decayed(jnp.maximum(gap, 0)), 0.0) * received, axis=0)
+    run = jnp.sum(decayed(to_edge) * received, axis=0)
+
+    w = lax.broadcasted_iota(jnp.int32, (far, 1, 1), 0)
+    runs = jnp.where(forward, far_index - w, w - far_index) - 1
+    inside = jnp.where(forward, near_index, near - 1 - near_index)
+    weight = jnp.where(runs >= 0, decayed(jnp.maximum(runs, 0) * near + inside), 0.0)
+    return total + jnp.sum(weight * everyone(run, "far", far), axis=0)
 
 
 def body(density, plane_slot, paint_weight, paint_bias, mix_weight, short_kernel):
     plane_count, row_count, col_count = density.shape
-    tile_count = lax.axis_size("tile")
+    tile = ("far", "near")
+    near_index, far_index = lax.axis_index("near"), lax.axis_index("far")
+    tile_count = lax.axis_size("far") * lax.axis_size("near")
     group_count = lax.axis_size("plane")
-    tile_index = lax.axis_index("tile")
+    tile_index = far_index * lax.axis_size("near") + near_index
     plane_index = lax.axis_index("plane")
     coarse_cols = col_count // 4
     row_scale = row_count * tile_count / 16.0
@@ -267,8 +316,8 @@
     decay = math.exp(-1.0 / row_scale)
 
     up = [(i, i + 1) for i in range(tile_count - 1)]
-    low = lax.ppermute(density[:, 3:8, :], "tile", up)
-    high = lax.ppermute(density[:, 0:5, :], "tile", [(b, a) for a, b in up])
+    low = lax.ppermute(density[:, 3:8, :], tile, up)
+    high = lax.ppermute(density[:, 0:5, :], tile, [(b, a) for a, b in up])
 
     edge = jnp.stack([tile_index, tile_count - 1 - tile_index]).astype(jnp.int32)
     mixing, bending = distances(plane_slot, 2 * plane_slot.shape[0])
@@ -304,7 +353,7 @@
     e = decay
     c0, c1 = coarse[0:3], coarse[3:6]
     message = jnp.concatenate([e * e * c0 + e * c1, e * c0 + e * e * c1, jnp.zeros_like(coarse[0:2])], axis=0)
-    received = row_scan(message, tile_index, tile_count)
+    received = row_scan(message, near_index, far_index)
 
     short_part = call(
         short_kernel_body,
@@ -316,17 +365,17 @@
         (10**7, 10**6, 0),
     )(short_kernel.reshape(25), convergence)
 
-    shear = call(
+    sent, shear = call(
         functools.partial(bend_kernel, decay, long_gain),
         "bend",
         1,
         5,
-        sds(group_count * 9, 8, 128),
-        [pltpu.VMEM((16, coarse_cols), f32), pltpu.VMEM((24, col_count), f32)],
+        (sds(group_count * 5, 8, 128), sds(group_count * 9, 8, 128)),
+        [pltpu.VMEM((16, coarse_cols), f32), pltpu.VMEM((24, col_count), f32), pltpu.VMEM((8, col_count), f32)],
         (10**8, 2 * 10**6, 0),
     )(edge, short_part, coarse, received, col_kernel, grow)
 
-    gathered = lax.all_to_all(shear, "plane", 0, 0, tiled=True)
+    gathered = lax.all_to_all(sent, "plane", 0, 0, tiled=True)
     states = call(scan_kernel, "scan", 2, 1, sds(group_count * 8, 8, 128), (), (10**7, 10**6, 0))(
         mixing, bending, gathered
     )
@@ -337,7 +386,10 @@
 
 
 def solution(mesh):
-    placed = (P("plane", "tile", None), P(), P(), P(), P(), P())
+    planes, tiles = mesh.devices.shape
+    split = Mesh(mesh.devices.reshape(planes, 4, tiles // 4), ("plane", "far", "near"))
+    tile = ("far", "near")
+    placed = (P("plane", tile, None), P(), P(), P(), P(), P())
     return jax.shard_map(
-        body, mesh=mesh, in_specs=placed, out_specs=P(None, "plane", "tile", None), check_vma=False
-    )
+        body, mesh=split, in_specs=placed, out_specs=P(None, "plane", tile, None), check_vma=False
+    )

time: 147 us -> 120 us (0.82)
  the two profiles are of different devices: /device:TPU:57 before, /device:TPU:64 now
where the time goes in v3:
time: 120 us; the launch traced here: 119 us
  blocking collectives  77.6 us (65%)
  starting transfers between devices  14.7 us (12%)
  Pallas kernels  9.97 us (8%)
  waiting for transfers between devices  9.15 us (8%)
  local copies, waits for them, and re-layouts  5.54 us (5%)
  other arithmetic  2.27 us (2%)
    all_to_all x1, blocking collectives, body(): gathered = lax.all_to_all(sent, 'plane', 0, 0, tiled=True)  41 us
    all_to_all x1, blocking collectives, body(): mine = lax.all_to_all(states, 'plane', 0, 0, tiled=True)  36.5 us
    all_to_all x2, starting transfers between devices, everyone(): return lax.all_to_all(copies, axis, 0, 0, tiled=True)  8.85 us
    all_to_all x2, waiting for transfers between devices, everyone(): return lax.all_to_all(copies, axis, 0, 0, tiled=True)  7.23 us
    ppermute x1, starting transfers between devices, body(): high = lax.ppermute(density[:, 0:5, :], tile, [(b, a) for a, b in up])  3.91 us
    pallas_call x1, Pallas kernels, body(): call(paint_kernel, 'paint', 2, 5, (sds(3, 16, col_count), sds(8, coarse_c...  3.13 us
  transfers between devices with their start and end apart: 4, of which 3 were waited for; matrix products, arithmetic and copies ran while one was open for 3% of the time, Pallas kernels for 2%

profile of v3, /device:TPU:64, one launch (start us, length us, event | category | flops | bytes accessed | tf_op | source)
XLA Modules:
  0.0 119.4 jit_solution(11916331794305799211)
XLA Ops:
  0.0 1.0 fusion.49
  1.1 3.9 %collective-permute-start.1 = (f32[3,5,2048]{2,1,0:T(8,128)S(1)}, f32[3,5,2048]{2,1,0:T(8,128)S(1)}, u32[]{:S(2)}, u32[]{:S(2)}) collective-permute-start(f32[3,5,2048]{2,1,0:T(8,128)S(1)} %get-tuple-element.27), channel_id=1, source_target_pairs={{1,0},{2,1},{3,2},{4,3},{5,4},{6,5},{7,6},{8,7},{9,8},{10,9},{11,1... | collective-permute-start | bytes 368648 | tf_op jit(solution)/shard_map/ppermute | solution.py:320
  5.0 1.9 %collective-permute-start = (f32[3,5,2048]{2,1,0:T(8,128)S(1)}, f32[3,5,2048]{2,1,0:T(8,128)S(1)}, u32[]{:S(2)}, u32[]{:S(2)}) collective-permute-start(f32[3,5,2048]{2,1,0:T(8,128)S(1)} %get-tuple-element.28), channel_id=1, source_target_pairs={{0,1},{1,2},{2,3},{3,4},{4,5},{5,6},{6,7},{7,8},{8,9},{9,10},{10,1... | collective-permute-start | bytes 368648 | tf_op jit(solution)/shard_map/ppermute | solution.py:319
  7.0 0.3 fusion.39.pool_ref
  7.3 0.0 copy-start.4
  7.4 0.6 copy-done.4
  8.0 0.1 fusion.53
  8.1 0.0 copy-start.5
  8.1 0.6 copy-done.5
  8.7 0.1 broadcast_in_dim.285
  8.8 0.1 broadcast_in_dim.286
  8.9 0.1 broadcast_in_dim.288
  9.0 0.1 broadcast_in_dim.289
  9.1 0.0 copy-start.2
  9.1 0.1 broadcast_in_dim.291
  9.2 0.1 broadcast_in_dim.292
  9.3 0.5 copy-done.2
  9.8 0.1 broadcast_in_dim.294
  9.9 0.1 reshape.241
  10.1 0.1 broadcast_in_dim.297
  10.2 0.1 reshape.242
  10.3 0.1 multiply_divide_fusion
  10.4 0.1 exponential_select_fusion
  10.5 1.1 fusion.26.w_ref
  11.6 0.0 copy-start
  11.6 0.2 multiply_exponential_fusion.ec_ref
  11.8 0.1 dynamic_slice.7.bending_ref
  11.9 0.1 dynamic_slice.6.mixing_ref
  12.0 0.1 pad.2.clone
  12.1 0.0 copy-start.1
  12.1 0.1 pad_add_fusion.edge_ref
  12.1 0.0 collective-permute-done.1.high_ref
  12.1 1.9 %collective-permute-done.low_ref = f32[3,5,2048]{2,1,0:T(8,128)S(1)} collective-permute-done((f32[3,5,2048]{2,1,0:T(8,128)S(1)}, f32[3,5,2048]{2,1,0:T(8,128)S(1)}, u32[]{:S(2)}, u32[]{:S(2)}) %collective-permute-start) | collective-permute-done | bytes 122912 | tf_op jit(solution)/shard_map/ppermute | solution.py:319
  14.1 0.0 copy-done
  14.1 0.0 copy-done.1
  14.1 3.1 %paint.1 = (f32[3,16,2048]{2,1,0:T(8,128)S(1)}, f32[8,512]{1,0:T(8,128)S(1)}) custom-call(s32[2]{0:T(128)S(1)} %pad_add_fusion.edge_ref, f32[32]{0:T(128)S(1)} %copy-done.1, f32[3,8,2048]{2,1,0:T(8,128)S(1)} %copy-done, f32[3,5,2048]{2,1,0:T(8,128)S(1)} %collective-permute-done.low_ref, f32[3,5,2048]{2,1,0:T(8,128)S(1)} %collective-permute-done.1.high_ref, ...), custom_call_target="tpu_custom_call" | custom-call | flops 8000000000 | bytes 2000000 | tf_op jit(solution)/shard_map/paint/pallas_call | solution.py:340
  17.2 0.1 maximum_maximum_fusion
  17.3 0.0 copy-start.3
  17.3 0.7 broadcast_in_dim.340
  18.0 4.2 %all-to-all-start = ((f32[8,8,512]{2,1,0:T(8,128)}), f32[8,8,512]{2,1,0:T(8,128)S(1)}, u32[]{:S(2)}, u32[]{:S(2)}) async-start(f32[8,8,512]{2,1,0:T(8,128)} %broadcast_in_dim.340), calls=%async_computation | async-start | bytes 262144 | tf_op jit(solution)/shard_map/all_to_all | solution.py:288
  22.2 0.0 copy-done.3
  22.2 0.1 reshape.243.k_ref
  22.3 6.0 %all-to-all-done = f32[8,8,512]{2,1,0:T(8,128)S(1)} async-done(((f32[8,8,512]{2,1,0:T(8,128)}), f32[8,8,512]{2,1,0:T(8,128)S(1)}, u32[]{:S(2)}, u32[]{:S(2)}) %all-to-all-start) | async-done | bytes 131104 | tf_op jit(solution)/shard_map/all_to_all | solution.py:288
  28.3 0.1 multiply_reduce_fusion
  28.4 0.6 broadcast_in_dim.348
  29.1 4.6 %all-to-all-start.1 = ((f32[4,8,512]{2,1,0:T(8,128)}), f32[4,8,512]{2,1,0:T(8,128)S(1)}, u32[]{:S(2)}, u32[]{:S(2)}) async-start(f32[4,8,512]{2,1,0:T(8,128)} %broadcast_in_dim.348), calls=%async_computation.1 | async-start | bytes 131072 | tf_op jit(solution)/shard_map/all_to_all | solution.py:288
  33.7 0.1 exponential_select_fusion.1
  33.8 2.3 %short.1.s_ref = f32[3,16,2048]{2,1,0:T(8,128)S(1)} custom-call(f32[25]{0:T(128)S(1)} %reshape.243.k_ref, f32[3,16,2048]{2,1,0:T(8,128)S(1)} %get-tuple-element.19.c_ref), custom_call_target="tpu_custom_call" | custom-call | flops 10000000 | bytes 1000000 | tf_op jit(solution)/shard_map/short/pallas_call | solution.py:358
  36.0 1.2 all-to-all-done.1
  37.2 0.1 multiply_reduce_fusion.2
  37.3 1.9 %bend.1 = (f32[80,8,128]{2,1,0:T(8,128)S(1)}, f32[144,8,128]{2,1,0:T(8,128)S(1)}) custom-call(s32[2]{0:T(128)S(1)} %pad_add_fusion.edge_ref, f32[3,16,2048]{2,1,0:T(8,128)S(1)} %short.1.s_ref, f32[8,512]{1,0:T(8,128)S(1)} %get-tuple-element.20.coarse_ref, f32[8,512]{1,0:T(8,128)S(1)} %add.164.acc_ref, f32[512,512]{1,0:T(8,128)S(1)} %multiply_exponential_fusion.ec_ref, ...), custom_call_target="tpu_custom_call" | custom-call | flops 100000000 | bytes 2000000 | tf_op jit(solution)/shard_map/bend/pallas_call | solution.py:368
  39.2 41.0 %all_to_all.20.sent_ref = f32[80,8,128]{2,1,0:T(8,128)S(1)} all-to-all(f32[80,8,128]{2,1,0:T(8,128)S(1)} %get-tuple-element.24), channel_id=1, replica_groups=mesh['plane'=16,'far'=4,'near'=8] {'plane'}, dimensions={0} | all-to-all | bytes 655360 | tf_op jit(solution)/shard_map/all_to_all | solution.py:378
  80.2 1.0 scan.1
  81.2 36.5 %all_to_all.21.state_ref = f32[128,8,128]{2,1,0:T(8,128)S(1)} all-to-all(f32[128,8,128]{2,1,0:T(8,128)S(1)} %scan.1), channel_id=1, replica_groups=mesh['plane'=16,'far'=4,'near'=8] {'plane'}, dimensions={0} | all-to-all | bytes 1048576 | tf_op jit(solution)/shard_map/all_to_all | solution.py:382
  117.7 1.8 %final.1 = f32[4,3,8,2048]{3,2,1,0:T(8,128)} custom-call(f32[3]{0:T(128)S(1)} %dynamic_slice.6.mixing_ref, f32[3]{0:T(128)S(1)} %dynamic_slice.7.bending_ref, f32[144,8,128]{2,1,0:T(8,128)S(1)} %get-tuple-element.21.u_ref, f32[128,8,128]{2,1,0:T(8,128)S(1)} %all_to_all.21.state_ref), custom_call_target="tpu_custom_call" | custom-call | flops 10000000 | bytes 1000000 | tf_op jit(solution)/shard_map/final/pallas_call | solution.py:383
  (23 shorter events, 0.1 us)
Async XLA Ops:
  1.1 11.1 %collective-permute-start.1 = (f32[3,5,2048]{2,1,0:T(8,128)S(1)}, f32[3,5,2048]{2,1,0:T(8,128)S(1)}, u32[]{:S(2)}, u32[]{:S(2)}) collective-permute-start(f32[3,5,2048]{2,1,0:T(8,128)S(1)} %get-tuple-element.27), channel_id=1, source_target_pairs={{1,0},{2,1},{3,2},{4,3},{5,4},{6,5},{7,6},{8,7},{9,8},{10,9},{11,1... | collective-permute-start | bytes 368648 | tf_op jit(solution)/shard_map/ppermute | solution.py:320
  5.0 9.1 %collective-permute-start = (f32[3,5,2048]{2,1,0:T(8,128)S(1)}, f32[3,5,2048]{2,1,0:T(8,128)S(1)}, u32[]{:S(2)}, u32[]{:S(2)}) collective-permute-start(f32[3,5,2048]{2,1,0:T(8,128)S(1)} %get-tuple-element.28), channel_id=1, source_target_pairs={{0,1},{1,2},{2,3},{3,4},{4,5},{5,6},{6,7},{7,8},{8,9},{9,10},{10,1... | collective-permute-start | bytes 368648 | tf_op jit(solution)/shard_map/ppermute | solution.py:319
  7.3 0.7 copy-start.4
  8.1 0.7 copy-start.5
  9.1 0.7 copy-start.2
  11.6 2.5 %copy-start = (f32[3,8,2048]{2,1,0:T(8,128)S(1)}, f32[3,8,2048]{2,1,0:T(8,128)}, u32[]{:S(2)}) copy-start(f32[3,8,2048]{2,1,0:T(8,128)} %x_ref.1) | copy-start | bytes 589828
  12.1 2.0 %copy-start.1 = (f32[32]{0:T(128)S(1)}, f32[32]{0:T(128)}, u32[]{:S(2)}) copy-start(f32[32]{0:T(128)} %mix_ref.1) | copy-start | bytes 388
  17.3 4.9 %copy-start.3 = (f32[5,5]{1,0:T(8,128)S(1)}, f32[5,5]{1,0:T(8,128)}, u32[]{:S(2)}) copy-start(f32[5,5]{1,0:T(8,128)} %param.11) | copy-start | bytes 304
  18.0 10.4 %all-to-all-start = ((f32[8,8,512]{2,1,0:T(8,128)}), f32[8,8,512]{2,1,0:T(8,128)S(1)}, u32[]{:S(2)}, u32[]{:S(2)}) async-start(f32[8,8,512]{2,1,0:T(8,128)} %broadcast_in_dim.340), calls=%async_computation | async-start | bytes 262144 | tf_op jit(solution)/shard_map/all_to_all | solution.py:288
  29.1 8.2 %all-to-all-start.1 = ((f32[4,8,512]{2,1,0:T(8,128)}), f32[4,8,512]{2,1,0:T(8,128)S(1)}, u32[]{:S(2)}, u32[]{:S(2)}) async-start(f32[4,8,512]{2,1,0:T(8,128)} %broadcast_in_dim.348), calls=%async_computation.1 | async-start | bytes 131072 | tf_op jit(solution)/shard_map/all_to_all | solution.py:288

commit v4 on v3

v4 whole, which is shorter than its diff:
```python
import functools
import math

import jax
import jax.numpy as jnp
from jax import lax
from jax.experimental import pallas as pl
from jax.experimental.pallas import tpu as pltpu
from jax.sharding import Mesh
from jax.sharding import PartitionSpec as P

f32 = jnp.float32
bf16 = jnp.bfloat16
lens_gain = 0.25
channels = 32
highest = lax.Precision.HIGHEST


def distances(plane_slot, slot_total):
    distance = (plane_slot.astype(f32) + 1.0) / slot_total
    before = jnp.concatenate([jnp.zeros((1,), f32), distance[:-1]])
    after = jnp.concatenate([distance[1:], jnp.full((1,), (slot_total + 1.0) / slot_total, f32)])
    mixing = before * (after - distance) / (distance * (after - before))
    bending = lens_gain * (after - distance) / after
    return (mixing, bending)


def shifted(value, by):
    width = value.shape[-1]
    rolled = pltpu.roll(value, (-by) % width, value.ndim - 1)
    lane = lax.broadcasted_iota(jnp.int32, value.shape, value.ndim - 1)
    keep = lane < width - by if by > 0 else lane >= -by
    return jnp.where(keep, rolled, 0.0)


def tile_place():
    near, far = lax.axis_index("near"), lax.axis_index("far")
    return near, far, far * lax.axis_size("near") + near


def weights_kernel(w_ref, b_ref, out_ref, pool_ref):
    group = lax.broadcasted_iota(jnp.int32, pool_ref.shape, 0) // 4
    pool_ref[...] = jnp.where(group == lax.broadcasted_iota(jnp.int32, pool_ref.shape, 1), 1.0 / 16.0, 0.0)
    shape = (8, 160)
    row = lax.broadcasted_iota(jnp.int32, shape, 0)
    col = lax.broadcasted_iota(jnp.int32, shape, 1)
    part, in_row = col // 16, col % 16
    taps = []
    for i in range(3):
        for j in range(3):
            here = (in_row == row + 2 * i) & (part % 3 == j) & (part < 9)
            taps.append(jnp.where(here, 1.0, 0.0))
    bias_here = jnp.where((col >= 144) & (col < 147), 1.0, 0.0)
    for c in range(channels):
        exact = b_ref[c] * bias_here
        for t in range(9):
            exact = exact + w_ref[c, t] * taps[t]
        first = exact.astype(bf16).astype(f32)
        second = (exact - first).astype(bf16).astype(f32)
        third = exact - first - second
        value = jnp.where((col < 96) | (col == 144), first, jnp.where(col < 146, second, third))
        out_ref[8 * c : 8 * c + 8, :] = value.astype(bf16)


def paint_window(w_ref, mix_ref, stack, value, store):
    cols = value.shape[-1]
    for j in range(3):
        moved = value if j == 1 else shifted(value, 2 * (j - 1))
        upper = moved.astype(bf16)
        lower = (moved - upper.astype(f32)).astype(bf16)
        stack[16 * j : 16 * j + 16, :] = upper
        stack[48 + 16 * j : 64 + 16 * j, :] = lower
        stack[96 + 16 * j : 112 + 16 * j, :] = upper

    def one_chunk(chunk, carry):
        at = pl.ds(pl.multiple_of(chunk * 256, 256), 256)
        before = jnp.dot(w_ref[...], stack[:, at], preferred_element_type=f32)
        total = jnp.zeros((8, 256), f32)
        for c in range(channels):
            total = total + mix_ref[channels + c] * jnp.tanh(before[8 * c : 8 * c + 8, :])
        store(at, total)
        return carry

    lax.fori_loop(0, cols // 256, one_chunk, 0, unroll=True)


def paint_kernel(decay, mix_ref, x_ref, low_ref, high_ref, w_ref, pool_ref, c_ref, coarse_ref, copies_ref, wide, stack, sums):
    cols = x_ref.shape[-1]
    wide[12:16, :] = jnp.zeros((4, cols), f32)
    sums[6:8, :] = jnp.zeros((2, cols), f32)
    stack[144:160, :] = jnp.ones((16, cols), bf16)
    for p in range(3):
        wide[0:2, :] = low_ref[p, 3:5, :]
        wide[2:10, :] = x_ref[p]
        wide[10:12, :] = high_ref[p, 0:2, :]

        def store(at, total):
            c_ref[p, :, at] = total
            sums[p : p + 1, at] = jnp.sum(total[0:4], axis=0, keepdims=True)
            sums[3 + p : 4 + p, at] = jnp.sum(total[4:8], axis=0, keepdims=True)

        paint_window(w_ref, mix_ref, stack, wide[...], store)
    quarter = cols // 4
    stacked = jnp.concatenate([sums[:, quarter * v : quarter * (v + 1)] for v in range(4)], axis=0)
    pooled = jnp.dot(stacked, pool_ref[...], precision=highest, preferred_element_type=f32)
    e = decay
    row = lax.broadcasted_iota(jnp.int32, (8, 128), 0)
    for v in range(4):
        at = slice(128 * v, 128 * v + 128)
        here = pooled[8 * v : 8 * v + 8]
        coarse_ref[:, at] = here
        turned = jnp.where(row < 3, pltpu.roll(here, 5, 0), pltpu.roll(here, 3, 0))
        upper = jnp.where(row < 3, here, turned)
        lower = jnp.where(row < 3, turned, here)
        message = jnp.where(row < 3, e * e * upper + e * lower, e * upper + e * e * lower)
        message = jnp.where(row < 6, message, 0.0)
        for q in range(copies_ref.shape[0] // 8):
            copies_ref[8 * q : 8 * q + 8, at] = message


def edge_kernel(mix_ref, x_ref, low_ref, high_ref, w_ref, main_ref, c_ref, wide, stack):
    cols = x_ref.shape[-1]
    near, far, tile = tile_place()
    top = tile != 0
    bottom = tile != lax.axis_size("near") * lax.axis_size("far") - 1
    stack[144:160, :] = jnp.ones((16, cols), bf16)
    c_ref[:, 14:16, :] = jnp.zeros((3, 2, cols), f32)
    for p in range(3):
        wide[0:5, :] = low_ref[p]
        wide[5:13, :] = x_ref[p]
        wide[13:16, :] = jnp.zeros((3, cols), f32)

        def store_above(at, total):
            c_ref[p, 0:3, at] = jnp.where(top, total[0:3], 0.0)

        paint_window(w_ref, mix_ref, stack, wide[...], store_above)
        wide[0:7, :] = x_ref[p, 1:8, :]
        wide[7:12, :] = high_ref[p]
        wide[12:16, :] = jnp.zeros((4, cols), f32)

        def store_below(at, total):
            c_ref[p, 11:14, at] = jnp.where(bottom, total[5:8], 0.0)

        paint_window(w_ref, mix_ref, stack, wide[...], store_below)
        c_ref[p, 3:11, :] = main_ref[p]


def tile_decay(tiles, used):
    return jnp.where(used, jnp.exp(jnp.maximum(tiles, 0).astype(f32) / -8.0), 0.0)


def runs_kernel(received_ref, total_ref, copies_ref):
    near = lax.axis_index("near")
    count = received_ref.shape[0] // 8
    cols = received_ref.shape[-1]
    forward = lax.broadcasted_iota(jnp.int32, (8, 128), 0) < 3
    totals = [jnp.zeros((8, 128), f32)] * (cols // 128)
    runs = [jnp.zeros((8, 128), f32)] * (cols // 128)
    for q in range(count):
        gap = jnp.where(forward, near - q, q - near) - 1
        weight = tile_decay(gap, gap >= 0)
        to_edge = jnp.where(forward, math.exp(-(count - 1 - q) / 8.0), math.exp(-q / 8.0))
        for v in range(cols // 128):
            value = received_ref[8 * q : 8 * q + 8, 128 * v : 128 * v + 128]
            totals[v] = totals[v] + weight * value
            runs[v] = runs[v] + to_edge * value
    for v in range(cols // 128):
        at = slice(128 * v, 128 * v + 128)
        total_ref[:, at] = totals[v]
        for w in range(copies_ref.shape[0] // 8):
            copies_ref[8 * w : 8 * w + 8, at] = runs[v]


def short_kernel_body(scale, k_ref, c_ref, s_ref, ec_ref, held):
    cols = c_ref.shape[-1]
    for p in range(3):
        held[0:16, :] = c_ref[p]
        held[16:24, :] = jnp.zeros((8, cols), f32)
        for window in range(2):
            total = jnp.zeros((8, cols), f32)
            for b in range(5):
                part = jnp.zeros((8, cols), f32)
                for a in range(5):
                    start = 8 * window + a
                    part = part + k_ref[a, b] * held[start : start + 8, :]
                total = total + (part if b == 2 else shifted(part, b - 2))
            s_ref[p, 8 * window : 8 * window + 8, :] = total
    gap = lax.broadcasted_iota(jnp.int32, ec_ref.shape, 0) - lax.broadcasted_iota(jnp.int32, ec_ref.shape, 1)
    ec_ref[...] = jnp.exp(-jnp.abs(gap.astype(f32)) / scale)


def side_matrix(back):
    shape = (128, 128)
    i = lax.broadcasted_iota(jnp.int32, shape, 1 if back else 0)
    j = lax.broadcasted_iota(jnp.int32, shape, 0 if back else 1)
    return jnp.where(j // 8 == i, jnp.where(i < 8, 1.0, 0.0), 0.0)


def own_lane():
    shape = (8, 128)
    lane = lax.broadcasted_iota(jnp.int32, shape, 1)
    return (lane < 64) & (lane % 8 == lax.broadcasted_iota(jnp.int32, shape, 0))


def bend_kernel(decay, gain, s_ref, coarse_ref, total_ref, run_ref, ec_ref, sent_ref, pot_ref, rows, rim):
    cols = s_ref.shape[-1]
    e = decay
    near, far, tile = tile_place()
    near_count = lax.axis_size("near")
    forward = lax.broadcasted_iota(jnp.int32, (8, rows.shape[-1]), 0) < 3
    acc = total_ref[...]
    inside = jnp.where(forward, near, near_count - 1 - near)
    for w in range(run_ref.shape[0] // 8):
        gap = jnp.where(forward, far - w, w - far) - 1
        acc = acc + tile_decay(gap * near_count + inside, gap >= 0) * run_ref[8 * w : 8 * w + 8, :]
    c0, c1 = coarse_ref[0:3, :], coarse_ref[3:6, :]
    up, down = acc[0:3, :], acc[3:6, :]
    rows[12:16, :] = jnp.zeros((4, rows.shape[-1]), f32)
    rows[0:3, :] = e * c0 + e * e * c1 + e * e * down + up * (1.0 / e)
    rows[3:6, :] = c0 + e * c1 + up + e * down
    rows[6:9, :] = c1 + e * c0 + e * up + down
    rows[9:12, :] = e * e * c0 + e * c1 + e * e * up + down * (1.0 / e)
    smooth = gain * jnp.dot(rows[...], ec_ref[...], precision=highest, preferred_element_type=f32)
    stacked = jnp.concatenate([smooth[:, 128 * v : 128 * v + 128] for v in range(4)], axis=0)
    shape = (128, 512)
    group = lax.broadcasted_iota(jnp.int32, shape, 1) // 4
    grow = jnp.where(group == lax.broadcasted_iota(jnp.int32, shape, 0), 1.0, 0.0)
    grown = jnp.dot(stacked, grow, precision=highest, preferred_element_type=f32)
    long = jnp.concatenate([grown[16 * v : 16 * v + 16] for v in range(4)], axis=1)
    row = lax.broadcasted_iota(jnp.int32, (8, cols), 0)
    lane = lax.broadcasted_iota(jnp.int32, (8, cols), 1) % 128
    top = tile != 0
    bottom = tile != near_count * lax.axis_size("far") - 1
    rim[6:8, :] = jnp.zeros((2, cols), f32)
    side = jnp.zeros((8, cols), f32)
    for p in range(3):
        part = s_ref[p]
        wide = jnp.where(
            row < 4,
            jnp.broadcast_to(long[3 + p : 4 + p], (8, cols)),
            jnp.broadcast_to(long[6 + p : 7 + p], (8, cols)),
        )
        here = part[1:9] + wide
        above_row = jnp.where(top, part[0:1] + long[p : p + 1], 0.0)
        below_row = jnp.where(bottom, part[9:10] + long[9 + p : 10 + p], 0.0)
        pot_ref[p, 7:8, :] = above_row
        pot_ref[p, 8:16, :] = here
        pot_ref[p, 16:17, :] = below_row
        rim[p : p + 1, :] = above_row
        rim[3 + p : 4 + p, :] = below_row
        side = jnp.where(lane == 2 * p, shifted(here, -1 - 2 * p), side)
        side = jnp.where(lane == 2 * p + 1, shifted(here, 127 - 2 * p), side)
        for d in range(cols // 128):
            at = slice(128 * d, 128 * d + 128)
            sent_ref[4 * d + p] = here[:, at]
    rim_rows = rim[...]
    side = jnp.where(lane == 6, shifted(rim_rows, -7), side)
    side = jnp.where(lane == 7, shifted(rim_rows, 121), side)
    blocks = cols // 128
    spread = side_matrix(False)
    lined = jnp.concatenate([side[:, 128 * d : 128 * d + 128] for d in range(blocks)], axis=0)
    lined = jnp.dot(lined, spread, precision=highest, preferred_element_type=f32)
    own = own_lane()
    row = lax.broadcasted_iota(jnp.int32, (8, 128), 0)
    for d in range(blocks):
        line = jnp.sum(jnp.where(own, lined[8 * d : 8 * d + 8], 0.0), axis=0, keepdims=True)
        line = jnp.broadcast_to(line, (8, 128))
        sent_ref[4 * d + 3] = jnp.where(row == 6, line, rim_rows[:, 128 * d : 128 * d + 128])


def own_hessian(pot_ref, u_ref):
    cols = pot_ref.shape[-1]
    for p in range(3):
        here = pot_ref[p, 8:16, :]
        above, below = pot_ref[p, 7:15, :], pot_ref[p, 9:17, :]
        u11 = below - 2.0 * here + above
        u22 = shifted(here, 1) - 2.0 * here + shifted(here, -1)
        step = below - above
        u12 = (shifted(step, 1) - shifted(step, -1)) * 0.25
        for d in range(cols // 128):
            at = slice(128 * d, 128 * d + 128)
            u_ref[9 * d + 3 * p] = u11[:, at]
            u_ref[9 * d + 3 * p + 1] = u12[:, at]
            u_ref[9 * d + 3 * p + 2] = u22[:, at]


def advance(previous, current, u11, u12, u22, mixing, bending):
    kept = 1.0 - mixing
    bent = (
        u11 * current[0] + u12 * current[2],
        u11 * current[1] + u12 * current[3],
        u12 * current[0] + u22 * current[2],
        u12 * current[1] + u22 * current[3],
    )
    return tuple(kept * previous[i] + mixing * current[i] - bending * bent[i] for i in range(4))


def beside(value, left, right):
    lane = lax.broadcasted_iota(jnp.int32, value.shape, 1)
    before = jnp.where(lane == 0, jnp.broadcast_to(left, value.shape), pltpu.roll(value, 1, 1))
    after = jnp.where(lane == 127, jnp.broadcast_to(right, value.shape), pltpu.roll(value, 127, 1))
    return before, after


def over_rows(value, above, below):
    row = lax.broadcasted_iota(jnp.int32, value.shape, 0)
    before = jnp.where(row == 0, jnp.broadcast_to(above, value.shape), pltpu.roll(value, 1, 0))
    after = jnp.where(row == 7, jnp.broadcast_to(below, value.shape), pltpu.roll(value, 7, 0))
    return before, after


def scan_kernel(mixing_ref, bending_ref, sent_ref, pot_ref, state_ref, u_ref):
    own_hessian(pot_ref, u_ref)
    one = jnp.ones((8, 128), f32)
    zero = jnp.zeros((8, 128), f32)
    groups = sent_ref.shape[0] // 4
    own = own_lane()
    lines = [jnp.broadcast_to(sent_ref[4 * g + 3, 6:7, :], (8, 128)) for g in range(groups)]
    lined = jnp.concatenate([jnp.where(own, line, 0.0) for line in lines], axis=0)
    sides = jnp.dot(lined, side_matrix(True), precision=highest, preferred_element_type=f32)

    previous = current = (one, zero, zero, one)
    for g in range(groups):
        for i in range(4):
            state_ref[8 * g + i] = previous[i]
            state_ref[8 * g + 4 + i] = current[i]
        rim = sent_ref[4 * g + 3]
        side = sides[8 * g : 8 * g + 8]
        rim_left, rim_right = beside(rim, side[:, 6:7], side[:, 7:8])
        rim_step = rim_right - rim_left
        for p in range(3):
            k = 3 * g + p
            here = sent_ref[4 * g + p]
            above, below = over_rows(here, rim[p : p + 1], rim[3 + p : 4 + p])
            left, right = beside(here, side[:, 2 * p : 2 * p + 1], side[:, 2 * p + 1 : 2 * p + 2])
            u11 = below - 2.0 * here + above
            u22 = right - 2.0 * here + left
            step_above, step_below = over_rows(right - left, rim_step[p : p + 1], rim_step[3 + p : 4 + p])
            u12 = (step_below - step_above) * 0.25
            later = advance(previous, current, u11, u12, u22, mixing_ref[k], bending_ref[k])
            previous, current = current, later


def final_kernel(mixing_ref, bending_ref, u_ref, state_ref, out_ref):
    blocks = u_ref.shape[0] // 9
    first = 3 * lax.axis_index("plane")

    def one_block(d, carry):
        at = pl.ds(pl.multiple_of(d * 128, 128), 128)
        previous = tuple(state_ref[8 * d + i] for i in range(4))
        current = tuple(state_ref[8 * d + 4 + i] for i in range(4))
        for p in range(3):
            k = 9 * d + 3 * p
            later = advance(
                previous,
                current,
                u_ref[k],
                u_ref[k + 1],
                u_ref[k + 2],
                mixing_ref[first + p],
                bending_ref[first + p],
            )
            for i in range(4):
                out_ref[i, p, :, at] = later[i]
            previous, current = current, later
        return carry

    lax.fori_loop(0, blocks, one_block, 0, unroll=True)


vmem = pl.BlockSpec(memory_space=pltpu.VMEM)
smem = pl.BlockSpec(memory_space=pltpu.SMEM)


def sds(*shape):
    return jax.ShapeDtypeStruct(shape, f32)


def call(kernel, name, n_smem, n_vmem, out_shape, scratch=(), cost=(0, 0, 0)):
    outs = jax.tree.map(lambda _: vmem, out_shape)
    return pl.pallas_call(
        kernel,
        name=name,
        out_shape=out_shape,
        in_specs=[smem] * n_smem + [vmem] * n_vmem,
        out_specs=outs,
        scratch_shapes=list(scratch),
        cost_estimate=pl.CostEstimate(flops=cost[0], bytes_accessed=cost[1], transcendentals=cost[2]),
        compiler_params=pltpu.CompilerParams(vmem_limit_bytes=24 << 20),
    )


def body(density, plane_slot, paint_weight, paint_bias, mix_weight, short_kernel):
    plane_count, row_count, col_count = density.shape
    tile = ("far", "near")
    near_count, far_count = lax.axis_size("near"), lax.axis_size("far")
    tile_count = far_count * near_count
    group_count = lax.axis_size("plane")
    coarse_cols = col_count // 4
    row_scale = row_count * tile_count / 16.0
    col_scale = col_count / 16.0
    long_gain = 1.0 / math.sqrt(row_scale * col_scale)
    decay = math.exp(-1.0 / row_scale)

    up = [(i, i + 1) for i in range(tile_count - 1)]
    low = lax.ppermute(density[:, 3:8, :], tile, up)
    high = lax.ppermute(density[:, 0:5, :], tile, [(b, a) for a, b in up])

    scalars = jnp.concatenate([paint_bias, mix_weight])
    weights, pool = call(
        weights_kernel,
        "weights",
        2,
        0,
        (jax.ShapeDtypeStruct((channels * 8, 160), bf16), sds(col_count // 4, col_count // 16)),
        (),
        (10**6, 10**5, 0),
    )(paint_weight, scalars)
    mixing, bending = distances(plane_slot, 2 * plane_slot.shape[0])
    main, coarse, copies = call(
        functools.partial(paint_kernel, decay),
        "paint",
        1,
        5,
        (
            sds(plane_count, row_count, col_count),
            sds(8, coarse_cols),
            sds(8 * near_count, coarse_cols),
        ),
        [pltpu.VMEM((16, col_count), f32), pltpu.VMEM((160, col_count), bf16), pltpu.VMEM((8, col_count), f32)],
        (4 * 10**9, 2 * 10**6, 10**6),
    )(scalars, density, low, high, weights, pool)
    copies, mixing, bending = lax.optimization_barrier((copies, mixing, bending))

    received = lax.all_to_all(copies, "near", 0, 0, tiled=True)
    convergence = call(
        edge_kernel,
        "edges",
        1,
        5,
        sds(plane_count, 16, col_count),
        [pltpu.VMEM((16, col_count), f32), pltpu.VMEM((160, col_count), bf16)],
        (8 * 10**9, 2 * 10**6, 10**6),
    )(scalars, density, low, high, weights, main)
    total, run_copies = call(
        runs_kernel, "runs", 0, 1, (sds(8, coarse_cols), sds(8 * far_count, coarse_cols)), (), (10**6, 10**5, 0)
    )(received)
    convergence, run_copies = lax.optimization_barrier((convergence, run_copies))
    runs = lax.all_to_all(run_copies, "far", 0, 0, tiled=True)
    short_part, col_kernel = call(
        functools.partial(short_kernel_body, col_scale),
        "short",
        1,
        1,
        (sds(plane_count, 16, col_count), sds(coarse_cols, coarse_cols)),
        [pltpu.VMEM((24, col_count), f32)],
        (10**7, 10**6, 0),
    )(short_kernel, convergence)

    sent, potential = call(
        functools.partial(bend_kernel, decay, long_gain),
        "bend",
        0,
        5,
        (sds(group_count * 4, 8, 128), sds(plane_count, 24, col_count)),
        [pltpu.VMEM((16, coarse_cols), f32), pltpu.VMEM((8, col_count), f32)],
        (10**8, 2 * 10**6, 0),
    )(short_part, coarse, total, runs, col_kernel)

    gathered = lax.all_to_all(sent, "plane", 0, 0, tiled=True)
    states, shear = call(
        scan_kernel,
        "scan",
        2,
        2,
        (sds(group_count * 8, 8, 128), sds(group_count * 9, 8, 128)),
        (),
        (10**7, 10**6, 0),
    )(mixing, bending, gathered, potential)
    mine = lax.all_to_all(states, "plane", 0, 0, tiled=True)
    return call(final_kernel, "final", 2, 2, sds(4, plane_count, row_count, col_count), (), (10**7, 10**6, 0))(
        mixing, bending, shear, mine
    )


def solution(mesh):
    planes, tiles = mesh.devices.shape
    split = Mesh(mesh.devices.reshape(planes, 4, tiles // 4), ("plane", "far", "near"))
    tile = ("far", "near")
    placed = (P("plane", tile, None), P(), P(), P(), P(), P())
    return jax.shard_map(
        body, mesh=split, in_specs=placed, out_specs=P(None, "plane", tile, None), check_vma=False
    )
```

time: 120 us -> 115 us (0.958)
  the two profiles are of different devices: /device:TPU:64 before, /device:TPU:49 now
where the time goes in v4:
time: 115 us; the launch traced here: 114 us
  blocking collectives  76.2 us (66%)
  starting transfers between devices  19.9 us (17%)
  Pallas kernels  14 us (12%)
  waiting for transfers between devices  2.07 us (2%)
  local copies, waits for them, and re-layouts  1.86 us (2%)
    all_to_all x1, blocking collectives, body(): gathered = lax.all_to_all(sent, 'plane', 0, 0, tiled=True)  38.9 us
    all_to_all x1, blocking collectives, body(): mine = lax.all_to_all(states, 'plane', 0, 0, tiled=True)  37.2 us
    all_to_all x1, starting transfers between devices, body(): received = lax.all_to_all(copies, 'near', 0, 0, tiled=True)  8.79 us
    all_to_all x1, starting transfers between devices, body(): runs = lax.all_to_all(run_copies, 'far', 0, 0, tiled=True)  5.57 us
    ppermute x1, starting transfers between devices, body(): low = lax.ppermute(density[:, 3:8, :], tile, up)  2.98 us
    pallas_call x1, Pallas kernels, body(): call(functools.partial(paint_kernel, decay), 'paint', 1, 5, (sds(plane_co...  2.76 us
    pallas_call x1, Pallas kernels, body(): call(functools.partial(short_kernel_body, col_scale), 'short', 1, 1, (sds...  2.72 us
    pallas_call x1, Pallas kernels, body(): call(edge_kernel, 'edges', 1, 5, sds(plane_count, 16, col_count), [pltpu....  2.63 us
  transfers between devices with their start and end apart: 4, of which 3 were waited for; matrix products, arithmetic and copies ran while one was open for 0% of the time, Pallas kernels for 6%

profile of v4, /device:TPU:49, one launch (start us, length us, event | category | flops | bytes accessed | tf_op | source)
XLA Modules:
  0.0 114.3 jit_solution(4310668020133298880)
XLA Ops:
  0.0 0.0 copy-start
  0.0 0.0 copy-start.2
  0.0 1.1 fusion
  1.1 0.0 copy-start.3
  1.1 2.6 %collective-permute-start.1 = (f32[3,5,2048]{2,1,0:T(8,128)S(1)}, f32[3,5,2048]{2,1,0:T(8,128)S(1)}, u32[]{:S(2)}, u32[]{:S(2)}) collective-permute-start(f32[3,5,2048]{2,1,0:T(8,128)S(1)} %get-tuple-element.41), channel_id=1, source_target_pairs={{1,0},{2,1},{3,2},{4,3},{5,4},{6,5},{7,6},{8,7},{9,8},{10,9},{11,1... | collective-permute-start | bytes 368648 | tf_op jit(solution)/shard_map/ppermute | solution.py:407
  3.7 3.0 %collective-permute-start = (f32[3,5,2048]{2,1,0:T(8,128)S(1)}, f32[3,5,2048]{2,1,0:T(8,128)S(1)}, u32[]{:S(2)}, u32[]{:S(2)}) collective-permute-start(f32[3,5,2048]{2,1,0:T(8,128)S(1)} %get-tuple-element.42), channel_id=1, source_target_pairs={{0,1},{1,2},{2,3},{3,4},{4,5},{5,6},{6,7},{7,8},{8,9},{9,10},{10,1... | collective-permute-start | bytes 368648 | tf_op jit(solution)/shard_map/ppermute | solution.py:406
  6.7 0.0 copy-done.3
  6.7 0.1 fusion.1
  6.8 0.0 copy-done.2
  6.8 0.0 copy-start.4
  6.8 0.0 copy-start.5
  6.8 0.1 copy.7.w_ref
  6.9 0.6 copy-done.4
  7.5 0.0 copy-done.5
  7.5 0.1 pad_maximum_fusion.b_ref.mix_ref
  7.5 1.1 weights.1
  8.7 0.1 multiply_divide_fusion
  8.8 0.0 collective-permute-done.1.high_ref
  8.8 0.5 collective-permute-done.low_ref
  9.3 0.0 copy-done
  9.3 2.8 %paint.1 = (f32[3,8,2048]{2,1,0:T(8,128)S(1)}, f32[8,512]{1,0:T(8,128)S(1)}, f32[64,512]{1,0:T(8,128)}) custom-call(f32[64]{0:T(128)S(1)} %pad_maximum_fusion.b_ref.mix_ref, f32[3,8,2048]{2,1,0:T(8,128)S(1)} %copy-done, f32[3,5,2048]{2,1,0:T(8,128)S(1)} %collective-permute-done.low_ref, f32[3,5,2048]{2,1,0:T(8,128)S(1)} %collective-permute-done.1.high_ref, ...), custom_call_target="tpu_custom_call" | custom-call | flops 4000000000 | bytes 2000000 | tf_op jit(solution)/shard_map/paint/pallas_call | solution.py:420
  12.1 8.8 %all-to-all-start = ((f32[8,8,512]{2,1,0:T(8,128)}), f32[8,8,512]{2,1,0:T(8,128)S(1)}, u32[]{:S(2)}, u32[]{:S(2)}) async-start(f32[8,8,512]{2,1,0:T(8,128)} %bitcast), calls=%async_computation | async-start | bytes 262144 | tf_op jit(solution)/shard_map/all_to_all | solution.py:435
  20.8 2.6 %edges.1.c_ref = f32[3,16,2048]{2,1,0:T(8,128)S(1)} custom-call(f32[64]{0:T(128)S(1)} %pad_maximum_fusion.b_ref.mix_ref, f32[3,8,2048]{2,1,0:T(8,128)S(1)} %copy-done, f32[3,5,2048]{2,1,0:T(8,128)S(1)} %collective-permute-done.low_ref, f32[3,5,2048]{2,1,0:T(8,128)S(1)} %collective-permute-done.1.high_ref, bf16[256,160]{1,0:T(8,128)(2,1)S(1)} %get-tuple-element.23.w_ref, ...), custom_call_target="tpu_custom_call" | custom-call | flops 8000000000 | bytes 2000000 | tf_op jit(solution)/shard_map/edges/pallas_call | solution.py:436
  23.5 0.5 all-to-all-done
  24.0 0.6 runs.1
  24.6 0.0 copy-start.1
  24.6 5.6 %all-to-all-start.1 = ((f32[4,8,512]{2,1,0:T(8,128)}), f32[4,8,512]{2,1,0:T(8,128)S(1)}, u32[]{:S(2)}, u32[]{:S(2)}) async-start(f32[4,8,512]{2,1,0:T(8,128)} %bitcast.2), calls=%async_computation.1 | async-start | bytes 131072 | tf_op jit(solution)/shard_map/all_to_all | solution.py:449
  30.2 0.0 copy-done.1
  30.2 2.7 %short.1 = (f32[3,16,2048]{2,1,0:T(8,128)S(1)}, f32[512,512]{1,0:T(8,128)S(1)}) custom-call(f32[5,5]{1,0:T(8,128)S(1)} %copy-done.1, f32[3,16,2048]{2,1,0:T(8,128)S(1)} %edges.1.c_ref), custom_call_target="tpu_custom_call" | custom-call | flops 10000000 | bytes 1000000 | tf_op jit(solution)/shard_map/short/pallas_call | solution.py:450
  32.9 1.0 all-to-all-done.1
  34.0 1.3 %bend.1 = (f32[64,8,128]{2,1,0:T(8,128)S(1)}, f32[3,24,2048]{2,1,0:T(8,128)S(1)}) custom-call(f32[3,16,2048]{2,1,0:T(8,128)S(1)} %get-tuple-element.32.s_ref, f32[8,512]{1,0:T(8,128)S(1)} %get-tuple-element.33.coarse_ref, f32[8,512]{1,0:T(8,128)S(1)} %get-tuple-element.34.total_ref, f32[32,512]{1,0:T(8,128)S(1)} %bitcast.5, ...), custom_call_target="tpu_custom_call" | custom-call | flops 100000000 | bytes 2000000 | tf_op jit(solution)/shard_map/bend/pallas_call | solution.py:460
  35.2 38.9 %all_to_all.32.sent_ref = f32[64,8,128]{2,1,0:T(8,128)S(1)} all-to-all(f32[64,8,128]{2,1,0:T(8,128)S(1)} %get-tuple-element.37), channel_id=1, replica_groups=mesh['plane'=16,'far'=4,'near'=8] {'plane'}, dimensions={0} | all-to-all | bytes 524288 | tf_op jit(solution)/shard_map/all_to_all | solution.py:470
  74.2 1.2 %scan.1 = (f32[128,8,128]{2,1,0:T(8,128)S(1)}, f32[144,8,128]{2,1,0:T(8,128)S(1)}) custom-call(f32[48]{0:T(128)S(1)} %get-tuple-element.26.mixing_ref, f32[48]{0:T(128)S(1)} %get-tuple-element.27.bending_ref, f32[64,8,128]{2,1,0:T(8,128)S(1)} %all_to_all.32.sent_ref, f32[3,24,2048]{2,1,0:T(8,128)S(1)} %get-tuple-element.38.pot_ref), custom_call_target="tpu_custom_call" | custom-call | flops 10000000 | bytes 1000000 | tf_op jit(solution)/shard_map/scan/pallas_call | solution.py:471
  75.4 37.2 %all_to_all.33.state_ref = f32[128,8,128]{2,1,0:T(8,128)S(1)} all-to-all(f32[128,8,128]{2,1,0:T(8,128)S(1)} %get-tuple-element.40), channel_id=1, replica_groups=mesh['plane'=16,'far'=4,'near'=8] {'plane'}, dimensions={0} | all-to-all | bytes 1048576 | tf_op jit(solution)/shard_map/all_to_all | solution.py:480
  112.6 1.7 %final.1 = f32[4,3,8,2048]{3,2,1,0:T(8,128)} custom-call(f32[48]{0:T(128)S(1)} %get-tuple-element.26.mixing_ref, f32[48]{0:T(128)S(1)} %get-tuple-element.27.bending_ref, f32[144,8,128]{2,1,0:T(8,128)S(1)} %get-tuple-element.39.u_ref, f32[128,8,128]{2,1,0:T(8,128)S(1)} %all_to_all.33.state_ref), custom_call_target="tpu_custom_call" | custom-call | flops 10000000 | bytes 1000000 | tf_op jit(solution)/shard_map/final/pallas_call | solution.py:481
  (1 shorter events, 0.0 us)
Async XLA Ops:
  0.0 9.3 %copy-start = (f32[3,8,2048]{2,1,0:T(8,128)S(1)}, f32[3,8,2048]{2,1,0:T(8,128)}, u32[]{:S(2)}) copy-start(f32[3,8,2048]{2,1,0:T(8,128)} %x_ref.3) | copy-start | bytes 589828
  0.0 6.8 %copy-start.2 = (f32[32,9]{0,1:T(8,128)S(1)}, f32[32,9]{0,1:T(8,128)}, u32[]{:S(2)}) copy-start(f32[32,9]{0,1:T(8,128)} %param.8) | copy-start | bytes 3460
  1.1 5.6 %copy-start.3 = (s32[48]{0:T(128)S(1)}, s32[48]{0:T(128)}, u32[]{:S(2)}) copy-start(s32[48]{0:T(128)} %param.7) | copy-start | bytes 580
  1.1 7.6 %collective-permute-start.1 = (f32[3,5,2048]{2,1,0:T(8,128)S(1)}, f32[3,5,2048]{2,1,0:T(8,128)S(1)}, u32[]{:S(2)}, u32[]{:S(2)}) collective-permute-start(f32[3,5,2048]{2,1,0:T(8,128)S(1)} %get-tuple-element.41), channel_id=1, source_target_pairs={{1,0},{2,1},{3,2},{4,3},{5,4},{6,5},{7,6},{8,7},{9,8},{10,9},{11,1... | collective-permute-start | bytes 368648 | tf_op jit(solution)/shard_map/ppermute | solution.py:407
  3.7 5.6 %collective-permute-start = (f32[3,5,2048]{2,1,0:T(8,128)S(1)}, f32[3,5,2048]{2,1,0:T(8,128)S(1)}, u32[]{:S(2)}, u32[]{:S(2)}) collective-permute-start(f32[3,5,2048]{2,1,0:T(8,128)S(1)} %get-tuple-element.42), channel_id=1, source_target_pairs={{0,1},{1,2},{2,3},{3,4},{4,5},{5,6},{6,7},{7,8},{8,9},{9,10},{10,1... | collective-permute-start | bytes 368648 | tf_op jit(solution)/shard_map/ppermute | solution.py:406
  6.8 0.7 copy-start.4
  6.8 0.7 copy-start.5
  12.1 11.9 %all-to-all-start = ((f32[8,8,512]{2,1,0:T(8,128)}), f32[8,8,512]{2,1,0:T(8,128)S(1)}, u32[]{:S(2)}, u32[]{:S(2)}) async-start(f32[8,8,512]{2,1,0:T(8,128)} %bitcast), calls=%async_computation | async-start | bytes 262144 | tf_op jit(solution)/shard_map/all_to_all | solution.py:435
  24.6 5.6 %copy-start.1 = (f32[5,5]{1,0:T(8,128)S(1)}, f32[5,5]{1,0:T(8,128)}, u32[]{:S(2)}) copy-start(f32[5,5]{1,0:T(8,128)} %k_ref.1) | copy-start | bytes 304
  24.6 9.3 %all-to-all-start.1 = ((f32[4,8,512]{2,1,0:T(8,128)}), f32[4,8,512]{2,1,0:T(8,128)S(1)}, u32[]{:S(2)}, u32[]{:S(2)}) async-start(f32[4,8,512]{2,1,0:T(8,128)} %bitcast.2), calls=%async_computation.1 | async-start | bytes 131072 | tf_op jit(solution)/shard_map/all_to_all | solution.py:449

commit v5 on v4

--- a/solution.py
+++ b/solution.py
@@ -315,22 +315,23 @@
     zero = jnp.zeros((8, 128), f32)
     groups = sent_ref.shape[0] // 4
     own = own_lane()
-    lines = [jnp.broadcast_to(sent_ref[4 * g + 3, 6:7, :], (8, 128)) for g in range(groups)]
+    at = [(g % 4) * (groups // 4) + g // 4 for g in range(groups)]
+    lines = [jnp.broadcast_to(sent_ref[4 * at[g] + 3, 6:7, :], (8, 128)) for g in range(groups)]
     lined = jnp.concatenate([jnp.where(own, line, 0.0) for line in lines], axis=0)
     sides = jnp.dot(lined, side_matrix(True), precision=highest, preferred_element_type=f32)
 
     previous = current = (one, zero, zero, one)
     for g in range(groups):
         for i in range(4):
-            state_ref[8 * g + i] = previous[i]
-            state_ref[8 * g + 4 + i] = current[i]
-        rim = sent_ref[4 * g + 3]
+            state_ref[8 * at[g] + i] = previous[i]
+            state_ref[8 * at[g] + 4 + i] = current[i]
+        rim = sent_ref[4 * at[g] + 3]
         side = sides[8 * g : 8 * g + 8]
         rim_left, rim_right = beside(rim, side[:, 6:7], side[:, 7:8])
         rim_step = rim_right - rim_left
         for p in range(3):
             k = 3 * g + p
-            here = sent_ref[4 * g + p]
+            here = sent_ref[4 * at[g] + p]
             above, below = over_rows(here, rim[p : p + 1], rim[3 + p : 4 + p])
             left, right = beside(here, side[:, 2 * p : 2 * p + 1], side[:, 2 * p + 1 : 2 * p + 2])
             u11 = below - 2.0 * here + above
@@ -343,7 +344,7 @@
 
 def final_kernel(mixing_ref, bending_ref, u_ref, state_ref, out_ref):
     blocks = u_ref.shape[0] // 9
-    first = 3 * lax.axis_index("plane")
+    first = 3 * (lax.axis_size("z") * lax.axis_index("x") + lax.axis_index("z"))
 
     def one_block(d, carry):
         at = pl.ds(pl.multiple_of(d * 128, 128), 128)
@@ -395,7 +396,7 @@
     tile = ("far", "near")
     near_count, far_count = lax.axis_size("near"), lax.axis_size("far")
     tile_count = far_count * near_count
-    group_count = lax.axis_size("plane")
+    group_count = lax.axis_size("x") * lax.axis_size("z")
     coarse_cols = col_count // 4
     row_scale = row_count * tile_count / 16.0
     col_scale = col_count / 16.0
@@ -467,7 +468,7 @@
         (10**8, 2 * 10**6, 0),
     )(short_part, coarse, total, runs, col_kernel)
 
-    gathered = lax.all_to_all(sent, "plane", 0, 0, tiled=True)
+    gathered = lax.all_to_all(sent, ("z", "x"), 0, 0, tiled=True)
     states, shear = call(
         scan_kernel,
         "scan",
@@ -477,7 +478,7 @@
         (),
         (10**7, 10**6, 0),
     )(mixing, bending, gathered, potential)
-    mine = lax.all_to_all(states, "plane", 0, 0, tiled=True)
+    mine = lax.all_to_all(states, ("z", "x"), 0, 0, tiled=True)
     return call(final_kernel, "final", 2, 2, sds(4, plane_count, row_count, col_count), (), (10**7, 10**6, 0))(
         mixing, bending, shear, mine
     )
@@ -485,9 +486,10 @@
 
 def solution(mesh):
     planes, tiles = mesh.devices.shape
-    split = Mesh(mesh.devices.reshape(planes, 4, tiles // 4), ("plane", "far", "near"))
+    split = Mesh(mesh.devices.reshape(planes // 4, 4, 4, tiles // 4), ("x", "z", "far", "near"))
     tile = ("far", "near")
-    placed = (P("plane", tile, None), P(), P(), P(), P(), P())
+    plane = ("x", "z")
+    placed = (P(plane, tile, None), P(), P(), P(), P(), P())
     return jax.shard_map(
-        body, mesh=split, in_specs=placed, out_specs=P(None, "plane", tile, None), check_vma=False
+        body, mesh=split, in_specs=placed, out_specs=P(None, plane, tile, None), check_vma=False
     )

time: 115 us -> 113 us (0.983)
  the two profiles are of different devices: /device:TPU:49 before, /device:TPU:6 now
where the time goes in v5:
time: 113 us; the launch traced here: 111 us
  blocking collectives  68.5 us (61%)
  starting transfers between devices  20.2 us (18%)
  Pallas kernels  14 us (12%)
  waiting for transfers between devices  6.52 us (6%)
  local copies, waits for them, and re-layouts  1.86 us (2%)
    all_to_all x1, blocking collectives, body(): gathered = lax.all_to_all(sent, ('z', 'x'), 0, 0, tiled=True)  34.7 us
    all_to_all x1, blocking collectives, body(): mine = lax.all_to_all(states, ('z', 'x'), 0, 0, tiled=True)  33.8 us
    all_to_all x1, starting transfers between devices, body(): runs = lax.all_to_all(run_copies, 'far', 0, 0, tiled=True)  8.32 us
    all_to_all x1, starting transfers between devices, body(): received = lax.all_to_all(copies, 'near', 0, 0, tiled=True)  7.58 us
    all_to_all x1, waiting for transfers between devices, body(): received = lax.all_to_all(copies, 'near', 0, 0, tiled=True)  3.5 us
    ppermute x1, starting transfers between devices, body(): low = lax.ppermute(density[:, 3:8, :], tile, up)  3.04 us
    all_to_all x1, waiting for transfers between devices, body(): runs = lax.all_to_all(run_copies, 'far', 0, 0, tiled=True)  3.02 us
    pallas_call x1, Pallas kernels, body(): call(functools.partial(paint_kernel, decay), 'paint', 1, 5, (sds(plane_co...  2.76 us
  transfers between devices with their start and end apart: 4, of which 2 were waited for; matrix products, arithmetic and copies ran while one was open for 0% of the time, Pallas kernels for 6%

profile of v5, /device:TPU:6, one launch (start us, length us, event | category | flops | bytes accessed | tf_op | source)
XLA Modules:
  0.0 111.4 jit_solution(18248631975445684278)
XLA Ops:
  0.0 0.0 copy-start
  0.0 0.0 copy-start.2
  0.0 1.1 fusion
  1.1 0.0 copy-start.3
  1.1 1.3 %collective-permute-start.1 = (f32[3,5,2048]{2,1,0:T(8,128)S(1)}, f32[3,5,2048]{2,1,0:T(8,128)S(1)}, u32[]{:S(2)}, u32[]{:S(2)}) collective-permute-start(f32[3,5,2048]{2,1,0:T(8,128)S(1)} %get-tuple-element.41), channel_id=1, source_target_pairs={{1,0},{2,1},{3,2},{4,3},{5,4},{6,5},{7,6},{8,7},{9,8},{10,9},{11,1... | collective-permute-start | bytes 368648 | tf_op jit(solution)/shard_map/ppermute | solution.py:408
  2.4 3.0 %collective-permute-start = (f32[3,5,2048]{2,1,0:T(8,128)S(1)}, f32[3,5,2048]{2,1,0:T(8,128)S(1)}, u32[]{:S(2)}, u32[]{:S(2)}) collective-permute-start(f32[3,5,2048]{2,1,0:T(8,128)S(1)} %get-tuple-element.42), channel_id=1, source_target_pairs={{0,1},{1,2},{2,3},{3,4},{4,5},{5,6},{6,7},{7,8},{8,9},{9,10},{10,1... | collective-permute-start | bytes 368648 | tf_op jit(solution)/shard_map/ppermute | solution.py:407
  5.5 0.0 copy-done.3
  5.5 0.1 fusion.1
  5.6 0.0 copy-done.2
  5.6 0.0 copy-start.4
  5.6 0.0 copy-start.5
  5.6 0.1 copy.7.w_ref
  5.7 0.6 copy-done.4
  6.2 0.0 copy-done.5
  6.2 0.1 pad_maximum_fusion.b_ref.mix_ref
  6.3 1.1 %weights.1 = (bf16[256,160]{1,0:T(8,128)(2,1)S(1)}, f32[512,128]{1,0:T(8,128)S(1)}) custom-call(f32[32,9]{1,0:T(8,128)S(1)} %copy.7.w_ref, f32[64]{0:T(128)S(1)} %pad_maximum_fusion.b_ref.mix_ref), custom_call_target="tpu_custom_call" | custom-call | flops 1000000 | bytes 100000 | tf_op jit(solution)/shard_map/weights/pallas_call | solution.py:411
  7.4 0.1 multiply_divide_fusion
  7.5 0.0 collective-permute-done.1.high_ref
  7.5 0.0 collective-permute-done.low_ref
  7.5 0.0 copy-done
  7.6 2.8 %paint.1 = (f32[3,8,2048]{2,1,0:T(8,128)S(1)}, f32[8,512]{1,0:T(8,128)S(1)}, f32[64,512]{1,0:T(8,128)}) custom-call(f32[64]{0:T(128)S(1)} %pad_maximum_fusion.b_ref.mix_ref, f32[3,8,2048]{2,1,0:T(8,128)S(1)} %copy-done, f32[3,5,2048]{2,1,0:T(8,128)S(1)} %collective-permute-done.low_ref, f32[3,5,2048]{2,1,0:T(8,128)S(1)} %collective-permute-done.1.high_ref, ...), custom_call_target="tpu_custom_call" | custom-call | flops 4000000000 | bytes 2000000 | tf_op jit(solution)/shard_map/paint/pallas_call | solution.py:421
  10.3 7.6 %all-to-all-start = ((f32[8,8,512]{2,1,0:T(8,128)}), f32[8,8,512]{2,1,0:T(8,128)S(1)}, u32[]{:S(2)}, u32[]{:S(2)}) async-start(f32[8,8,512]{2,1,0:T(8,128)} %bitcast), calls=%async_computation | async-start | bytes 262144 | tf_op jit(solution)/shard_map/all_to_all | solution.py:436
  17.9 2.6 %edges.1.c_ref = f32[3,16,2048]{2,1,0:T(8,128)S(1)} custom-call(f32[64]{0:T(128)S(1)} %pad_maximum_fusion.b_ref.mix_ref, f32[3,8,2048]{2,1,0:T(8,128)S(1)} %copy-done, f32[3,5,2048]{2,1,0:T(8,128)S(1)} %collective-permute-done.low_ref, f32[3,5,2048]{2,1,0:T(8,128)S(1)} %collective-permute-done.1.high_ref, bf16[256,160]{1,0:T(8,128)(2,1)S(1)} %get-tuple-element.23.w_ref, ...), custom_call_target="tpu_custom_call" | custom-call | flops 8000000000 | bytes 2000000 | tf_op jit(solution)/shard_map/edges/pallas_call | solution.py:437
  20.5 3.5 %all-to-all-done = f32[8,8,512]{2,1,0:T(8,128)S(1)} async-done(((f32[8,8,512]{2,1,0:T(8,128)}), f32[8,8,512]{2,1,0:T(8,128)S(1)}, u32[]{:S(2)}, u32[]{:S(2)}) %all-to-all-start) | async-done | bytes 131104 | tf_op jit(solution)/shard_map/all_to_all | solution.py:436
  24.0 0.6 runs.1
  24.7 0.0 copy-start.1
  24.7 8.3 %all-to-all-start.1 = ((f32[4,8,512]{2,1,0:T(8,128)}), f32[4,8,512]{2,1,0:T(8,128)S(1)}, u32[]{:S(2)}, u32[]{:S(2)}) async-start(f32[4,8,512]{2,1,0:T(8,128)} %bitcast.2), calls=%async_computation.1 | async-start | bytes 131072 | tf_op jit(solution)/shard_map/all_to_all | solution.py:450
  33.0 0.0 copy-done.1
  33.0 2.7 %short.1 = (f32[3,16,2048]{2,1,0:T(8,128)S(1)}, f32[512,512]{1,0:T(8,128)S(1)}) custom-call(f32[5,5]{1,0:T(8,128)S(1)} %copy-done.1, f32[3,16,2048]{2,1,0:T(8,128)S(1)} %edges.1.c_ref), custom_call_target="tpu_custom_call" | custom-call | flops 10000000 | bytes 1000000 | tf_op jit(solution)/shard_map/short/pallas_call | solution.py:451
  35.7 3.0 %all-to-all-done.1 = f32[4,8,512]{2,1,0:T(8,128)S(1)} async-done(((f32[4,8,512]{2,1,0:T(8,128)}), f32[4,8,512]{2,1,0:T(8,128)S(1)}, u32[]{:S(2)}, u32[]{:S(2)}) %all-to-all-start.1) | async-done | bytes 65568 | tf_op jit(solution)/shard_map/all_to_all | solution.py:450
  38.8 1.3 %bend.1 = (f32[64,8,128]{2,1,0:T(8,128)S(1)}, f32[3,24,2048]{2,1,0:T(8,128)S(1)}) custom-call(f32[3,16,2048]{2,1,0:T(8,128)S(1)} %get-tuple-element.32.s_ref, f32[8,512]{1,0:T(8,128)S(1)} %get-tuple-element.33.coarse_ref, f32[8,512]{1,0:T(8,128)S(1)} %get-tuple-element.34.total_ref, f32[32,512]{1,0:T(8,128)S(1)} %bitcast.5, ...), custom_call_target="tpu_custom_call" | custom-call | flops 100000000 | bytes 2000000 | tf_op jit(solution)/shard_map/bend/pallas_call | solution.py:461
  40.0 34.7 %all_to_all.32.sent_ref = f32[64,8,128]{2,1,0:T(8,128)S(1)} all-to-all(f32[64,8,128]{2,1,0:T(8,128)S(1)} %get-tuple-element.37), channel_id=1, replica_groups=mesh['x'=4,'z'=4,'far'=4,'near'=8] {'z','x'}, dimensions={0} | all-to-all | bytes 524288 | tf_op jit(solution)/shard_map/all_to_all | solution.py:471
  74.7 1.2 %scan.1 = (f32[128,8,128]{2,1,0:T(8,128)S(1)}, f32[144,8,128]{2,1,0:T(8,128)S(1)}) custom-call(f32[48]{0:T(128)S(1)} %get-tuple-element.26.mixing_ref, f32[48]{0:T(128)S(1)} %get-tuple-element.27.bending_ref, f32[64,8,128]{2,1,0:T(8,128)S(1)} %all_to_all.32.sent_ref, f32[3,24,2048]{2,1,0:T(8,128)S(1)} %get-tuple-element.38.pot_ref), custom_call_target="tpu_custom_call" | custom-call | flops 10000000 | bytes 1000000 | tf_op jit(solution)/shard_map/scan/pallas_call | solution.py:472
  75.9 33.8 %all_to_all.33.state_ref = f32[128,8,128]{2,1,0:T(8,128)S(1)} all-to-all(f32[128,8,128]{2,1,0:T(8,128)S(1)} %get-tuple-element.40), channel_id=1, replica_groups=mesh['x'=4,'z'=4,'far'=4,'near'=8] {'z','x'}, dimensions={0} | all-to-all | bytes 1048576 | tf_op jit(solution)/shard_map/all_to_all | solution.py:481
  109.8 1.7 %final.1 = f32[4,3,8,2048]{3,2,1,0:T(8,128)} custom-call(f32[48]{0:T(128)S(1)} %get-tuple-element.26.mixing_ref, f32[48]{0:T(128)S(1)} %get-tuple-element.27.bending_ref, f32[144,8,128]{2,1,0:T(8,128)S(1)} %get-tuple-element.39.u_ref, f32[128,8,128]{2,1,0:T(8,128)S(1)} %all_to_all.33.state_ref), custom_call_target="tpu_custom_call" | custom-call | flops 10000000 | bytes 1000000 | tf_op jit(solution)/shard_map/final/pallas_call | solution.py:482
  (1 shorter events, 0.0 us)
Async XLA Ops:
  0.0 7.5 %copy-start = (f32[3,8,2048]{2,1,0:T(8,128)S(1)}, f32[3,8,2048]{2,1,0:T(8,128)}, u32[]{:S(2)}) copy-start(f32[3,8,2048]{2,1,0:T(8,128)} %x_ref.3) | copy-start | bytes 589828
  0.0 5.6 %copy-start.2 = (f32[32,9]{0,1:T(8,128)S(1)}, f32[32,9]{0,1:T(8,128)}, u32[]{:S(2)}) copy-start(f32[32,9]{0,1:T(8,128)} %param.8) | copy-start | bytes 3460
  1.1 4.4 %copy-start.3 = (s32[48]{0:T(128)S(1)}, s32[48]{0:T(128)}, u32[]{:S(2)}) copy-start(s32[48]{0:T(128)} %param.7) | copy-start | bytes 580
  1.1 6.4 %collective-permute-start.1 = (f32[3,5,2048]{2,1,0:T(8,128)S(1)}, f32[3,5,2048]{2,1,0:T(8,128)S(1)}, u32[]{:S(2)}, u32[]{:S(2)}) collective-permute-start(f32[3,5,2048]{2,1,0:T(8,128)S(1)} %get-tuple-element.41), channel_id=1, source_target_pairs={{1,0},{2,1},{3,2},{4,3},{5,4},{6,5},{7,6},{8,7},{9,8},{10,9},{11,1... | collective-permute-start | bytes 368648 | tf_op jit(solution)/shard_map/ppermute | solution.py:408
  2.4 5.1 %collective-permute-start = (f32[3,5,2048]{2,1,0:T(8,128)S(1)}, f32[3,5,2048]{2,1,0:T(8,128)S(1)}, u32[]{:S(2)}, u32[]{:S(2)}) collective-permute-start(f32[3,5,2048]{2,1,0:T(8,128)S(1)} %get-tuple-element.42), channel_id=1, source_target_pairs={{0,1},{1,2},{2,3},{3,4},{4,5},{5,6},{6,7},{7,8},{8,9},{9,10},{10,1... | collective-permute-start | bytes 368648 | tf_op jit(solution)/shard_map/ppermute | solution.py:407
  5.6 0.7 copy-start.4
  5.6 0.7 copy-start.5
  10.3 13.7 %all-to-all-start = ((f32[8,8,512]{2,1,0:T(8,128)}), f32[8,8,512]{2,1,0:T(8,128)S(1)}, u32[]{:S(2)}, u32[]{:S(2)}) async-start(f32[8,8,512]{2,1,0:T(8,128)} %bitcast), calls=%async_computation | async-start | bytes 262144 | tf_op jit(solution)/shard_map/all_to_all | solution.py:436
  24.7 8.3 %copy-start.1 = (f32[5,5]{1,0:T(8,128)S(1)}, f32[5,5]{1,0:T(8,128)}, u32[]{:S(2)}) copy-start(f32[5,5]{1,0:T(8,128)} %k_ref.1) | copy-start | bytes 304
  24.7 14.1 %all-to-all-start.1 = ((f32[4,8,512]{2,1,0:T(8,128)}), f32[4,8,512]{2,1,0:T(8,128)S(1)}, u32[]{:S(2)}, u32[]{:S(2)}) async-start(f32[4,8,512]{2,1,0:T(8,128)} %bitcast.2), calls=%async_computation.1 | async-start | bytes 131072 | tf_op jit(solution)/shard_map/all_to_all | solution.py:450

commit v6 on v5

--- a/solution.py
+++ b/solution.py
@@ -84,15 +84,16 @@
     lax.fori_loop(0, cols // 256, one_chunk, 0, unroll=True)
 
 
-def paint_kernel(decay, mix_ref, x_ref, low_ref, high_ref, w_ref, pool_ref, c_ref, coarse_ref, copies_ref, wide, stack, sums):
+def paint_kernel(decay, mix_ref, x_ref, mate_ref, other_ref, w_ref, pool_ref, c_ref, coarse_ref, copies_ref, wide, stack, sums):
     cols = x_ref.shape[-1]
     wide[12:16, :] = jnp.zeros((4, cols), f32)
     sums[6:8, :] = jnp.zeros((2, cols), f32)
     stack[144:160, :] = jnp.ones((16, cols), bf16)
     for p in range(3):
-        wide[0:2, :] = low_ref[p, 3:5, :]
+        low, high = beside_rows(mate_ref, other_ref, p)
+        wide[0:2, :] = low[3:5]
         wide[2:10, :] = x_ref[p]
-        wide[10:12, :] = high_ref[p, 0:2, :]
+        wide[10:12, :] = high[0:2]
 
         def store(at, total):
             c_ref[p, :, at] = total
@@ -118,7 +119,7 @@
             copies_ref[8 * q : 8 * q + 8, at] = message
 
 
-def edge_kernel(mix_ref, x_ref, low_ref, high_ref, w_ref, main_ref, c_ref, wide, stack):
+def edge_kernel(mix_ref, x_ref, mate_ref, other_ref, w_ref, main_ref, c_ref, wide, stack):
     cols = x_ref.shape[-1]
     near, far, tile = tile_place()
     top = tile != 0
@@ -126,7 +127,8 @@
     stack[144:160, :] = jnp.ones((16, cols), bf16)
     c_ref[:, 14:16, :] = jnp.zeros((3, 2, cols), f32)
     for p in range(3):
-        wide[0:5, :] = low_ref[p]
+        low, high = beside_rows(mate_ref, other_ref, p)
+        wide[0:5, :] = low
         wide[5:13, :] = x_ref[p]
         wide[13:16, :] = jnp.zeros((3, cols), f32)
 
@@ -135,7 +137,7 @@
 
         paint_window(w_ref, mix_ref, stack, wide[...], store_above)
         wide[0:7, :] = x_ref[p, 1:8, :]
-        wide[7:12, :] = high_ref[p]
+        wide[7:12, :] = high
         wide[12:16, :] = jnp.zeros((4, cols), f32)
 
         def store_below(at, total):
@@ -143,6 +145,12 @@
 
         paint_window(w_ref, mix_ref, stack, wide[...], store_below)
         c_ref[p, 3:11, :] = main_ref[p]
+
+
+def beside_rows(mate_ref, other_ref, p):
+    even = lax.axis_index("near") % 2 == 0
+    mate, other = mate_ref[p], other_ref[p]
+    return jnp.where(even, other, mate), jnp.where(even, mate, other)
 
 
 def tile_decay(tiles, used):
@@ -394,6 +402,7 @@
 def body(density, plane_slot, paint_weight, paint_bias, mix_weight, short_kernel):
     plane_count, row_count, col_count = density.shape
     tile = ("far", "near")
+    near_index = lax.axis_index("near")
     near_count, far_count = lax.axis_size("near"), lax.axis_size("far")
     tile_count = far_count * near_count
     group_count = lax.axis_size("x") * lax.axis_size("z")
@@ -403,9 +412,12 @@
     long_gain = 1.0 / math.sqrt(row_scale * col_scale)
     decay = math.exp(-1.0 / row_scale)
 
-    up = [(i, i + 1) for i in range(tile_count - 1)]
-    low = lax.ppermute(density[:, 3:8, :], tile, up)
-    high = lax.ppermute(density[:, 0:5, :], tile, [(b, a) for a, b in up])
+    even = near_index % 2 == 0
+    last_rows, first_rows = density[:, 3:8, :], density[:, 0:5, :]
+    pairs = [(i, i ^ 1) for i in range(tile_count)]
+    mate = lax.ppermute(jnp.where(even, last_rows, first_rows), tile, pairs)
+    pairs = [(i, ((i + 1) ^ 1) - 1) for i in range(1, tile_count - 1)]
+    other = lax.ppermute(jnp.where(even, first_rows, last_rows), tile, pairs)
 
     scalars = jnp.concatenate([paint_bias, mix_weight])
     weights, pool = call(
@@ -430,7 +442,7 @@
         ),
         [pltpu.VMEM((16, col_count), f32), pltpu.VMEM((160, col_count), bf16), pltpu.VMEM((8, col_count), f32)],
         (4 * 10**9, 2 * 10**6, 10**6),
-    )(scalars, density, low, high, weights, pool)
+    )(scalars, density, mate, other, weights, pool)
     copies, mixing, bending = lax.optimization_barrier((copies, mixing, bending))
 
     received = lax.all_to_all(copies, "near", 0, 0, tiled=True)
@@ -442,7 +454,7 @@
         sds(plane_count, 16, col_count),
         [pltpu.VMEM((16, col_count), f32), pltpu.VMEM((160, col_count), bf16)],
         (8 * 10**9, 2 * 10**6, 10**6),
-    )(scalars, density, low, high, weights, main)
+    )(scalars, density, mate, other, weights, main)
     total, run_copies = call(
         runs_kernel, "runs", 0, 1, (sds(8, coarse_cols), sds(8 * far_count, coarse_cols)), (), (10**6, 10**5, 0)
     )(received)

time: 113 us -> 110 us (0.973)
  starting transfers between devices: 20.2 us -> 16.3 us
  blocking collectives: 68.5 us -> 70.5 us
    all_to_all x1, blocking collectives: 33.8 us -> 37.1 us  [body(): mine = lax.all_to_all(states, ('z', 'x'), 0, 0, tiled=True)]
    all_to_all x1, starting transfers between devices: 8.32 us -> 5.6 us  [body(): runs = lax.all_to_all(run_copies, 'far', 0, 0, tiled=True)]
    all_to_all x1, starting transfers between devices: 7.58 us -> 5.22 us  [body(): received = lax.all_to_all(copies, 'near', 0, 0, tiled=True)]
    all_to_all x1, blocking collectives: 34.7 us -> 33.4 us  [body(): gathered = lax.all_to_all(sent, ('z', 'x'), 0, 0, tiled=True)]
    ppermute x2, starting transfers between devices: 4.33 us -> 5.51 us  [the longest x1 4.84 us: body(): mate = lax.ppermute(jnp.where(even, last_rows, first_rows), tile, pairs)]
where the time goes in v6:
time: 110 us
  blocking collectives  70.5 us (64%)
  starting transfers between devices  16.3 us (15%)
  Pallas kernels  14 us (13%)
  waiting for transfers between devices  6.48 us (6%)
  other arithmetic  1.27 us (1%)
    all_to_all x1, blocking collectives, body(): mine = lax.all_to_all(states, ('z', 'x'), 0, 0, tiled=True)  37.1 us
    all_to_all x1, blocking collectives, body(): gathered = lax.all_to_all(sent, ('z', 'x'), 0, 0, tiled=True)  33.4 us
    all_to_all x1, starting transfers between devices, body(): runs = lax.all_to_all(run_copies, 'far', 0, 0, tiled=True)  5.6 us
    all_to_all x1, starting transfers between devices, body(): received = lax.all_to_all(copies, 'near', 0, 0, tiled=True)  5.22 us
    ppermute x1, starting transfers between devices, body(): mate = lax.ppermute(jnp.where(even, last_rows, first_rows), tile, pairs)  4.84 us
    all_to_all x1, waiting for transfers between devices, body(): received = lax.all_to_all(copies, 'near', 0, 0, tiled=True)  3.46 us
    all_to_all x1, waiting for transfers between devices, body(): runs = lax.all_to_all(run_copies, 'far', 0, 0, tiled=True)  3.02 us
    pallas_call x1, Pallas kernels, body(): call(functools.partial(paint_kernel, decay), 'paint', 1, 5, (sds(plane_co...  2.77 us
  transfers between devices with their start and end apart: 4, of which 2 were waited for; matrix products, arithmetic and copies ran while one was open for 0% of the time, Pallas kernels for 6%

profile of v6, /device:TPU:6, one launch (start us, length us, event | category | flops | bytes accessed | tf_op | source)
XLA Modules:
  0.0 109.5 jit_solution(14066271663354823170)
XLA Ops:
  0.0 0.0 copy-start.2
  0.0 0.0 copy-start
  0.0 1.1 %slice_select_fusion = (f32[3,5,2048]{2,1,0:T(8,128)S(1)}, f32[3,5,2048]{2,1,0:T(8,128)S(1)}) fusion(f32[3,8,2048]{2,1,0:T(8,128)} %x_ref.3, pred[]{:T(512)S(6)} %eq.5), kind=kLoop, calls=%fused_computation | loop fusion | flops 61440 | bytes 491521 | tf_op jit(solution)/shard_map/jit(_where)/select_n | solution.py:420
  1.1 0.0 copy-start.3
  1.1 0.7 collective-permute-start.1
  1.8 4.8 %collective-permute-start = (f32[3,5,2048]{2,1,0:T(8,128)S(1)}, f32[3,5,2048]{2,1,0:T(8,128)S(1)}, u32[]{:S(2)}, u32[]{:S(2)}) collective-permute-start(f32[3,5,2048]{2,1,0:T(8,128)S(1)} %get-tuple-element.42), channel_id=1, source_target_pairs={{0,1},{1,0},{2,3},{3,2},{4,5},{5,4},{6,7},{7,6},{8,9},{9,8},{10,11... | collective-permute-start | bytes 368648 | tf_op jit(solution)/shard_map/ppermute | solution.py:418
  6.6 0.0 copy-done.3
  6.7 0.1 fusion
  6.7 0.0 copy-done.2
  6.7 0.0 copy-start.4
  6.7 0.0 copy-start.5
  6.7 0.1 copy.7.w_ref
  6.8 0.6 copy-done.4
  7.4 0.0 copy-done.5
  7.4 0.1 pad_maximum_fusion.b_ref.mix_ref
  7.5 1.1 %weights.1 = (bf16[256,160]{1,0:T(8,128)(2,1)S(1)}, f32[512,128]{1,0:T(8,128)S(1)}) custom-call(f32[32,9]{1,0:T(8,128)S(1)} %copy.7.w_ref, f32[64]{0:T(128)S(1)} %pad_maximum_fusion.b_ref.mix_ref), custom_call_target="tpu_custom_call" | custom-call | flops 1000000 | bytes 100000 | tf_op jit(solution)/shard_map/weights/pallas_call | solution.py:423
  8.6 0.1 multiply_divide_fusion
  8.7 0.0 collective-permute-done.1.other_ref
  8.7 0.0 collective-permute-done.mate_ref
  8.7 0.0 copy-done
  8.7 2.8 %paint.1 = (f32[3,8,2048]{2,1,0:T(8,128)S(1)}, f32[8,512]{1,0:T(8,128)S(1)}, f32[64,512]{1,0:T(8,128)}) custom-call(f32[64]{0:T(128)S(1)} %pad_maximum_fusion.b_ref.mix_ref, f32[3,8,2048]{2,1,0:T(8,128)S(1)} %copy-done, f32[3,5,2048]{2,1,0:T(8,128)S(1)} %collective-permute-done.mate_ref, f32[3,5,2048]{2,1,0:T(8,128)S(1)} %collective-permute-done.1.other_ref, ...), custom_call_target="tpu_custom_call" | custom-call | flops 4000000000 | bytes 2000000 | tf_op jit(solution)/shard_map/paint/pallas_call | solution.py:433
  11.5 5.2 %all-to-all-start = ((f32[8,8,512]{2,1,0:T(8,128)}), f32[8,8,512]{2,1,0:T(8,128)S(1)}, u32[]{:S(2)}, u32[]{:S(2)}) async-start(f32[8,8,512]{2,1,0:T(8,128)} %bitcast), calls=%async_computation | async-start | bytes 262144 | tf_op jit(solution)/shard_map/all_to_all | solution.py:448
  16.7 2.7 %edges.1.c_ref = f32[3,16,2048]{2,1,0:T(8,128)S(1)} custom-call(f32[64]{0:T(128)S(1)} %pad_maximum_fusion.b_ref.mix_ref, f32[3,8,2048]{2,1,0:T(8,128)S(1)} %copy-done, f32[3,5,2048]{2,1,0:T(8,128)S(1)} %collective-permute-done.mate_ref, f32[3,5,2048]{2,1,0:T(8,128)S(1)} %collective-permute-done.1.other_ref, bf16[256,160]{1,0:T(8,128)(2,1)S(1)} %get-tuple-element.23.w_ref, ...), custom_call_target="tpu_custom_call" | custom-call | flops 8000000000 | bytes 2000000 | tf_op jit(solution)/shard_map/edges/pallas_call | solution.py:449
  19.4 3.5 %all-to-all-done = f32[8,8,512]{2,1,0:T(8,128)S(1)} async-done(((f32[8,8,512]{2,1,0:T(8,128)}), f32[8,8,512]{2,1,0:T(8,128)S(1)}, u32[]{:S(2)}, u32[]{:S(2)}) %all-to-all-start) | async-done | bytes 131104 | tf_op jit(solution)/shard_map/all_to_all | solution.py:448
  22.9 0.6 runs.1
  23.5 0.0 copy-start.1
  23.5 5.6 %all-to-all-start.1 = ((f32[4,8,512]{2,1,0:T(8,128)}), f32[4,8,512]{2,1,0:T(8,128)S(1)}, u32[]{:S(2)}, u32[]{:S(2)}) async-start(f32[4,8,512]{2,1,0:T(8,128)} %bitcast.2), calls=%async_computation.1 | async-start | bytes 131072 | tf_op jit(solution)/shard_map/all_to_all | solution.py:462
  29.1 0.0 copy-done.1
  29.1 2.7 %short.1 = (f32[3,16,2048]{2,1,0:T(8,128)S(1)}, f32[512,512]{1,0:T(8,128)S(1)}) custom-call(f32[5,5]{1,0:T(8,128)S(1)} %copy-done.1, f32[3,16,2048]{2,1,0:T(8,128)S(1)} %edges.1.c_ref), custom_call_target="tpu_custom_call" | custom-call | flops 10000000 | bytes 1000000 | tf_op jit(solution)/shard_map/short/pallas_call | solution.py:463
  31.8 3.0 %all-to-all-done.1 = f32[4,8,512]{2,1,0:T(8,128)S(1)} async-done(((f32[4,8,512]{2,1,0:T(8,128)}), f32[4,8,512]{2,1,0:T(8,128)S(1)}, u32[]{:S(2)}, u32[]{:S(2)}) %all-to-all-start.1) | async-done | bytes 65568 | tf_op jit(solution)/shard_map/all_to_all | solution.py:462
  34.8 1.3 %bend.1 = (f32[64,8,128]{2,1,0:T(8,128)S(1)}, f32[3,24,2048]{2,1,0:T(8,128)S(1)}) custom-call(f32[3,16,2048]{2,1,0:T(8,128)S(1)} %get-tuple-element.32.s_ref, f32[8,512]{1,0:T(8,128)S(1)} %get-tuple-element.33.coarse_ref, f32[8,512]{1,0:T(8,128)S(1)} %get-tuple-element.34.total_ref, f32[32,512]{1,0:T(8,128)S(1)} %bitcast.5, ...), custom_call_target="tpu_custom_call" | custom-call | flops 100000000 | bytes 2000000 | tf_op jit(solution)/shard_map/bend/pallas_call | solution.py:473
  36.1 33.4 %all_to_all.32.sent_ref = f32[64,8,128]{2,1,0:T(8,128)S(1)} all-to-all(f32[64,8,128]{2,1,0:T(8,128)S(1)} %get-tuple-element.37), channel_id=1, replica_groups=mesh['x'=4,'z'=4,'far'=4,'near'=8] {'z','x'}, dimensions={0} | all-to-all | bytes 524288 | tf_op jit(solution)/shard_map/all_to_all | solution.py:483
  69.5 1.2 %scan.1 = (f32[128,8,128]{2,1,0:T(8,128)S(1)}, f32[144,8,128]{2,1,0:T(8,128)S(1)}) custom-call(f32[48]{0:T(128)S(1)} %get-tuple-element.26.mixing_ref, f32[48]{0:T(128)S(1)} %get-tuple-element.27.bending_ref, f32[64,8,128]{2,1,0:T(8,128)S(1)} %all_to_all.32.sent_ref, f32[3,24,2048]{2,1,0:T(8,128)S(1)} %get-tuple-element.38.pot_ref), custom_call_target="tpu_custom_call" | custom-call | flops 10000000 | bytes 1000000 | tf_op jit(solution)/shard_map/scan/pallas_call | solution.py:484
  70.7 37.1 %all_to_all.33.state_ref = f32[128,8,128]{2,1,0:T(8,128)S(1)} all-to-all(f32[128,8,128]{2,1,0:T(8,128)S(1)} %get-tuple-element.40), channel_id=1, replica_groups=mesh['x'=4,'z'=4,'far'=4,'near'=8] {'z','x'}, dimensions={0} | all-to-all | bytes 1048576 | tf_op jit(solution)/shard_map/all_to_all | solution.py:493
  107.8 1.7 %final.1 = f32[4,3,8,2048]{3,2,1,0:T(8,128)} custom-call(f32[48]{0:T(128)S(1)} %get-tuple-element.26.mixing_ref, f32[48]{0:T(128)S(1)} %get-tuple-element.27.bending_ref, f32[144,8,128]{2,1,0:T(8,128)S(1)} %get-tuple-element.39.u_ref, f32[128,8,128]{2,1,0:T(8,128)S(1)} %all_to_all.33.state_ref), custom_call_target="tpu_custom_call" | custom-call | flops 10000000 | bytes 1000000 | tf_op jit(solution)/shard_map/final/pallas_call | solution.py:494
  (1 shorter events, 0.0 us)
Async XLA Ops:
  0.0 6.7 %copy-start.2 = (f32[32,9]{0,1:T(8,128)S(1)}, f32[32,9]{0,1:T(8,128)}, u32[]{:S(2)}) copy-start(f32[32,9]{0,1:T(8,128)} %param.8) | copy-start | bytes 3460
  0.0 8.7 %copy-start = (f32[3,8,2048]{2,1,0:T(8,128)S(1)}, f32[3,8,2048]{2,1,0:T(8,128)}, u32[]{:S(2)}) copy-start(f32[3,8,2048]{2,1,0:T(8,128)} %x_ref.3) | copy-start | bytes 589828
  1.1 5.5 %copy-start.3 = (s32[48]{0:T(128)S(1)}, s32[48]{0:T(128)}, u32[]{:S(2)}) copy-start(s32[48]{0:T(128)} %param.7) | copy-start | bytes 580
  1.1 7.6 %collective-permute-start.1 = (f32[3,5,2048]{2,1,0:T(8,128)S(1)}, f32[3,5,2048]{2,1,0:T(8,128)S(1)}, u32[]{:S(2)}, u32[]{:S(2)}) collective-permute-start(f32[3,5,2048]{2,1,0:T(8,128)S(1)} %get-tuple-element.41), channel_id=1, source_target_pairs={{1,2},{2,1},{3,4},{4,3},{5,6},{6,5},{7,8},{8,7},{9,10},{10,9},{11,... | collective-permute-start | bytes 368648 | tf_op jit(solution)/shard_map/ppermute | solution.py:420
  1.8 6.9 %collective-permute-start = (f32[3,5,2048]{2,1,0:T(8,128)S(1)}, f32[3,5,2048]{2,1,0:T(8,128)S(1)}, u32[]{:S(2)}, u32[]{:S(2)}) collective-permute-start(f32[3,5,2048]{2,1,0:T(8,128)S(1)} %get-tuple-element.42), channel_id=1, source_target_pairs={{0,1},{1,0},{2,3},{3,2},{4,5},{5,4},{6,7},{7,6},{8,9},{9,8},{10,11... | collective-permute-start | bytes 368648 | tf_op jit(solution)/shard_map/ppermute | solution.py:418
  6.7 0.7 copy-start.4
  6.7 0.7 copy-start.5
  11.5 11.4 %all-to-all-start = ((f32[8,8,512]{2,1,0:T(8,128)}), f32[8,8,512]{2,1,0:T(8,128)S(1)}, u32[]{:S(2)}, u32[]{:S(2)}) async-start(f32[8,8,512]{2,1,0:T(8,128)} %bitcast), calls=%async_computation | async-start | bytes 262144 | tf_op jit(solution)/shard_map/all_to_all | solution.py:448
  23.5 5.6 %copy-start.1 = (f32[5,5]{1,0:T(8,128)S(1)}, f32[5,5]{1,0:T(8,128)}, u32[]{:S(2)}) copy-start(f32[5,5]{1,0:T(8,128)} %k_ref.1) | copy-start | bytes 304
  23.5 11.3 %all-to-all-start.1 = ((f32[4,8,512]{2,1,0:T(8,128)}), f32[4,8,512]{2,1,0:T(8,128)S(1)}, u32[]{:S(2)}, u32[]{:S(2)}) async-start(f32[4,8,512]{2,1,0:T(8,128)} %bitcast.2), calls=%async_computation.1 | async-start | bytes 131072 | tf_op jit(solution)/shard_map/all_to_all | solution.py:462

commit v7 on v6

--- a/solution.py
+++ b/solution.py
@@ -34,8 +34,8 @@
 
 
 def tile_place():
-    near, far = lax.axis_index("near"), lax.axis_index("far")
-    return near, far, far * lax.axis_size("near") + near
+    near, far = (2 * lax.axis_index("y") + lax.axis_index("core")), lax.axis_index("far")
+    return near, far, far * 8 + near
 
 
 def weights_kernel(w_ref, b_ref, out_ref, pool_ref):
@@ -123,7 +123,7 @@
     cols = x_ref.shape[-1]
     near, far, tile = tile_place()
     top = tile != 0
-    bottom = tile != lax.axis_size("near") * lax.axis_size("far") - 1
+    bottom = tile != 8 * lax.axis_size("far") - 1
     stack[144:160, :] = jnp.ones((16, cols), bf16)
     c_ref[:, 14:16, :] = jnp.zeros((3, 2, cols), f32)
     for p in range(3):
@@ -148,7 +148,7 @@
 
 
 def beside_rows(mate_ref, other_ref, p):
-    even = lax.axis_index("near") % 2 == 0
+    even = (2 * lax.axis_index("y") + lax.axis_index("core")) % 2 == 0
     mate, other = mate_ref[p], other_ref[p]
     return jnp.where(even, other, mate), jnp.where(even, mate, other)
 
@@ -158,7 +158,7 @@
 
 
 def runs_kernel(received_ref, total_ref, copies_ref):
-    near = lax.axis_index("near")
+    near = (2 * lax.axis_index("y") + lax.axis_index("core"))
     count = received_ref.shape[0] // 8
     cols = received_ref.shape[-1]
     forward = lax.broadcasted_iota(jnp.int32, (8, 128), 0) < 3
@@ -169,7 +169,8 @@
         weight = tile_decay(gap, gap >= 0)
         to_edge = jnp.where(forward, math.exp(-(count - 1 - q) / 8.0), math.exp(-q / 8.0))
         for v in range(cols // 128):
-            value = received_ref[8 * q : 8 * q + 8, 128 * v : 128 * v + 128]
+            at = 8 * (q // 2 + 4 * (q % 2))
+            value = received_ref[at : at + 8, 128 * v : 128 * v + 128]
             totals[v] = totals[v] + weight * value
             runs[v] = runs[v] + to_edge * value
     for v in range(cols // 128):
@@ -214,7 +215,7 @@
     cols = s_ref.shape[-1]
     e = decay
     near, far, tile = tile_place()
-    near_count = lax.axis_size("near")
+    near_count = 8
     forward = lax.broadcasted_iota(jnp.int32, (8, rows.shape[-1]), 0) < 3
     acc = total_ref[...]
     inside = jnp.where(forward, near, near_count - 1 - near)
@@ -350,31 +351,33 @@
             previous, current = current, later
 
 
-def final_kernel(mixing_ref, bending_ref, u_ref, state_ref, out_ref):
+def final_kernel(mixing_ref, bending_ref, u_ref, state_ref, out_ref, held, sems):
     blocks = u_ref.shape[0] // 9
     first = 3 * (lax.axis_size("z") * lax.axis_index("x") + lax.axis_index("z"))
-
-    def one_block(d, carry):
-        at = pl.ds(pl.multiple_of(d * 128, 128), 128)
-        previous = tuple(state_ref[8 * d + i] for i in range(4))
-        current = tuple(state_ref[8 * d + 4 + i] for i in range(4))
-        for p in range(3):
+    copies = []
+    for p in range(3):
+        for d in range(blocks):
+            at = slice(128 * d, 128 * d + 128)
+            if p == 0:
+                previous = tuple(state_ref[8 * d + i] for i in range(4))
+                current = tuple(state_ref[8 * d + 4 + i] for i in range(4))
+            else:
+                current = tuple(held[p - 1, i, :, at] for i in range(4))
+                if p == 1:
+                    previous = tuple(state_ref[8 * d + 4 + i] for i in range(4))
+                else:
+                    previous = tuple(held[p - 2, i, :, at] for i in range(4))
             k = 9 * d + 3 * p
             later = advance(
-                previous,
-                current,
-                u_ref[k],
-                u_ref[k + 1],
-                u_ref[k + 2],
-                mixing_ref[first + p],
-                bending_ref[first + p],
+                previous, current, u_ref[k], u_ref[k + 1], u_ref[k + 2], mixing_ref[first + p], bending_ref[first + p]
             )
             for i in range(4):
-                out_ref[i, p, :, at] = later[i]
-            previous, current = current, later
-        return carry
-
-    lax.fori_loop(0, blocks, one_block, 0, unroll=True)
+                held[p, i, :, at] = later[i]
+        copy = pltpu.make_async_copy(held.at[p], out_ref.at[:, p], sems.at[p])
+        copy.start()
+        copies.append(copy)
+    for copy in copies:
+        copy.wait()
 
 
 vmem = pl.BlockSpec(memory_space=pltpu.VMEM)
@@ -401,9 +404,9 @@
 
 def body(density, plane_slot, paint_weight, paint_bias, mix_weight, short_kernel):
     plane_count, row_count, col_count = density.shape
-    tile = ("far", "near")
-    near_index = lax.axis_index("near")
-    near_count, far_count = lax.axis_size("near"), lax.axis_size("far")
+    tile = ("far", "y", "core")
+    near_index = (2 * lax.axis_index("y") + lax.axis_index("core"))
+    near_count, far_count = 8, lax.axis_size("far")
     tile_count = far_count * near_count
     group_count = lax.axis_size("x") * lax.axis_size("z")
     coarse_cols = col_count // 4
@@ -445,7 +448,7 @@
     )(scalars, density, mate, other, weights, pool)
     copies, mixing, bending = lax.optimization_barrier((copies, mixing, bending))
 
-    received = lax.all_to_all(copies, "near", 0, 0, tiled=True)
+    received = lax.all_to_all(copies, ("core", "y"), 0, 0, tiled=True)
     convergence = call(
         edge_kernel,
         "edges",
@@ -491,15 +494,22 @@
         (10**7, 10**6, 0),
     )(mixing, bending, gathered, potential)
     mine = lax.all_to_all(states, ("z", "x"), 0, 0, tiled=True)
-    return call(final_kernel, "final", 2, 2, sds(4, plane_count, row_count, col_count), (), (10**7, 10**6, 0))(
-        mixing, bending, shear, mine
-    )
+    return pl.pallas_call(
+        final_kernel,
+        name="final",
+        out_shape=sds(4, plane_count, row_count, col_count),
+        in_specs=[smem, smem, vmem, vmem],
+        out_specs=pl.BlockSpec(memory_space=pl.ANY),
+        scratch_shapes=[pltpu.VMEM((plane_count, 4, row_count, col_count), f32), pltpu.SemaphoreType.DMA((3,))],
+        cost_estimate=pl.CostEstimate(flops=10**7, bytes_accessed=10**6, transcendentals=0),
+        compiler_params=pltpu.CompilerParams(vmem_limit_bytes=24 << 20),
+    )(mixing, bending, shear, mine)
 
 
 def solution(mesh):
     planes, tiles = mesh.devices.shape
-    split = Mesh(mesh.devices.reshape(planes // 4, 4, 4, tiles // 4), ("x", "z", "far", "near"))
-    tile = ("far", "near")
+    split = Mesh(mesh.devices.reshape(planes // 4, 4, 4, tiles // 8, 2), ("x", "z", "far", "y", "core"))
+    tile = ("far", "y", "core")
     plane = ("x", "z")
     placed = (P(plane, tile, None), P(), P(), P(), P(), P())
     return jax.shard_map(

time: 110 us -> 110 us (level); the launches traced: 110 us -> 108 us
  blocking collectives: 70.5 us -> 69.2 us
    all_to_all x1, blocking collectives: 37.1 us -> 35.9 us  [body(): mine = lax.all_to_all(states, ('z', 'x'), 0, 0, tiled=True)]
where the time goes in v7:
time: 110 us; the launch traced here: 108 us
  blocking collectives  69.2 us (63%)
  starting transfers between devices  16.3 us (15%)
  Pallas kernels  13.9 us (13%)
  waiting for transfers between devices  5.9 us (5%)
  other arithmetic  1.27 us (1%)
    all_to_all x1, blocking collectives, body(): mine = lax.all_to_all(states, ('z', 'x'), 0, 0, tiled=True)  35.9 us
    all_to_all x1, blocking collectives, body(): gathered = lax.all_to_all(sent, ('z', 'x'), 0, 0, tiled=True)  33.3 us
    all_to_all x1, starting transfers between devices, body(): runs = lax.all_to_all(run_copies, 'far', 0, 0, tiled=True)  5.58 us
    all_to_all x1, starting transfers between devices, body(): received = lax.all_to_all(copies, ('core', 'y'), 0, 0, tiled=True)  5.23 us
    ppermute x1, starting transfers between devices, body(): mate = lax.ppermute(jnp.where(even, last_rows, first_rows), tile, pairs)  4.84 us
    all_to_all x1, waiting for transfers between devices, body(): runs = lax.all_to_all(run_copies, 'far', 0, 0, tiled=True)  3.02 us
    all_to_all x1, waiting for transfers between devices, body(): received = lax.all_to_all(copies, ('core', 'y'), 0, 0, tiled=True)  2.88 us
    pallas_call x1, Pallas kernels, body(): call(functools.partial(paint_kernel, decay), 'paint', 1, 5, (sds(plane_co...  2.77 us
  transfers between devices with their start and end apart: 4, of which 2 were waited for; matrix products, arithmetic and copies ran while one was open for 0% of the time, Pallas kernels for 6%

profile of v7, /device:TPU:6, one launch (start us, length us, event | category | flops | bytes accessed | tf_op | source)
XLA Modules:
  0.0 107.5 jit_solution(13247203773300032616)
XLA Ops:
  0.0 0.0 copy-start.2
  0.0 0.0 copy-start
  0.0 1.1 %slice_select_fusion = (f32[3,5,2048]{2,1,0:T(8,128)S(1)}, f32[3,5,2048]{2,1,0:T(8,128)S(1)}) fusion(f32[3,8,2048]{2,1,0:T(8,128)} %x_ref.3, pred[]{:T(512)S(6)} %eq.5), kind=kLoop, calls=%fused_computation | loop fusion | flops 61440 | bytes 491521 | tf_op jit(solution)/shard_map/jit(_where)/select_n | solution.py:423
  1.1 0.0 copy-start.3
  1.1 0.7 collective-permute-start.1
  1.8 4.8 %collective-permute-start = (f32[3,5,2048]{2,1,0:T(8,128)S(1)}, f32[3,5,2048]{2,1,0:T(8,128)S(1)}, u32[]{:S(2)}, u32[]{:S(2)}) collective-permute-start(f32[3,5,2048]{2,1,0:T(8,128)S(1)} %get-tuple-element.42), channel_id=1, source_target_pairs={{0,1},{1,0},{2,3},{3,2},{4,5},{5,4},{6,7},{7,6},{8,9},{9,8},{10,11... | collective-permute-start | bytes 368648 | tf_op jit(solution)/shard_map/ppermute | solution.py:421
  6.6 0.0 copy-done.3
  6.7 0.1 fusion
  6.7 0.0 copy-done.2
  6.7 0.0 copy-start.4
  6.7 0.0 copy-start.5
  6.7 0.1 copy.7.w_ref
  6.8 0.6 copy-done.4
  7.4 0.0 copy-done.5
  7.4 0.1 pad_maximum_fusion.b_ref.mix_ref
  7.5 1.1 %weights.1 = (bf16[256,160]{1,0:T(8,128)(2,1)S(1)}, f32[512,128]{1,0:T(8,128)S(1)}) custom-call(f32[32,9]{1,0:T(8,128)S(1)} %copy.7.w_ref, f32[64]{0:T(128)S(1)} %pad_maximum_fusion.b_ref.mix_ref), custom_call_target="tpu_custom_call" | custom-call | flops 1000000 | bytes 100000 | tf_op jit(solution)/shard_map/weights/pallas_call | solution.py:426
  8.6 0.1 multiply_divide_fusion
  8.7 0.0 collective-permute-done.1.other_ref
  8.7 0.0 collective-permute-done.mate_ref
  8.7 0.0 copy-done
  8.7 2.8 %paint.1 = (f32[3,8,2048]{2,1,0:T(8,128)S(1)}, f32[8,512]{1,0:T(8,128)S(1)}, f32[64,512]{1,0:T(8,128)}) custom-call(f32[64]{0:T(128)S(1)} %pad_maximum_fusion.b_ref.mix_ref, f32[3,8,2048]{2,1,0:T(8,128)S(1)} %copy-done, f32[3,5,2048]{2,1,0:T(8,128)S(1)} %collective-permute-done.mate_ref, f32[3,5,2048]{2,1,0:T(8,128)S(1)} %collective-permute-done.1.other_ref, ...), custom_call_target="tpu_custom_call" | custom-call | flops 4000000000 | bytes 2000000 | tf_op jit(solution)/shard_map/paint/pallas_call | solution.py:436
  11.5 5.2 %all-to-all-start = ((f32[8,8,512]{2,1,0:T(8,128)}), f32[8,8,512]{2,1,0:T(8,128)S(1)}, u32[]{:S(2)}, u32[]{:S(2)}) async-start(f32[8,8,512]{2,1,0:T(8,128)} %bitcast), calls=%async_computation | async-start | bytes 262144 | tf_op jit(solution)/shard_map/all_to_all | solution.py:451
  16.7 2.7 %edges.1.c_ref = f32[3,16,2048]{2,1,0:T(8,128)S(1)} custom-call(f32[64]{0:T(128)S(1)} %pad_maximum_fusion.b_ref.mix_ref, f32[3,8,2048]{2,1,0:T(8,128)S(1)} %copy-done, f32[3,5,2048]{2,1,0:T(8,128)S(1)} %collective-permute-done.mate_ref, f32[3,5,2048]{2,1,0:T(8,128)S(1)} %collective-permute-done.1.other_ref, bf16[256,160]{1,0:T(8,128)(2,1)S(1)} %get-tuple-element.23.w_ref, ...), custom_call_target="tpu_custom_call" | custom-call | flops 8000000000 | bytes 2000000 | tf_op jit(solution)/shard_map/edges/pallas_call | solution.py:452
  19.4 2.9 %all-to-all-done = f32[8,8,512]{2,1,0:T(8,128)S(1)} async-done(((f32[8,8,512]{2,1,0:T(8,128)}), f32[8,8,512]{2,1,0:T(8,128)S(1)}, u32[]{:S(2)}, u32[]{:S(2)}) %all-to-all-start) | async-done | bytes 131104 | tf_op jit(solution)/shard_map/all_to_all | solution.py:451
  22.3 0.6 runs.1
  22.9 0.0 copy-start.1
  22.9 5.6 %all-to-all-start.1 = ((f32[4,8,512]{2,1,0:T(8,128)}), f32[4,8,512]{2,1,0:T(8,128)S(1)}, u32[]{:S(2)}, u32[]{:S(2)}) async-start(f32[4,8,512]{2,1,0:T(8,128)} %bitcast.2), calls=%async_computation.1 | async-start | bytes 131072 | tf_op jit(solution)/shard_map/all_to_all | solution.py:465
  28.5 0.0 copy-done.1
  28.5 2.7 %short.1 = (f32[3,16,2048]{2,1,0:T(8,128)S(1)}, f32[512,512]{1,0:T(8,128)S(1)}) custom-call(f32[5,5]{1,0:T(8,128)S(1)} %copy-done.1, f32[3,16,2048]{2,1,0:T(8,128)S(1)} %edges.1.c_ref), custom_call_target="tpu_custom_call" | custom-call | flops 10000000 | bytes 1000000 | tf_op jit(solution)/shard_map/short/pallas_call | solution.py:466
  31.2 3.0 %all-to-all-done.1 = f32[4,8,512]{2,1,0:T(8,128)S(1)} async-done(((f32[4,8,512]{2,1,0:T(8,128)}), f32[4,8,512]{2,1,0:T(8,128)S(1)}, u32[]{:S(2)}, u32[]{:S(2)}) %all-to-all-start.1) | async-done | bytes 65568 | tf_op jit(solution)/shard_map/all_to_all | solution.py:465
  34.3 1.3 %bend.1 = (f32[64,8,128]{2,1,0:T(8,128)S(1)}, f32[3,24,2048]{2,1,0:T(8,128)S(1)}) custom-call(f32[3,16,2048]{2,1,0:T(8,128)S(1)} %get-tuple-element.32.s_ref, f32[8,512]{1,0:T(8,128)S(1)} %get-tuple-element.33.coarse_ref, f32[8,512]{1,0:T(8,128)S(1)} %get-tuple-element.34.total_ref, f32[32,512]{1,0:T(8,128)S(1)} %bitcast.5, ...), custom_call_target="tpu_custom_call" | custom-call | flops 100000000 | bytes 2000000 | tf_op jit(solution)/shard_map/bend/pallas_call | solution.py:476
  35.5 33.3 %all_to_all.32.sent_ref = f32[64,8,128]{2,1,0:T(8,128)S(1)} all-to-all(f32[64,8,128]{2,1,0:T(8,128)S(1)} %get-tuple-element.37), channel_id=1, replica_groups=mesh['x'=4,'z'=4,'far'=4,'y'=4,'core'=2] {'z','x'}, dimensions={0} | all-to-all | bytes 524288 | tf_op jit(solution)/shard_map/all_to_all | solution.py:486
  68.8 1.2 %scan.1 = (f32[128,8,128]{2,1,0:T(8,128)S(1)}, f32[144,8,128]{2,1,0:T(8,128)S(1)}) custom-call(f32[48]{0:T(128)S(1)} %get-tuple-element.26.mixing_ref, f32[48]{0:T(128)S(1)} %get-tuple-element.27.bending_ref, f32[64,8,128]{2,1,0:T(8,128)S(1)} %all_to_all.32.sent_ref, f32[3,24,2048]{2,1,0:T(8,128)S(1)} %get-tuple-element.38.pot_ref), custom_call_target="tpu_custom_call" | custom-call | flops 10000000 | bytes 1000000 | tf_op jit(solution)/shard_map/scan/pallas_call | solution.py:487
  70.0 35.9 %all_to_all.33.state_ref = f32[128,8,128]{2,1,0:T(8,128)S(1)} all-to-all(f32[128,8,128]{2,1,0:T(8,128)S(1)} %get-tuple-element.40), channel_id=1, replica_groups=mesh['x'=4,'z'=4,'far'=4,'y'=4,'core'=2] {'z','x'}, dimensions={0} | all-to-all | bytes 1048576 | tf_op jit(solution)/shard_map/all_to_all | solution.py:496
  106.0 1.5 %final.1 = f32[4,3,8,2048]{3,2,1,0:T(8,128)} custom-call(f32[48]{0:T(128)S(1)} %get-tuple-element.26.mixing_ref, f32[48]{0:T(128)S(1)} %get-tuple-element.27.bending_ref, f32[144,8,128]{2,1,0:T(8,128)S(1)} %get-tuple-element.39.u_ref, f32[128,8,128]{2,1,0:T(8,128)S(1)} %all_to_all.33.state_ref), custom_call_target="tpu_custom_call" | custom-call | flops 10000000 | bytes 1000000 | tf_op jit(solution)/shard_map/final/pallas_call | solution.py:497
  (1 shorter events, 0.0 us)
Async XLA Ops:
  0.0 6.7 %copy-start.2 = (f32[32,9]{0,1:T(8,128)S(1)}, f32[32,9]{0,1:T(8,128)}, u32[]{:S(2)}) copy-start(f32[32,9]{0,1:T(8,128)} %param.8) | copy-start | bytes 3460
  0.0 8.7 %copy-start = (f32[3,8,2048]{2,1,0:T(8,128)S(1)}, f32[3,8,2048]{2,1,0:T(8,128)}, u32[]{:S(2)}) copy-start(f32[3,8,2048]{2,1,0:T(8,128)} %x_ref.3) | copy-start | bytes 589828
  1.1 5.5 %copy-start.3 = (s32[48]{0:T(128)S(1)}, s32[48]{0:T(128)}, u32[]{:S(2)}) copy-start(s32[48]{0:T(128)} %param.7) | copy-start | bytes 580
  1.1 7.6 %collective-permute-start.1 = (f32[3,5,2048]{2,1,0:T(8,128)S(1)}, f32[3,5,2048]{2,1,0:T(8,128)S(1)}, u32[]{:S(2)}, u32[]{:S(2)}) collective-permute-start(f32[3,5,2048]{2,1,0:T(8,128)S(1)} %get-tuple-element.41), channel_id=1, source_target_pairs={{1,2},{2,1},{3,4},{4,3},{5,6},{6,5},{7,8},{8,7},{9,10},{10,9},{11,... | collective-permute-start | bytes 368648 | tf_op jit(solution)/shard_map/ppermute | solution.py:423
  1.8 6.9 %collective-permute-start = (f32[3,5,2048]{2,1,0:T(8,128)S(1)}, f32[3,5,2048]{2,1,0:T(8,128)S(1)}, u32[]{:S(2)}, u32[]{:S(2)}) collective-permute-start(f32[3,5,2048]{2,1,0:T(8,128)S(1)} %get-tuple-element.42), channel_id=1, source_target_pairs={{0,1},{1,0},{2,3},{3,2},{4,5},{5,4},{6,7},{7,6},{8,9},{9,8},{10,11... | collective-permute-start | bytes 368648 | tf_op jit(solution)/shard_map/ppermute | solution.py:421
  6.7 0.7 copy-start.4
  6.7 0.7 copy-start.5
  11.5 10.8 %all-to-all-start = ((f32[8,8,512]{2,1,0:T(8,128)}), f32[8,8,512]{2,1,0:T(8,128)S(1)}, u32[]{:S(2)}, u32[]{:S(2)}) async-start(f32[8,8,512]{2,1,0:T(8,128)} %bitcast), calls=%async_computation | async-start | bytes 262144 | tf_op jit(solution)/shard_map/all_to_all | solution.py:451
  22.9 5.6 %copy-start.1 = (f32[5,5]{1,0:T(8,128)S(1)}, f32[5,5]{1,0:T(8,128)}, u32[]{:S(2)}) copy-start(f32[5,5]{1,0:T(8,128)} %k_ref.1) | copy-start | bytes 304
  22.9 11.3 %all-to-all-start.1 = ((f32[4,8,512]{2,1,0:T(8,128)}), f32[4,8,512]{2,1,0:T(8,128)S(1)}, u32[]{:S(2)}, u32[]{:S(2)}) async-start(f32[4,8,512]{2,1,0:T(8,128)} %bitcast.2), calls=%async_computation.1 | async-start | bytes 131072 | tf_op jit(solution)/shard_map/all_to_all | solution.py:465
